TPU v7x, 32 devices: a whole 2x2x4 slice. The times are simulated.
32 devices in a mesh: azim: 8 (over z, y), dom: 4 (over x, core).
Axes of the slice: x: 2, y: 2, z: 4, core: 2. Of those that a mesh axis runs over, the one named last changes fastest.
Arguments:
- search_basis: float32 [16, 2, 16, 64, 512], P(None, None, 'azim', 'dom'), may hold values from -4 to 4
- coefficients: float32 [2, 16], replicated, may hold values from -4 to 4
- target_shift: float32 [2], replicated, may hold values from 1.5 to 2.5
- stiffness_diag: float32 [16, 64, 512], P('azim', 'dom'), may hold values from 0.25 to 2
- flame_mats: bfloat16 [256, 2, 512, 512], P(('azim', 'dom')), may hold values from -0.5 to 0.5
- flame_count: int32 [32], P(('azim', 'dom')), may hold values from 0 to 8, as said below
- flame_line: int32 [256], P(('azim', 'dom')), may hold values from 16 to 31
- flame_burner: int32 [256], P(('azim', 'dom')), may hold values from 0 to 1
- reference_part: int32 [16], P('azim'), may hold values from 0 to 3
- reference_line: int32 [16], P('azim'), may hold values from 0 to 15
Outputs:
- new_vector: float32 [2, 16, 64, 512], P(None, 'azim', 'dom')
- ritz_value: float32 [2], replicated
Inputs may be any that keep to these rules, and one draw needn't show every extreme that they name: `flame_count`: in each sector exactly two devices hold 8 live flame slots; each other device holds none or one. Live slots come first on a device. `flame_line`: flame lines lie at local indices 16 or more, reference lines below 16, so the two never coincide.
All inputs are finite; a program needn't handle non-finite values.
Results may differ from a plain program's by a relative error of at most 0.0012.
Values may be sent and summed in bfloat16 or wider, within the bound.
No kernel may reach another device: no remote copies, remote signals or barrier semaphores. Data moves between devices by JAX's collectives and lax.ppermute only.
A program may use at most 64 MiB of HBM per device.

v0:
```python
import jax
import jax.numpy as jnp
from jax import lax
from jax.sharding import PartitionSpec as P

INNER_STEPS = 3


EPSILON = 1e-06
PRECISION_HIGH = lax.Precision.HIGHEST


def padded_2(shard, sides, width, wrap):
    for axis, dim in sides:
        count, length = (lax.axis_size(axis), shard.shape[dim])
        up = [(i, (i + 1) % count) for i in range(count if wrap else count - 1)]
        down = [(j, i) for i, j in up]
        last = lax.slice_in_dim(shard, length - width, length, axis=dim)
        leading = lax.slice_in_dim(shard, 0, width, axis=dim)
        before = lax.ppermute(last, axis, up)
        after = lax.ppermute(leading, axis, down)
        shard = jnp.concatenate([before, shard, after], axis=dim)
    return shard


def local_inner(stacked, vector):
    flat_many = stacked.reshape(stacked.shape[0], 2, -1)
    flat_one = vector.reshape(2, -1)
    cross = jnp.einsum("kcn,dn->kcd", flat_many, flat_one, precision=PRECISION_HIGH)
    return (cross[:, 0, 0] + cross[:, 1, 1], cross[:, 0, 1] - cross[:, 1, 0])


def combine(coef_re, coef_im, stacked):
    real_part = jnp.einsum(
        "k,k...->...", coef_re, stacked[:, 0], precision=PRECISION_HIGH
    ) - jnp.einsum("k,k...->...", coef_im, stacked[:, 1], precision=PRECISION_HIGH)
    imag_part = jnp.einsum(
        "k,k...->...", coef_re, stacked[:, 1], precision=PRECISION_HIGH
    ) + jnp.einsum("k,k...->...", coef_im, stacked[:, 0], precision=PRECISION_HIGH)
    return jnp.stack([real_part, imag_part])


def scale_field(scale_re, scale_im, vector):
    return jnp.stack(
        [scale_re * vector[0] - scale_im * vector[1], scale_re * vector[1] + scale_im * vector[0]]
    )


def flame_product(matrix, source):
    size_line = matrix.shape[1]
    product = jnp.dot(
        matrix.reshape(2 * size_line, size_line), source.T, preferred_element_type=jnp.float32
    )
    return jnp.stack(
        [
            product[:size_line, 0] - product[size_line:, 1],
            product[:size_line, 1] + product[size_line:, 0],
        ]
    )


def least_squares(hess_re, hess_im, beta):
    columns = hess_re.shape[1]
    upper = jnp.concatenate([hess_re, -hess_im], axis=1)
    lower = jnp.concatenate([hess_im, hess_re], axis=1)
    system = jnp.concatenate([upper, lower], axis=0)
    wanted = jnp.zeros((system.shape[0],), system.dtype).at[0].set(beta)
    normal = jnp.dot(system.T, system, precision=PRECISION_HIGH)
    moment = jnp.dot(system.T, wanted, precision=PRECISION_HIGH)
    factor = jnp.linalg.cholesky(normal)
    middle = lax.linalg.triangular_solve(factor, moment[:, None], left_side=True, lower=True)
    solved = lax.linalg.triangular_solve(
        factor, middle, left_side=True, lower=True, transpose_a=True
    )
    return (solved[:columns, 0], solved[columns:, 0])


def gram_apply(gram_re, gram_im, coef_re, coef_im):
    mixed_re = jnp.dot(gram_re, coef_re, precision=PRECISION_HIGH) - jnp.dot(
        gram_im, coef_im, precision=PRECISION_HIGH
    )
    mixed_im = jnp.dot(gram_re, coef_im, precision=PRECISION_HIGH) + jnp.dot(
        gram_im, coef_re, precision=PRECISION_HIGH
    )
    return (mixed_re, mixed_im)


def on_device(
    search_basis,
    coefficients,
    target_shift,
    stiffness_diag,
    flame_mats,
    flame_count,
    flame_line,
    flame_burner,
    reference_part,
    reference_line,
):
    part_count = lax.axis_size("dom")
    sectors = lax.axis_size("azim")
    my_part = lax.axis_index("dom")
    dof_total = float(stiffness_diag.size * part_count * sectors)
    line_total = stiffness_diag.shape[0] * stiffness_diag.shape[1]
    line_width = stiffness_diag.shape[2]
    live_count = flame_count[0]
    empty_lines = jnp.zeros((2, line_total, line_width), jnp.float32)

    def burner_rows_of(vector):
        flattened = vector.reshape(2, line_total, line_width)
        picked = jnp.take(flattened, reference_line, axis=1)
        owned_rows = reference_part == my_part
        partial_rows = jnp.where(owned_rows[None, :, None], picked, 0.0)
        summed = lax.psum(partial_rows.astype(jnp.bfloat16), "dom")
        return summed

    def flame_lines(vector):
        burner_rows = burner_rows_of(vector)

        def one_slot(position, line_sums):
            matrix = lax.dynamic_index_in_dim(flame_mats, position, 0, keepdims=False)
            source = lax.dynamic_index_in_dim(
                burner_rows, flame_burner[position], 1, keepdims=False
            )
            result = flame_product(matrix, source)
            target = flame_line[position]
            before = lax.dynamic_index_in_dim(line_sums, target, 1, keepdims=False)
            return lax.dynamic_update_index_in_dim(line_sums, before + result, target, 1)

        return lax.fori_loop(0, live_count, one_slot, empty_lines)

    def operate(vector):
        beside_all = padded_2(vector, (("azim", 1),), 1, True)
        radial = padded_2(vector, (("dom", 2),), 1, False)
        around_sum = beside_all[:, 2:] + beside_all[:, :-2]
        radial_sum = radial[:, :, 2:] + radial[:, :, :-2]
        padded = jnp.pad(vector, ((0, 0), (0, 0), (0, 0), (1, 1)))
        beside = around_sum + radial_sum + (padded[..., 2:] + padded[..., :-2])
        stiffness_part = (6.0 + stiffness_diag) * vector - beside
        flame_part = flame_lines(vector).reshape(vector.shape)
        return stiffness_part - scale_field(target_shift[0], target_shift[1], vector) + flame_part

    start = combine(coefficients[0], coefficients[1], search_basis)
    start_local = local_inner(start[None], start)[0][0]
    flat_basis = search_basis.reshape(search_basis.shape[0], 2, -1)
    basis_cross = jnp.einsum("icn,jdn->icjd", flat_basis, flat_basis, precision=PRECISION_HIGH)
    gram_re = basis_cross[:, 0, :, 0] + basis_cross[:, 1, :, 1]
    gram_im = basis_cross[:, 0, :, 1] - basis_cross[:, 1, :, 0]
    start_sq, gram_re, gram_im = lax.psum((start_local, gram_re, gram_im), ("azim", "dom"))
    start_sq = start_sq / dof_total
    gram_re = gram_re / dof_total
    gram_im = gram_im / dof_total
    ritz_vector = start / jnp.sqrt(start_sq + EPSILON)
    image = operate(ritz_vector)
    image_local = local_inner(image[None], image)[0][0]
    cross_re, cross_im = local_inner(image[None], ritz_vector)
    image_sq, cross_re, cross_im = lax.psum(
        (image_local, cross_re[0], cross_im[0]), ("azim", "dom")
    )
    image_sq = image_sq / dof_total
    cross_re = cross_re / dof_total
    cross_im = cross_im / dof_total
    denominator = cross_re * cross_re + cross_im * cross_im
    theta_re = image_sq * cross_re / denominator
    theta_im = -image_sq * cross_im / denominator
    residual = image - scale_field(theta_re, theta_im, ritz_vector)
    along_re, along_im = local_inner(ritz_vector[None], residual)
    resid_local = local_inner(residual[None], residual)[0][0]
    along_re, along_im, resid_sq = lax.psum(
        (along_re[0], along_im[0], resid_local), ("azim", "dom")
    )
    along_re = along_re / dof_total
    along_im = along_im / dof_total
    resid_sq = resid_sq / dof_total
    right_side = -(residual - scale_field(along_re, along_im, ritz_vector))
    unit_sq = start_sq / (start_sq + EPSILON)
    along_sq = along_re * along_re + along_im * along_im
    right_sq = resid_sq - 2.0 * along_sq + along_sq * unit_sq
    beta = jnp.sqrt(right_sq + EPSILON)
    krylov = [right_side / beta]
    hess_re = jnp.zeros((INNER_STEPS + 1, INNER_STEPS), jnp.float32)
    hess_im = jnp.zeros((INNER_STEPS + 1, INNER_STEPS), jnp.float32)
    for column in range(INNER_STEPS):
        current = krylov[-1]
        candidate = operate(current) - scale_field(theta_re, theta_im, current)
        stacked = jnp.stack(krylov)
        proj_re, proj_im = local_inner(ritz_vector[None], candidate)
        dots_re, dots_im = local_inner(stacked, candidate)
        whole_sq = local_inner(candidate[None], candidate)[0][0]
        proj_re, proj_im, dots_re, dots_im, whole_sq = lax.psum(
            (proj_re[0], proj_im[0], dots_re, dots_im, whole_sq), ("azim", "dom")
        )
        proj_re = proj_re / dof_total
        proj_im = proj_im / dof_total
        dots_re = dots_re / dof_total
        dots_im = dots_im / dof_total
        whole_sq = whole_sq / dof_total
        candidate = candidate - scale_field(proj_re, proj_im, ritz_vector)
        candidate = candidate - combine(dots_re, dots_im, stacked)
        length_sq = (
            whole_sq
            - (proj_re * proj_re + proj_im * proj_im)
            - jnp.sum(dots_re * dots_re + dots_im * dots_im)
        )
        length = jnp.sqrt(length_sq + EPSILON)
        hess_re = hess_re.at[: column + 1, column].set(dots_re)
        hess_im = hess_im.at[: column + 1, column].set(dots_im)
        hess_re = hess_re.at[column + 1, column].set(length)
        if column + 1 < INNER_STEPS:
            krylov.append(candidate / length)
    solve_re, solve_im = least_squares(hess_re, hess_im, beta)
    update = combine(solve_re, solve_im, jnp.stack(krylov))
    first_re, first_im = local_inner(search_basis, update)
    update_local = local_inner(update[None], update)[0][0]
    first_re, first_im, update_sq = lax.psum((first_re, first_im, update_local), ("azim", "dom"))
    first_re = first_re / dof_total
    first_im = first_im / dof_total
    update_sq = update_sq / dof_total
    update = update - combine(first_re, first_im, search_basis)
    mixed_re, mixed_im = gram_apply(gram_re, gram_im, first_re, first_im)
    middle_sq = (
        update_sq
        - 2.0 * jnp.sum(first_re * first_re + first_im * first_im)
        + jnp.sum(first_re * mixed_re + first_im * mixed_im)
    )
    second_re = first_re - mixed_re
    second_im = first_im - mixed_im
    update = update - combine(second_re, second_im, search_basis)
    again_re, again_im = gram_apply(gram_re, gram_im, second_re, second_im)
    final_sq = (
        middle_sq
        - 2.0 * jnp.sum(second_re * second_re + second_im * second_im)
        + jnp.sum(second_re * again_re + second_im * again_im)
    )
    new_vector = update / jnp.sqrt(final_sq + EPSILON)
    return (new_vector, jnp.stack([theta_re, theta_im]))


def solution(mesh):
    placed = (
        P(None, None, "azim", "dom", None),
        P(),
        P(),
        P("azim", "dom", None),
        P(("azim", "dom"), None, None, None),
        P(("azim", "dom")),
        P(("azim", "dom")),
        P(("azim", "dom")),
        P("azim"),
        P("azim"),
    )
    return jax.shard_map(
        on_device,
        mesh=mesh,
        in_specs=placed,
        out_specs=(P(None, "azim", "dom", None), P()),
        check_vma=False,
    )
```

profile of v0, /device:TPU:0, one launch (start us, length us, event | category | flops | bytes accessed | tf_op | source)
XLA Modules:
  0.0 800.5 jit_solution(13781380476342268423)
XLA Ops:
  0.6 1.9 slice_bitcast_fusion
  10.5 42.7 %psum.217 = f32[]{:T(128)} all-reduce(f32[]{:T(128)} %bitcast.47), channel_id=1, replica_groups=mesh['azim'=8,'dom'=4] {'azim','dom'}, use_global_device_ids=true, to_apply=%region_0.0 | all-reduce | flops 1 | bytes 8 | tf_op jit(solution)/shard_map/psum | solution.py:149
  55.2 3.0 collective-permute-start.3
  58.3 4.2 collective-permute-start
  64.5 10.8 %fusion.30 = f32[16,2,16,2]{2,0,3,1:T(8,128)S(1)} fusion(f32[16,2,2,16,512]{4,3,2,1,0:T(8,128)} %param.40, f32[16,2,2,16,512,1]{4,3,2,1,0,5:T(8,128)} %bitcast.544), kind=kOutput, calls=%fused_computation.50 | convolution fusion | flops 201326592 | bytes 4198400 | tf_op jit(solution)/shard_map/icn,jdn->icjd/dot_general | solution.py:146
  76.4 5.9 psum.218
  82.4 8.2 %while.50 = (s32[]{:T(128)}, f32[2,32,512]{2,1,0:T(8,128)S(1)}, s32[]{:T(128)}, s32[8]{0:T(128)S(1)}, bf16[8,2,512,512]{3,2,1,0:T(8,128)(2,1)}, /*index=5*/s32[8...) while((s32[]{:T(128)}, f32[2,32,512]{2,1,0:T(8,128)S(1)}, ...), condition=%wide.region_3.5_spmd, body=%wide.region_2.4_spmd.sunk | while | flops 2100235 | bytes 3189003 | solution.py:130
  101.0 93.9 %all-reduce.12 = (f32[]{:T(128)}, f32[]{:T(128)}, f32[]{:T(128)}) all-reduce(f32[]{:T(128)} %bitcast.60, f32[]{:T(128)} %bitcast.67, f32[]{:T(128)} %bitcast.66), channel_id=1, replica_groups=mesh['azim'=8,'dom'=4] {'azim','dom'}, use_global_device_ids=true, to_apply=%region_4.6 | all-reduce | flops 3 | bytes 24 | tf_op jit(solution)/shard_map/psum | solution.py:157
  201.6 1.3 convolution_bitcast_fusion.11
  208.0 43.8 %all-reduce.11 = (f32[]{:T(128)}, f32[]{:T(128)}, f32[]{:T(128)}) all-reduce(f32[]{:T(128)} %bitcast.74, f32[]{:T(128)} %bitcast.73, f32[]{:T(128)} %bitcast.80), channel_id=1, replica_groups=mesh['azim'=8,'dom'=4] {'azim','dom'}, use_global_device_ids=true, to_apply=%region_8.10 | all-reduce | flops 3 | bytes 24 | tf_op jit(solution)/shard_map/psum | solution.py:169
  259.1 3.0 collective-permute-start.7
  262.9 7.6 psum.225
  270.6 8.0 %while.51 = (s32[]{:T(128)}, f32[2,32,512]{2,1,0:T(8,128)S(1)}, s32[]{:T(128)}, s32[8]{0:T(128)S(1)}, bf16[8,2,512,512]{3,2,1,0:T(8,128)(2,1)}, /*index=5*/s32[8...) while((s32[]{:T(128)}, f32[2,32,512]{2,1,0:T(8,128)S(1)}, ...), condition=%wide.region_12.14_spmd, body=%wide.region_11.13_spmd.sunk | while | flops 2100235 | bytes 3189003 | solution.py:130
  278.6 54.0 %collective-permute-start.4 = (f32[2,1,16,512]{3,2,1,0:T(8,128)S(1)}, f32[2,1,16,512]{3,2,1,0:T(8,128)S(1)}, u32[]{:S(2)}, u32[]{:S(2)}) collective-permute-start(f32[2,1,16,512]{3,2,1,0:T(8,128)S(1)} %get-tuple-element.416), channel_id=1, source_target_pairs={{4,0},{8,4},{12,8},{16,12},{20,16},{24,20},{28,24},{0,28},{5,1},{9... | collective-permute-start | bytes 196616 | tf_op jit(solution)/shard_map/ppermute | solution.py:21
  334.6 5.1 collective-permute-done.5
  342.3 1.3 convolution_bitcast_fusion.7
  352.1 40.0 %all-reduce.10 = (f32[]{:T(128)}, f32[]{:T(128)}, f32[1]{0:T(128)}, f32[1]{0:T(128)}, f32[]{:T(128)}) all-reduce(f32[]{:T(128)} %bitcast.103, f32[]{:T(128)} %bitcast.102, f32[1]{0:T(128)} %bitcast.104, f32[1]{0:T(128)} %bitcast.89, f32[]{:T(128)} %bitcast.96), channel_id=1, replica_groups=mesh['azim'=8,'dom'=4] {'azim','dom'}, use_global_device_ids=true, to_apply=%region_16.18 | all-reduce | flops 5 | bytes 40 | tf_op jit(solution)/shard_map/psum | solution.py:190
  403.8 3.6 collective-permute-start.11
  408.2 7.0 psum.231
  415.2 8.0 %while.52 = (s32[]{:T(128)}, f32[2,32,512]{2,1,0:T(8,128)S(1)}, s32[]{:T(128)}, s32[8]{0:T(128)S(1)}, bf16[8,2,512,512]{3,2,1,0:T(8,128)(2,1)}, /*index=5*/s32[8...) while((s32[]{:T(128)}, f32[2,32,512]{2,1,0:T(8,128)S(1)}, ...), condition=%wide.region_21.23_spmd, body=%wide.region_20.22_spmd.sunk | while | flops 2100235 | bytes 3189003 | solution.py:130
  423.3 54.7 %collective-permute-start.8 = (f32[2,1,16,512]{3,2,1,0:T(8,128)S(1)}, f32[2,1,16,512]{3,2,1,0:T(8,128)S(1)}, u32[]{:S(2)}, u32[]{:S(2)}) collective-permute-start(f32[2,1,16,512]{3,2,1,0:T(8,128)S(1)} %get-tuple-element.404), channel_id=1, source_target_pairs={{4,0},{8,4},{12,8},{16,12},{20,16},{24,20},{28,24},{0,28},{5,1},{9... | collective-permute-start | bytes 196616 | tf_op jit(solution)/shard_map/ppermute | solution.py:21
  479.8 1.3 scatter.35
  481.2 3.8 collective-permute-done.9
  487.3 1.3 convolution_bitcast_fusion.5
  488.6 3.2 convolution_bitcast_fusion
  497.0 39.2 %all-reduce.9 = (f32[]{:T(128)}, f32[]{:T(128)}, f32[2]{0:T(128)S(1)}, f32[2]{0:T(128)S(1)}, f32[]{:T(128)}) all-reduce(f32[]{:T(128)} %bitcast.135, f32[]{:T(128)} %bitcast.134, f32[2]{0:T(128)S(1)} %get-tuple-element.288, f32[2]{0:T(128)S(1)} %get-tuple-element.287, f32[]{:T(128)} %bitcast.128), channel_id=1, replica_groups=mesh['azim'=8,'dom'=4] {'azim','dom'}, use_global_device_ids=true, to_apply=%region_25.27 | all-reduce | flops 7 | bytes 56 | tf_op jit(solution)/shard_map/psum | solution.py:190
  540.5 1.5 fusion.136
  542.1 1.5 fusion.138
  543.6 1.5 fusion.140
  548.4 1.9 multiply_subtract_fusion
  551.6 3.6 collective-permute-start.15
  556.1 7.0 psum.237
  563.1 9.4 %while.53 = (s32[]{:T(128)}, f32[2,32,512]{2,1,0:T(8,128)S(1)}, s32[]{:T(128)}, s32[8]{0:T(128)}, bf16[8,2,512,512]{3,2,1,0:T(8,128)(2,1)}, /*index=5*/s32[8]{0:...) while((s32[]{:T(128)}, f32[2,32,512]{2,1,0:T(8,128)S(1)}, ...), condition=%wide.region_31.33_spmd, body=%wide.region_30.32_spmd.sunk | while | flops 2100235 | bytes 3189003 | solution.py:130
  572.5 64.1 %collective-permute-start.12 = (f32[2,1,16,512]{3,2,1,0:T(8,128)}, f32[2,1,16,512]{3,2,1,0:T(8,128)}, u32[]{:S(2)}, u32[]{:S(2)}) collective-permute-start(f32[2,1,16,512]{3,2,1,0:T(8,128)} %get-tuple-element.394), channel_id=1, source_target_pairs={{4,0},{8,4},{12,8},{16,12},{20,16},{24,20},{28,24},{0,28},{5,1},{9... | collective-permute-start | bytes 196616 | tf_op jit(solution)/shard_map/ppermute | solution.py:21
  636.7 3.2 broadcast_select_fusion.2
  639.8 3.1 broadcast_select_fusion.3
  643.0 2.5 scatter.36
  645.5 2.5 scatter.45
  648.1 1.3 scatter.39
  653.1 7.0 convolution_bitcast_fusion.1
  665.1 42.0 %all-reduce.8 = (f32[3]{0:T(128)S(1)}, f32[]{:T(128)}, f32[]{:T(128)}, f32[]{:T(128)}, f32[3]{0:T(128)S(1)}) all-reduce(f32[3]{0:T(128)S(1)} %get-tuple-element.438, f32[]{:T(128)} %bitcast.170, f32[]{:T(128)} %bitcast.176, f32[]{:T(128)} %bitcast.177, f32[3]{0:T(128)S(1)} %get-tuple-element.437), channel_id=1, replica_groups=mesh['azim'=8,'dom'=4] {'azim','dom'}, use_global_device_ids=true, to_apply=%region_32.34 | all-reduce | flops 9 | bytes 72 | tf_op jit(solution)/shard_map/psum | solution.py:190
  711.6 2.5 broadcast_select_fusion.1
  714.0 2.5 broadcast_select_fusion
  716.5 2.5 scatter.46
  719.0 2.4 scatter.40
  722.1 1.3 scatter.41
  732.2 7.4 fusion.35
  741.5 42.1 %all-reduce.7 = (f32[16]{0:T(128)S(1)}, f32[16]{0:T(128)S(1)}, f32[16,16]{1,0:T(8,128)S(1)}, f32[16,16]{1,0:T(8,128)S(1)}, f32[]{:T(128)}) all-reduce(f32[16]{0:T(128)S(1)} %get-tuple-element.436, f32[16]{0:T(128)S(1)} %get-tuple-element.435, f32[16,16]{1,0:T(8,128)S(1)} %get-tuple-element.431, ...), channel_id=1, replica_groups=mesh['azim'=8,'dom'=4] {'azim','dom'}, use_global_device_ids=true, to_apply=%region_41.43 | all-reduce | flops 545 | bytes 4360 | tf_op jit(solution)/shard_map/psum | solution.py:215
  (239 shorter events, 86.3 us)
Async XLA Ops:
  0.6 1.9 copy-start.4
  4.9 57.8 %copy-start.19 = (s32[2]{0:T(128)S(1)}, s32[2]{0:T(128)}, u32[]{:S(2)}) copy-start(s32[2]{0:T(128)} %constant.423.clone.1) | copy-start | bytes 28
  4.9 58.4 %copy-start.11 = (s32[2]{0:T(128)S(1)}, s32[2]{0:T(128)}, u32[]{:S(2)}) copy-start(s32[2]{0:T(128)} %param.49) | copy-start | bytes 28
  4.9 59.0 %copy-start.10 = (f32[2]{0:T(128)S(1)}, f32[2]{0:T(128)}, u32[]{:S(2)}) copy-start(f32[2]{0:T(128)} %param.42) | copy-start | bytes 28
  53.9 39.2 %collective-permute-start.2 = (f32[2,2,1,512]{3,2,1,0:T(1,128)S(1)}, f32[2,2,1,512]{3,2,1,0:T(1,128)S(1)}, u32[]{:S(2)}, u32[]{:S(2)}) collective-permute-start(f32[2,2,1,512]{3,2,1,0:T(1,128)S(1)} %get-tuple-element.428), channel_id=1, source_target_pairs={{1,0},{2,1},{3,2},{5,4},{6,5},{7,6},{9,8},{10,9},{11,10},{13,12},{... | collective-permute-start | bytes 24584 | tf_op jit(solution)/shard_map/ppermute | solution.py:21
  55.2 37.9 %collective-permute-start.3 = (f32[2,2,1,512]{3,2,1,0:T(1,128)S(1)}, f32[2,2,1,512]{3,2,1,0:T(1,128)S(1)}, u32[]{:S(2)}, u32[]{:S(2)}) collective-permute-start(f32[2,2,1,512]{3,2,1,0:T(1,128)S(1)} %get-tuple-element.429), channel_id=1, source_target_pairs={{0,1},{1,2},{2,3},{4,5},{5,6},{6,7},{8,9},{9,10},{10,11},{12,13},{... | collective-permute-start | bytes 24584 | tf_op jit(solution)/shard_map/ppermute | solution.py:20
  58.3 34.9 %collective-permute-start = (f32[2,1,16,512]{3,2,1,0:T(8,128)S(1)}, f32[2,1,16,512]{3,2,1,0:T(8,128)S(1)}, u32[]{:S(2)}, u32[]{:S(2)}) collective-permute-start(f32[2,1,16,512]{3,2,1,0:T(8,128)S(1)} %get-tuple-element.426), channel_id=1, source_target_pairs={{4,0},{8,4},{12,8},{16,12},{20,16},{24,20},{28,24},{0,28},{5,1},{9... | collective-permute-start | bytes 196616 | tf_op jit(solution)/shard_map/ppermute | solution.py:21
  62.4 30.7 %collective-permute-start.1 = (f32[2,1,16,512]{3,2,1,0:T(8,128)S(1)}, f32[2,1,16,512]{3,2,1,0:T(8,128)S(1)}, u32[]{:S(2)}, u32[]{:S(2)}) collective-permute-start(f32[2,1,16,512]{3,2,1,0:T(8,128)S(1)} %get-tuple-element.427), channel_id=1, source_target_pairs={{0,4},{4,8},{8,12},{12,16},{16,20},{20,24},{24,28},{28,0},{1,5},{5... | collective-permute-start | bytes 196616 | tf_op jit(solution)/shard_map/ppermute | solution.py:20
  64.5 343.1 %copy-start.9 = (s32[1024]{0:T(1024)}, s32[1024]{0:T(1024)S(1)}, u32[]{:S(2)}) copy-start(s32[1024]{0:T(1024)S(1)} %pad_clamp_fusion) | copy-start | bytes 12292
  64.5 10.9 %copy-start.2 = (f32[2,16,512]{2,1,0:T(8,128)S(1)}, f32[2,16,512]{2,1,0:T(8,128)}, u32[]{:S(2)}) copy-start(f32[2,16,512]{2,1,0:T(8,128)} %param.43) | copy-start | bytes 196612
  64.5 11.1 %copy-start.12 = (s32[2]{0:T(128)S(1)}, s32[2]{0:T(128)}, u32[]{:S(2)}) copy-start(s32[2]{0:T(128)} %param.48) | copy-start | bytes 28
  64.5 17.8 %copy-start.15 = (s32[8]{0:T(128)S(1)}, s32[8]{0:T(128)}, u32[]{:S(2)}) copy-start(s32[8]{0:T(128)} %param.46) | copy-start | bytes 100
  64.5 17.8 %copy-start.17 = (s32[8]{0:T(128)S(1)}, s32[8]{0:T(128)}, u32[]{:S(2)}) copy-start(s32[8]{0:T(128)} %param.47) | copy-start | bytes 100
  75.6 332.5 %copy-start.5 = (pred[2]{0:T(512)(128)(4,1)}, pred[2]{0:T(512)(128)(4,1)S(1)}, u32[]{:S(2)}) copy-start(pred[2]{0:T(512)(128)(4,1)S(1)} %get-tuple-element.483) | copy-start | bytes 10
  75.6 332.5 %copy-start.7 = (pred[2]{0:T(512)(128)(4,1)}, pred[2]{0:T(512)(128)(4,1)S(1)}, u32[]{:S(2)}) copy-start(pred[2]{0:T(512)(128)(4,1)S(1)} %get-tuple-element.484) | copy-start | bytes 10
  257.8 75.4 %collective-permute-start.6 = (f32[2,2,1,512]{3,2,1,0:T(1,128)S(1)}, f32[2,2,1,512]{3,2,1,0:T(1,128)S(1)}, u32[]{:S(2)}, u32[]{:S(2)}) collective-permute-start(f32[2,2,1,512]{3,2,1,0:T(1,128)S(1)} %get-tuple-element.418), channel_id=1, source_target_pairs={{1,0},{2,1},{3,2},{5,4},{6,5},{7,6},{9,8},{10,9},{11,10},{13,12},{... | collective-permute-start | bytes 24584 | tf_op jit(solution)/shard_map/ppermute | solution.py:21
  259.1 74.1 %collective-permute-start.7 = (f32[2,2,1,512]{3,2,1,0:T(1,128)S(1)}, f32[2,2,1,512]{3,2,1,0:T(1,128)S(1)}, u32[]{:S(2)}, u32[]{:S(2)}) collective-permute-start(f32[2,2,1,512]{3,2,1,0:T(1,128)S(1)} %get-tuple-element.419), channel_id=1, source_target_pairs={{0,1},{1,2},{2,3},{4,5},{5,6},{6,7},{8,9},{9,10},{10,11},{12,13},{... | collective-permute-start | bytes 24584 | tf_op jit(solution)/shard_map/ppermute | solution.py:20
  278.6 55.9 %collective-permute-start.4 = (f32[2,1,16,512]{3,2,1,0:T(8,128)S(1)}, f32[2,1,16,512]{3,2,1,0:T(8,128)S(1)}, u32[]{:S(2)}, u32[]{:S(2)}) collective-permute-start(f32[2,1,16,512]{3,2,1,0:T(8,128)S(1)} %get-tuple-element.416), channel_id=1, source_target_pairs={{4,0},{8,4},{12,8},{16,12},{20,16},{24,20},{28,24},{0,28},{5,1},{9... | collective-permute-start | bytes 196616 | tf_op jit(solution)/shard_map/ppermute | solution.py:21
  332.7 7.0 collective-permute-start.5
  402.5 78.7 %collective-permute-start.10 = (f32[2,2,1,512]{3,2,1,0:T(1,128)}, f32[2,2,1,512]{3,2,1,0:T(1,128)}, u32[]{:S(2)}, u32[]{:S(2)}) collective-permute-start(f32[2,2,1,512]{3,2,1,0:T(1,128)} %get-tuple-element.406), channel_id=1, source_target_pairs={{1,0},{2,1},{3,2},{5,4},{6,5},{7,6},{9,8},{10,9},{11,10},{13,12},{... | collective-permute-start | bytes 24584 | tf_op jit(solution)/shard_map/ppermute | solution.py:21
  403.8 77.4 %collective-permute-start.11 = (f32[2,2,1,512]{3,2,1,0:T(1,128)}, f32[2,2,1,512]{3,2,1,0:T(1,128)}, u32[]{:S(2)}, u32[]{:S(2)}) collective-permute-start(f32[2,2,1,512]{3,2,1,0:T(1,128)} %get-tuple-element.407), channel_id=1, source_target_pairs={{0,1},{1,2},{2,3},{4,5},{5,6},{6,7},{8,9},{9,10},{10,11},{12,13},{... | collective-permute-start | bytes 24584 | tf_op jit(solution)/shard_map/ppermute | solution.py:20
  423.2 54.7 %copy-start.16 = (s32[8]{0:T(128)}, s32[8]{0:T(128)S(1)}, u32[]{:S(2)}) copy-start(s32[8]{0:T(128)S(1)} %get-tuple-element.845) | copy-start | bytes 100
  423.3 54.7 %copy-start.18 = (s32[8]{0:T(128)}, s32[8]{0:T(128)S(1)}, u32[]{:S(2)}) copy-start(s32[8]{0:T(128)S(1)} %get-tuple-element.848) | copy-start | bytes 100
  423.3 57.9 %collective-permute-start.8 = (f32[2,1,16,512]{3,2,1,0:T(8,128)S(1)}, f32[2,1,16,512]{3,2,1,0:T(8,128)S(1)}, u32[]{:S(2)}, u32[]{:S(2)}) collective-permute-start(f32[2,1,16,512]{3,2,1,0:T(8,128)S(1)} %get-tuple-element.404), channel_id=1, source_target_pairs={{4,0},{8,4},{12,8},{16,12},{20,16},{24,20},{28,24},{0,28},{5,1},{9... | collective-permute-start | bytes 196616 | tf_op jit(solution)/shard_map/ppermute | solution.py:21
  477.9 7.1 collective-permute-start.9
  481.2 3.8 copy-start.3
  486.1 59.0 %copy-start.1 = (f32[2,2,16,512]{3,2,1,0:T(8,128)S(1)}, f32[2,2,16,512]{3,2,1,0:T(8,128)}, u32[]{:S(2)}) copy-start(f32[2,2,16,512]{3,2,1,0:T(8,128)} %get-tuple-element.389) | copy-start | bytes 393220
  536.1 7.5 copy-start.14
  536.1 12.3 %copy-start.13 = (f32[2]{0:T(128)}, f32[2]{0:T(128)S(1)}, u32[]{:S(2)}) copy-start(f32[2]{0:T(128)S(1)} %get-tuple-element.360) | copy-start | bytes 28
  542.0 14.0 %copy-start.6 = (pred[2]{0:T(512)(128)(4,1)S(1)}, pred[2]{0:T(512)(128)(4,1)}, u32[]{:S(2)}) copy-start(pred[2]{0:T(512)(128)(4,1)} %copy-done.5) | copy-start | bytes 10
  542.1 14.0 %copy-start.8 = (pred[2]{0:T(512)(128)(4,1)S(1)}, pred[2]{0:T(512)(128)(4,1)}, u32[]{:S(2)}) copy-start(pred[2]{0:T(512)(128)(4,1)} %copy-done.7) | copy-start | bytes 10
  550.3 99.1 %collective-permute-start.14 = (f32[2,2,1,512]{3,2,1,0:T(1,128)}, f32[2,2,1,512]{3,2,1,0:T(1,128)}, u32[]{:S(2)}, u32[]{:S(2)}) collective-permute-start(f32[2,2,1,512]{3,2,1,0:T(1,128)} %get-tuple-element.396), channel_id=1, source_target_pairs={{1,0},{2,1},{3,2},{5,4},{6,5},{7,6},{9,8},{10,9},{11,10},{13,12},{... | collective-permute-start | bytes 24584 | tf_op jit(solution)/shard_map/ppermute | solution.py:21
  551.6 97.8 %collective-permute-start.15 = (f32[2,2,1,512]{3,2,1,0:T(1,128)}, f32[2,2,1,512]{3,2,1,0:T(1,128)}, u32[]{:S(2)}, u32[]{:S(2)}) collective-permute-start(f32[2,2,1,512]{3,2,1,0:T(1,128)} %get-tuple-element.397), channel_id=1, source_target_pairs={{0,1},{1,2},{2,3},{4,5},{5,6},{6,7},{8,9},{9,10},{10,11},{12,13},{... | collective-permute-start | bytes 24584 | tf_op jit(solution)/shard_map/ppermute | solution.py:20
  572.5 76.9 %collective-permute-start.12 = (f32[2,1,16,512]{3,2,1,0:T(8,128)}, f32[2,1,16,512]{3,2,1,0:T(8,128)}, u32[]{:S(2)}, u32[]{:S(2)}) collective-permute-start(f32[2,1,16,512]{3,2,1,0:T(8,128)} %get-tuple-element.394), channel_id=1, source_target_pairs={{4,0},{8,4},{12,8},{16,12},{20,16},{24,20},{28,24},{0,28},{5,1},{9... | collective-permute-start | bytes 196616 | tf_op jit(solution)/shard_map/ppermute | solution.py:21
  636.6 12.8 %collective-permute-start.13 = (f32[2,1,16,512]{3,2,1,0:T(8,128)}, f32[2,1,16,512]{3,2,1,0:T(8,128)}, u32[]{:S(2)}, u32[]{:S(2)}) collective-permute-start(f32[2,1,16,512]{3,2,1,0:T(8,128)} %get-tuple-element.395), channel_id=1, source_target_pairs={{0,4},{4,8},{8,12},{12,16},{16,20},{20,24},{24,28},{28,0},{1,5},{5... | collective-permute-start | bytes 196616 | tf_op jit(solution)/shard_map/ppermute | solution.py:20
  727.8 4.4 copy-start
where the time goes:
time: 812 us; the launch traced here: 801 us
  blocking collectives  371 us (46%)
  starting transfers between devices  196 us (24%)
  matrix products  73.1 us (9%)
  between operations  57.6 us (7%)
  local copies, waits for them, and re-layouts  44.6 us (5%)
  other arithmetic  27.8 us (3%)
  loops' own time  20.5 us (3%)
  waiting for transfers between devices  10.2 us (1%)
    ppermute x8, starting transfers between devices, padded_2(): after = lax.ppermute(leading, axis, down)  182 us
    psum x3, blocking collectives, on_device(): lax.psum((proj_re[0], proj_im[0], dots_re, dots_im, whole_sq), ('azim', '...  121 us
    psum x1, blocking collectives, on_device(): lax.psum((image_local, cross_re[0], cross_im[0]), ('azim', 'dom'))  93.9 us
    psum x1, blocking collectives, on_device(): lax.psum((along_re[0], along_im[0], resid_local), ('azim', 'dom'))  43.8 us
    psum x1, blocking collectives, on_device(): lax.psum((start_local, gram_re, gram_im), ('azim', 'dom'))  42.7 us
    psum x1, blocking collectives, on_device(): lax.psum((first_re, first_im, update_local), ('azim', 'dom'))  42.1 us
    dot_general x16, matrix products, local_inner(): jnp.einsum('kcn,dn->kcd', flat_many, flat_one, precision=PRECISION_HIGH)  34.3 us
    psum x4, blocking collectives, burner_rows_of(): summed = lax.psum(partial_rows.astype(jnp.bfloat16), 'dom')  27.5 us
  transfers between devices with their start and end apart: 16, of which 3 were waited for; matrix products, arithmetic and copies ran while one was open for 6% of the time, Pallas kernels for 0%

commit v1 on v0

v1 whole, which is shorter than its diff:
```python
import functools

import jax
import jax.numpy as jnp
from jax import lax
from jax.experimental import pallas as pl
from jax.experimental.pallas import tpu as pltpu
from jax.sharding import PartitionSpec as P

INNER_STEPS = 3
EPSILON = 1e-06
CENTRE = 7.125
HIGHEST = lax.Precision.HIGHEST
VMEM = pltpu.VMEM
SMEM = pltpu.SMEM


def vmem(count):
    return [pl.BlockSpec(memory_space=VMEM) for _ in range(count)]


def smem(count):
    return [pl.BlockSpec(memory_space=SMEM) for _ in range(count)]


def call(kernel, outs, specs, args, scratch=(), cost=None, limit=16 << 20):
    return pl.pallas_call(
        kernel,
        out_shape=outs,
        in_specs=specs,
        out_specs=jax.tree.map(lambda _: pl.BlockSpec(memory_space=VMEM), outs),
        scratch_shapes=list(scratch),
        compiler_params=pltpu.CompilerParams(vmem_limit_bytes=limit),
        cost_estimate=cost,
    )(*args)


def write_edges(rows, depth, field, ref_part, ref_line, azim_x, azim_y, dom_x, dom_y):
    odd_a = lax.axis_index("azim") % 2
    part = lax.axis_index("dom")
    odd_d = part % 2
    last = (rows - 1) * depth
    x_start = pl.multiple_of((1 - odd_a) * last, depth)
    y_start = pl.multiple_of(odd_a * last, depth)
    for c in range(2):
        azim_x[c] = field[c, pl.ds(x_start, depth), :]
        azim_y[c] = field[c, pl.ds(y_start, depth), :]
        for a in range(rows):
            x_row = a * depth + (1 - odd_d) * (depth - 1)
            y_row = a * depth + odd_d * (depth - 1)
            at = c * rows + a
            dom_x[at : at + 1, :] = field[c, pl.ds(x_row, 1), :]
            dom_y[at : at + 1, :] = field[c, pl.ds(y_row, 1), :]
    base = 2 * rows
    for b in range(ref_part.shape[0]):
        mine = ref_part[b] == part
        for c in range(2):
            at = base + 2 * b + c
            line = field[c, pl.ds(ref_line[b], 1), :]
            dom_x[at : at + 1, :] = jnp.where(mine, line, 0.0)
            dom_y[at : at + 1, :] = jnp.zeros_like(line)


def start_kernel(rows, depth, coef, ref_part, ref_line, basis, field, azim_x, azim_y, dom_x, dom_y):
    count = basis.shape[0]
    for a in range(rows):
        span = slice(a * depth, (a + 1) * depth)
        real = jnp.zeros((depth, basis.shape[3]), jnp.float32)
        imag = real
        for i in range(count):
            re, im = basis[i, 0, span, :], basis[i, 1, span, :]
            real = real + (coef[0, i] * re - coef[1, i] * im)
            imag = imag + (coef[0, i] * im + coef[1, i] * re)
        field[0, span, :] = real
        field[1, span, :] = imag
    write_edges(rows, depth, field, ref_part, ref_line, azim_x, azim_y, dom_x, dom_y)


def flame_kernel(base, k, live, lines, burners, mats, sums, basis, *refs):
    powers, (out, dots_out, source, held) = refs[: k + 1], refs[-4:]
    dots_in = refs[k + 1] if k else None
    add_dots(k, basis, powers[:-1], powers[-1], dots_in, dots_out, held)
    width = sums.shape[1]
    count = (sums.shape[0] - base) // 2
    for b in range(count):
        for c in range(2):
            row = sums[base + 2 * b + c : base + 2 * b + c + 1, :]
            high = row.astype(jnp.bfloat16)
            low = (row - high.astype(jnp.float32)).astype(jnp.bfloat16)
            source[b, 2 * c : 2 * c + 1, :] = high
            source[b, 2 * c + 1 : 2 * c + 2, :] = low
    out[...] = jnp.zeros_like(out)

    def slot(s, carry):
        product = lax.dot_general(
            source[burners[s]],
            mats[s],
            (((1,), (1,)), ((), ())),
            preferred_element_type=jnp.float32,
        )
        by_re = product[0:1] + product[1:2]
        by_im = product[2:3] + product[3:4]
        at = pl.ds(lines[s], 1)
        out[0, at, :] += by_re[:, :width] - by_im[:, width:]
        out[1, at, :] += by_im[:, :width] + by_re[:, width:]
        return carry

    lax.fori_loop(0, live[0], slot, 0)


def step_kernel(
    rows, depth, ref_part, ref_line, old, flame, diag, from_ax, from_ay, from_dx, from_dy,
    field, azim_x, azim_y, dom_x, dom_y,
):
    width = old.shape[2]
    odd_a = lax.axis_index("azim") % 2 == 1
    part = lax.axis_index("dom")
    odd_d = part % 2 == 1
    row_at = lax.broadcasted_iota(jnp.int32, (depth, width), 0)
    lane_at = lax.broadcasted_iota(jnp.int32, (depth, width), 1)
    for c in range(2):
        before = jnp.where(odd_a, from_ax[c], from_ay[c])
        after = jnp.where(odd_a, from_ay[c], from_ax[c])
        planes = [old[c, a * depth : (a + 1) * depth, :] for a in range(rows)]
        around = [before, *planes, after]
        for a in range(rows):
            here = planes[a]
            at = c * rows + a
            one, two = from_dx[at : at + 1, :], from_dy[at : at + 1, :]
            inner = jnp.where(part == 0, 0.0, jnp.where(odd_d, one, two))
            outer = jnp.where(part == lax.axis_size("dom") - 1, 0.0, jnp.where(odd_d, two, one))
            down = jnp.where(row_at == 0, inner, pltpu.roll(here, 1, 0))
            up = jnp.where(row_at == depth - 1, outer, pltpu.roll(here, depth - 1, 0))
            left = jnp.where(lane_at == 0, 0.0, pltpu.roll(here, 1, 1))
            right = jnp.where(lane_at == width - 1, 0.0, pltpu.roll(here, width - 1, 1))
            beside = (around[a] + around[a + 2]) + (down + up) + (left + right)
            span = slice(a * depth, (a + 1) * depth)
            factor = diag[span, :] + (6.0 - CENTRE)
            field[c, span, :] = factor * here - beside + flame[c, span, :]
    if azim_x is not None:
        write_edges(rows, depth, field, ref_part, ref_line, azim_x, azim_y, dom_x, dom_y)


def last_kernel(rows, depth, *refs):
    first, powers, (dots_in, dots_out, field, held) = refs[:7], refs[7:-4], refs[-4:]
    step_kernel(rows, depth, None, None, *first, field, None, None, None, None)
    add_dots(len(powers), None, powers, field, dots_in, dots_out, held)


def folded(x):
    tall = total_of(x[i : i + 8] for i in range(0, x.shape[0], 8))
    tile = total_of(tall[:, j : j + 128] for j in range(0, x.shape[1], 128))
    return jnp.sum(tile, axis=0, keepdims=True)


def total_of(terms):
    terms = list(terms)
    while len(terms) > 1:
        terms = [
            terms[i] + terms[i + 1] if i + 1 < len(terms) else terms[i]
            for i in range(0, len(terms), 2)
        ]
    return terms[0]


def add_dots(k, basis, powers, current, dots_in, dots_out, held):
    held[...] = jnp.zeros_like(held)
    re, im = current[0], current[1]
    count = 0
    if basis is not None:
        count = basis.shape[0]

        def one(i, carry):
            left_re, left_im = basis[i, 0], basis[i, 1]
            held[pl.ds(i, 1), :] = folded(left_re * re + left_im * im)
            held[pl.ds(count + i, 1), :] = folded(left_re * im - left_im * re)
            return carry

        lax.fori_loop(0, count, one, 0)
    first = held.shape[0] - 16
    for j, power in enumerate([*powers, current]):
        left_re, left_im = power[0], power[1]
        held[first + j : first + j + 1, :] = folded(left_re * re + left_im * im)
        held[first + 8 + j : first + 9 + j, :] = folded(left_re * im - left_im * re)
    row = lax.dot_general(
        jnp.ones((8, 128), jnp.float32), held[...], (((1,), (1,)), ((), ())),
        precision=HIGHEST, preferred_element_type=jnp.float32,
    )
    at = lax.broadcasted_iota(jnp.int32, row.shape, 0)
    wide = row.shape[1]
    dots_out[...] = jnp.zeros_like(dots_out)
    dots_out[:, :wide] = jnp.where(at == k, row, 0.0 if dots_in is None else dots_in[:, :wide])


class Cx:
    def __init__(self, re, im):
        self.re, self.im = re, im

    def __add__(self, o):
        return Cx(self.re + o.re, self.im + o.im)

    def __sub__(self, o):
        return Cx(self.re - o.re, self.im - o.im)

    def __mul__(self, o):
        if isinstance(o, Cx):
            return Cx(self.re * o.re - self.im * o.im, self.re * o.im + self.im * o.re)
        return Cx(self.re * o, self.im * o)

    def conj(self):
        return Cx(self.re, -self.im)

    def sq(self):
        return self.re * self.re + self.im * self.im


def small_problem(gram, mu):
    steps = INNER_STEPS

    def applied(vec):
        return {j: total_of(gram[j][k] * v for k, v in vec.items()) for j in range(steps + 2)}

    def dot(left, image):
        return total_of(v.conj() * image[k] for k, v in left.items())

    def less(vec, scale, other):
        out = dict(vec)
        for k, v in other.items():
            out[k] = out[k] - scale * v if k in out else Cx(-(scale * v).re, -(scale * v).im)
        return out

    def scaled(vec, by):
        return {k: v * by for k, v in vec.items()}

    def times_operator(vec, shift):
        out = {}
        for k, v in vec.items():
            out[k + 1] = v
        for k, v in vec.items():
            out[k] = out[k] + shift * v if k in out else shift * v
        return out

    first = gram[0][0].re
    unit = 1.0 / jnp.sqrt(first + EPSILON)
    zero = jnp.zeros_like(first)
    u = {0: Cx(unit, zero)}
    u_image = applied(u)
    w = times_operator(u, mu)
    w_image = applied(w)
    image_sq = dot(w, w_image).re
    cross = dot(w, u_image)
    bottom = cross.sq()
    theta = Cx(image_sq * cross.re / bottom, -image_sq * cross.im / bottom)
    r = less(w, theta, u)
    along = dot(u, applied(r))
    b = scaled(less(r, along, u), -1.0)
    beta = jnp.sqrt(dot(b, applied(b)).re + EPSILON)
    q = [scaled(b, 1.0 / beta)]
    q_image = [applied(q[0])]
    hess = []
    shift = mu - theta
    for column in range(steps):
        z = times_operator(q[-1], shift)
        z = less(z, dot(u, applied(z)), u)
        z_image = applied(z)
        column_dots = [dot(one, z_image) for one in q]
        for value, one in zip(column_dots, q):
            z = less(z, value, one)
        z_image = applied(z)
        length = jnp.sqrt(dot(z, z_image).re + EPSILON)
        hess.append((column_dots, length))
        if column + 1 < steps:
            q.append(scaled(z, 1.0 / length))
    full = []
    for column, (dots, length) in enumerate(hess):
        entries = {i: v for i, v in enumerate(dots)}
        entries[column + 1] = Cx(length, zero)
        full.append(entries)

    def column_dot(i, j):
        return total_of(full[i][k].conj() * full[j][k] for k in full[i] if k in full[j])

    low = [[None] * steps for _ in range(steps)]
    for j in range(steps):
        diagonal = column_dot(j, j).re
        for k in range(j):
            diagonal = diagonal - low[j][k].sq()
        root = jnp.sqrt(diagonal)
        low[j][j] = root
        for i in range(j + 1, steps):
            value = column_dot(i, j)
            for k in range(j):
                value = value - low[i][k] * low[j][k].conj()
            low[i][j] = value * (1.0 / root)
    middle = []
    for i in range(steps):
        value = full[i][0].conj() * beta
        for k in range(i):
            value = value - low[i][k] * middle[k]
        middle.append(value * (1.0 / low[i][i]))
    solved = [None] * steps
    for i in reversed(range(steps)):
        value = middle[i]
        for k in range(i + 1, steps):
            value = value - low[k][i].conj() * solved[k]
        solved[i] = value * (1.0 / low[i][i])
    update = {}
    for value, one in zip(solved, q):
        for k, v in one.items():
            update[k] = update[k] + value * v if k in update else value * v
    update_sq = dot(update, applied(update)).re
    return theta, update, update_sq


def end_kernel(rows, depth, scale, shift, gram_s, gram, basis, *refs):
    powers, out, ritz, column = refs[: INNER_STEPS + 1], refs[-3], refs[-2], refs[-1]
    count = basis.shape[0]
    width = basis.shape[3]
    base = 2 * count
    tile = (8, 128)

    def splat(i, j):
        return jnp.full(tile, gram_s[i, j] * scale, jnp.float32)

    size = INNER_STEPS + 2
    table = [[None] * size for _ in range(size)]
    for i in range(size):
        for j in range(i, size):
            im = splat(j, base + 8 + i) if i != j else jnp.zeros(tile, jnp.float32)
            table[i][j] = Cx(splat(j, base + i), im)
            if i != j:
                table[j][i] = table[i][j].conj()
    mu = Cx(
        jnp.full(tile, CENTRE - shift[0], jnp.float32), jnp.full(tile, -shift[1], jnp.float32)
    )
    theta, update, update_sq = small_problem(table, mu)
    lane = lax.broadcasted_iota(jnp.int32, (1, 128), 1)
    ritz[...] = jnp.where(lane == 0, theta.re[0:1], theta.im[0:1])

    def lanes(x):
        return jnp.sum(x, axis=1, keepdims=True)

    def sublanes(x):
        return jnp.sum(x, axis=0, keepdims=True)

    def shifted(x, by):
        return pltpu.roll(x, 128 - by, 1)

    packed = gram[8:16, :] * scale
    folds = 128 // base
    whole = jnp.concatenate([packed] + [shifted(packed, base * q) for q in range(1, folds)], axis=0)
    top, bottom = whole[:count], whole[count:base]
    g_re = top + shifted(bottom, count)
    g_im = shifted(top, count) - bottom
    lane = lax.broadcasted_iota(jnp.int32, (count, 128), 1)
    same = lax.broadcasted_iota(jnp.int32, (count, 128), 0) == lane
    by_re = total_of(gram[k : k + 1, :] * v.re[0:1] for k, v in update.items()) * scale
    by_im = total_of(gram[k : k + 1, :] * v.im[0:1] for k, v in update.items()) * scale
    first_re = lanes(jnp.where(same, by_re - shifted(by_im, count), 0.0))
    first_im = lanes(jnp.where(same, by_im + shifted(by_re, count), 0.0))

    def across(col):
        return sublanes(jnp.where(same, col, 0.0))

    def mixed(col_re, col_im):
        row_re, row_im = across(col_re), across(col_im)
        return (
            lanes(g_re * row_re - g_im * row_im),
            lanes(g_re * row_im + g_im * row_re),
        )

    mixed_re, mixed_im = mixed(first_re, first_im)
    second_re, second_im = first_re - mixed_re, first_im - mixed_im
    again_re, again_im = mixed(second_re, second_im)
    change = (
        -2.0 * (first_re * first_re + first_im * first_im)
        + (first_re * mixed_re + first_im * mixed_im)
        - 2.0 * (second_re * second_re + second_im * second_im)
        + (second_re * again_re + second_im * again_im)
    )
    final_sq = update_sq[0:1, 0:1] + sublanes(change)
    inverse = 1.0 / jnp.sqrt(final_sq + EPSILON)
    column[0] = jnp.broadcast_to((first_re + second_re) * inverse, (count, 128))
    column[1] = jnp.broadcast_to((first_im + second_im) * inverse, (count, 128))
    full_inverse = jnp.broadcast_to(inverse, tile)
    coefs = {k: v * full_inverse for k, v in update.items()}

    def wide(x):
        return jnp.tile(x[0:1, :], (1, width // 128))

    coefs = {k: Cx(wide(v.re), wide(v.im)) for k, v in coefs.items()}
    for a in range(rows):
        span = slice(a * depth, (a + 1) * depth)
        real = jnp.zeros((depth, width), jnp.float32)
        imag = real
        for k, v in coefs.items():
            re, im = powers[k][0, span, :], powers[k][1, span, :]
            real = real + (v.re * re - v.im * im)
            imag = imag + (v.re * im + v.im * re)
        for i in range(count):
            v = Cx(wide(column[0, i : i + 1, :]), wide(column[1, i : i + 1, :]))
            re, im = basis[i, 0, span, :], basis[i, 1, span, :]
            real = real - (v.re * re - v.im * im)
            imag = imag - (v.re * im + v.im * re)
        out[0, span, :] = real
        out[1, span, :] = imag


def on_device(
    search_basis, coefficients, target_shift, stiffness_diag, flame_mats,
    flame_count, flame_line, flame_burner, reference_part, reference_line,
):
    n_azim, n_dom = lax.axis_size("azim"), lax.axis_size("dom")
    count, _, rows, depth, width = search_basis.shape
    lines = rows * depth
    scale = 1.0 / float(stiffness_diag.size * n_azim * n_dom)
    slots = flame_mats.shape[0]
    base = 2 * rows
    tall = base + 2 * reference_part.shape[0]
    basis = search_basis.reshape(count, 2, lines, width)
    basis_rows = search_basis.reshape(count * 2 * lines, width)
    diag = stiffness_diag.reshape(lines, width)
    mats = flame_mats.reshape(slots, 2 * width, width)

    def exchange(values, axis, pairs):
        both = pairs + [(j, i) for i, j in pairs]
        return lax.ppermute(values, axis, both)

    azim_even = [(i, i + 1) for i in range(0, n_azim, 2)]
    azim_odd = [(i, (i + 1) % n_azim) for i in range(1, n_azim, 2)]
    dom_even = [(i, i + 1) for i in range(0, n_dom, 2)]
    dom_odd = [(i, (i + 1) % n_dom) for i in range(1, n_dom, 2)]

    def shape(*dims):
        return jax.ShapeDtypeStruct(dims, jnp.float32)

    fields = [
        shape(2, lines, width),
        shape(2, depth, width),
        shape(2, depth, width),
        shape(tall, width),
        shape(tall, width),
    ]
    here = functools.partial(start_kernel, rows, depth)
    power, azim_x, azim_y, dom_x, dom_y = call(
        here, fields, smem(3) + vmem(1), (coefficients, reference_part, reference_line, basis)
    )
    powers = [power]
    held = VMEM((2 * count + 16, 128), jnp.float32)
    cross = jnp.einsum("icarl,jdarl->cidj", search_basis, search_basis, precision=HIGHEST)
    folded_gram = cross.reshape(-1, 8, 2 * count).transpose(1, 0, 2).reshape(8, 8 * count)
    is_sum = lax.broadcasted_iota(jnp.int32, (tall, width), 0) >= base
    for step in range(INNER_STEPS + 1):
        from_ay = exchange(azim_y, "azim", azim_odd)
        from_dx = exchange(dom_x, "dom", dom_even)
        dom_y = jnp.where(is_sum, dom_x + from_dx, dom_y)
        from_dy = exchange(dom_y, "dom", dom_odd)
        from_ax = exchange(azim_x, "azim", azim_even)
        sums = dom_y + from_dy
        reach = 4
        while reach < n_dom:
            pairs = [(i, i ^ reach) for i in range(n_dom) if i < i ^ reach]
            sums = sums + exchange(sums, "dom", pairs)
            reach *= 2
        given = (mats, sums, basis, *powers, *([dots] if step else []))
        flame, dots = call(
            functools.partial(flame_kernel, base, step),
            [shape(2, lines, width), shape(8, 128)],
            smem(3) + vmem(len(given)),
            (flame_count, flame_line, flame_burner, *given),
            [VMEM((reference_part.shape[0], 16, width), jnp.bfloat16), held],
        )
        received = (power, flame, diag, from_ax, from_ay, from_dx, from_dy)
        if step < INNER_STEPS:
            power, azim_x, azim_y, dom_x, dom_y = call(
                functools.partial(step_kernel, rows, depth),
                fields,
                smem(2) + vmem(7),
                (reference_part, reference_line, *received),
            )
        else:
            dots = call(
                functools.partial(last_kernel, rows, depth),
                shape(8, 128),
                vmem(8 + len(powers)),
                (*received, *powers, dots),
                [VMEM((2, lines, width), jnp.float32), held],
            )
        powers.append(power)
    devices = n_azim * n_dom
    packed = jnp.concatenate([dots, folded_gram], axis=0)
    spread = jnp.broadcast_to(packed[None], (devices, *packed.shape))
    gram = jnp.sum(lax.all_to_all(spread, ("azim", "dom"), 0, 0), axis=0)
    new_vector, ritz = call(
        functools.partial(end_kernel, rows, depth, scale),
        [shape(2, lines, width), shape(1, 128)],
        smem(2) + vmem(2 + INNER_STEPS + 1),
        (target_shift, gram, gram, basis, *powers[: INNER_STEPS + 1]),
        [VMEM((2, count, 128), jnp.float32)],
    )
    return new_vector.reshape(2, rows, depth, width), ritz[0, :2]


def solution(mesh):
    placed = (
        P(None, None, "azim", "dom", None),
        P(),
        P(),
        P("azim", "dom", None),
        P(("azim", "dom"), None, None, None),
        P(("azim", "dom")),
        P(("azim", "dom")),
        P(("azim", "dom")),
        P("azim"),
        P("azim"),
    )
    return jax.shard_map(
        on_device,
        mesh=mesh,
        in_specs=placed,
        out_specs=(P(None, "azim", "dom", None), P()),
        check_vma=False,
    )
```

time: 812 us -> 84.4 us (0.10); the launches traced: 801 us -> 84.2 us
  blocking collectives: 371 us -> 17.7 us
  starting transfers between devices: 196 us -> 25.3 us
  matrix products: 73.1 us -> 8.66 us
  between operations: 57.6 us -> 1.55 us
  local copies, waits for them, and re-layouts: 44.6 us -> 11.2 us
  other arithmetic: 27.8 us -> 0.35 us
  loops' own time: 20.5 us -> 0 us
  Pallas kernels: 0 us -> 12.6 us
    psum x11 -> x0, blocking collectives: 371 us -> none  [the longest x3 121 us: on_device(): lax.psum((proj_re[0], proj_im[0], dots_re, dots_im, whole_sq), ('azim', '...]
    ppermute x16, starting transfers between devices: 196 us -> 25.3 us  [exchange(): return lax.ppermute(values, axis, both)]
    dot_general x51 -> x1, matrix products: 72.8 us -> 8.66 us  [on_device(): jnp.einsum('icarl,jdarl->cidj', search_basis, search_basis, precision=HIG...]
    another operation x4 -> x0, loops' own time: 20.5 us -> none  [flame_lines(): return lax.fori_loop(0, live_count, one_slot, empty_lines)]
    all_to_all x0 -> x1, blocking collectives: none -> 17.7 us  [on_device(): gram = jnp.sum(lax.all_to_all(spread, ('azim', 'dom'), 0, 0), axis=0)]
    another operation x22 -> x0, other arithmetic: 15.7 us -> none
    scatter x9 -> x0, local copies, waits for them, and re-layouts: 15.1 us -> none  [the longest x3 5.58 us: on_device(): hess_im = hess_im.at[:column + 1, column].set(dots_im)]
    pallas_call x0 -> x10, Pallas kernels: none -> 12.6 us  [call(): pl.pallas_call(kernel, out_shape=outs, in_specs=specs, out_specs=jax.tree...]
  transfers between devices with their start and end apart: 16 -> 16, of which waited for: 3 -> 3; matrix products, arithmetic and copies ran while one was open for 6% -> 11% of each run, Pallas kernels for 0% -> 8%
where the time goes in v1:
time: 84.4 us; the launch traced here: 84.2 us
  starting transfers between devices  25.3 us (30%)
  blocking collectives  17.7 us (21%)
  Pallas kernels  12.6 us (15%)
  local copies, waits for them, and re-layouts  11.2 us (13%)
  matrix products  8.66 us (10%)
  waiting for transfers between devices  6.8 us (8%)
  between operations  1.55 us (2%)
    ppermute x16, starting transfers between devices, exchange(): return lax.ppermute(values, axis, both)  25.3 us
    all_to_all x1, blocking collectives, on_device(): gram = jnp.sum(lax.all_to_all(spread, ('azim', 'dom'), 0, 0), axis=0)  17.7 us
    pallas_call x10, Pallas kernels, call(): pl.pallas_call(kernel, out_shape=outs, in_specs=specs, out_specs=jax.tree...  12.6 us
    unnamed x24, local copies, waits for them, and re-layouts  10.4 us
    dot_general x1, matrix products, on_device(): jnp.einsum('icarl,jdarl->cidj', search_basis, search_basis, precision=HIG...  8.66 us
    ppermute x16, waiting for transfers between devices, exchange(): return lax.ppermute(values, axis, both)  6.8 us
  transfers between devices with their start and end apart: 16, of which 3 were waited for; matrix products, arithmetic and copies ran while one was open for 11% of the time, Pallas kernels for 8%

profile of v1, /device:TPU:0, one launch (start us, length us, event | category | flops | bytes accessed | tf_op | source)
XLA Modules:
  0.0 84.2 jit_solution(13770276074702052103)
XLA Ops:
  0.7 1.6 %copy-done.2 = f32[16,2,2,16,512]{4,3,2,1,0:T(8,128)S(1)} copy-done((f32[16,2,2,16,512]{4,3,2,1,0:T(8,128)S(1)}, f32[16,2,2,16,512]{4,3,2,1,0:T(8,128)}, u32[]{:S(2)}) %copy-start.2) | copy-done | bytes 2097176
  2.3 0.7 copy-done.5
  2.9 0.7 copy-done.7
  3.6 0.7 copy-done.10
  4.2 0.9 %shard_map.113 = (f32[2,32,512]{2,1,0:T(8,128)S(1)}, f32[2,16,512]{2,1,0:T(8,128)S(1)}, f32[2,16,512]{2,1,0:T(8,128)S(1)}, f32[8,512]{1,0:T(8,128)S(1)}, f32[8,512]{1,0:T(8,128)S(1)}) custom-call(f32[2,16]{1,0:T(2,128)S(1)} %copy-done.10, s32[2]{0:T(128)S(1)} %copy-done.5, s32[2]{0:T(128)S(1)} %copy-done.7, f32[16,2,32,512]{3,2,1,0:T(8,128)S(1)} %bitcast.23), custom_call_target="tpu_custom_call" | custom-call | tf_op jit(solution)/shard_map/pallas_call | solution.py:27
  5.1 0.6 collective-permute-start
  5.7 2.6 %collective-permute-start.2 = (f32[2,16,512]{2,1,0:T(8,128)S(1)}, f32[2,16,512]{2,1,0:T(8,128)S(1)}, u32[]{:S(2)}, u32[]{:S(2)}) collective-permute-start(f32[2,16,512]{2,1,0:T(8,128)S(1)} %get-tuple-element.36), channel_id=1, source_target_pairs={{0,4},{8,12},{16,20},{24,28},{4,0},{12,8},{20,16},{28,24},{1,5},{9... | collective-permute-start | bytes 196616 | tf_op jit(solution)/shard_map/ppermute | solution.py:427
  8.3 3.5 %collective-permute-start.3 = (f32[2,16,512]{2,1,0:T(8,128)S(1)}, f32[2,16,512]{2,1,0:T(8,128)S(1)}, u32[]{:S(2)}, u32[]{:S(2)}) collective-permute-start(f32[2,16,512]{2,1,0:T(8,128)S(1)} %get-tuple-element.37), channel_id=1, source_target_pairs={{4,8},{12,16},{20,24},{28,0},{8,4},{16,12},{24,20},{0,28},{5,9},{1... | collective-permute-start | bytes 196616 | tf_op jit(solution)/shard_map/ppermute | solution.py:427
  11.8 0.0 collective-permute-done.from_dx
  11.8 0.1 add_select_fusion.3
  11.9 1.0 %collective-permute-start.1 = (f32[8,512]{1,0:T(8,128)S(1)}, f32[8,512]{1,0:T(8,128)S(1)}, u32[]{:S(2)}, u32[]{:S(2)}) collective-permute-start(f32[8,512]{1,0:T(8,128)S(1)} %add_select_fusion.3), channel_id=1, source_target_pairs={{1,2},{3,0},{2,1},{0,3},{5,6},{7,4},{6,5},{4,7},{9,10},{11,8},{10,... | collective-permute-start | bytes 49160 | tf_op jit(solution)/shard_map/ppermute | solution.py:427
  13.5 1.7 %collective-permute-done.1.from_dy = f32[8,512]{1,0:T(8,128)S(1)} collective-permute-done((f32[8,512]{1,0:T(8,128)S(1)}, f32[8,512]{1,0:T(8,128)S(1)}, u32[]{:S(2)}, u32[]{:S(2)}) %collective-permute-start.1) | collective-permute-done | bytes 16416 | tf_op jit(solution)/shard_map/ppermute | solution.py:427
  15.2 0.0 copy-start
  15.2 3.4 %copy-done = bf16[8,2,512,512]{3,2,1,0:T(8,128)(2,1)S(1)} copy-done((bf16[8,2,512,512]{3,2,1,0:T(8,128)(2,1)S(1)}, bf16[8,2,512,512]{3,2,1,0:T(8,128)(2,1)}, u32[]{:S(2)}) %copy-start) | copy-done | bytes 8388632
  18.6 1.7 %shard_map.114 = (f32[2,32,512]{2,1,0:T(8,128)S(1)}, f32[8,128]{1,0:T(8,128)S(1)}) custom-call(s32[1]{0:T(128)S(6)} %copy.36.live, s32[8]{0:T(128)S(1)} %copy-done.8, s32[8]{0:T(128)S(1)} %copy-done.9, bf16[8,1024,512]{2,1,0:T(8,128)(2,1)S(1)} %bitcast.19, f32[8,512]{1,0:T(8,128)S(1)} %add.25.sums, f32[16,2,32,512]{3,2,1,0:T(8,128)S(1)} %bitcast.24, ...), custom_call_target="tpu_custom_call" | custom-call | tf_op jit(solution)/shard_map/pallas_call | solution.py:27
  20.3 0.7 shard_map.115
  21.0 3.0 %collective-permute-start.4 = (f32[8,512]{1,0:T(8,128)S(1)}, f32[8,512]{1,0:T(8,128)S(1)}, u32[]{:S(2)}, u32[]{:S(2)}) collective-permute-start(f32[8,512]{1,0:T(8,128)S(1)} %get-tuple-element.39), channel_id=1, source_target_pairs={{0,1},{2,3},{1,0},{3,2},{4,5},{6,7},{5,4},{7,6},{8,9},{10,11},{9,8... | collective-permute-start | bytes 49160 | tf_op jit(solution)/shard_map/ppermute | solution.py:427
  24.1 1.9 %collective-permute-start.7 = (f32[2,16,512]{2,1,0:T(8,128)S(1)}, f32[2,16,512]{2,1,0:T(8,128)S(1)}, u32[]{:S(2)}, u32[]{:S(2)}) collective-permute-start(f32[2,16,512]{2,1,0:T(8,128)S(1)} %get-tuple-element.44), channel_id=1, source_target_pairs={{4,8},{12,16},{20,24},{28,0},{8,4},{16,12},{24,20},{0,28},{5,9},{1... | collective-permute-start | bytes 196616 | tf_op jit(solution)/shard_map/ppermute | solution.py:427
  25.9 0.1 add_select_fusion.2
  26.0 0.9 %collective-permute-start.5 = (f32[8,512]{1,0:T(8,128)S(1)}, f32[8,512]{1,0:T(8,128)S(1)}, u32[]{:S(2)}, u32[]{:S(2)}) collective-permute-start(f32[8,512]{1,0:T(8,128)S(1)} %add_select_fusion.2), channel_id=1, source_target_pairs={{1,2},{3,0},{2,1},{0,3},{5,6},{7,4},{6,5},{4,7},{9,10},{11,8},{10,... | collective-permute-start | bytes 49160 | tf_op jit(solution)/shard_map/ppermute | solution.py:427
  26.9 2.4 %collective-permute-done.5.from_dy = f32[8,512]{1,0:T(8,128)S(1)} collective-permute-done((f32[8,512]{1,0:T(8,128)S(1)}, f32[8,512]{1,0:T(8,128)S(1)}, u32[]{:S(2)}, u32[]{:S(2)}) %collective-permute-start.5) | collective-permute-done | bytes 16416 | tf_op jit(solution)/shard_map/ppermute | solution.py:427
  29.3 1.7 %shard_map.116 = (f32[2,32,512]{2,1,0:T(8,128)S(1)}, f32[8,128]{1,0:T(8,128)S(1)}) custom-call(s32[1]{0:T(128)S(6)} %copy.36.live, s32[8]{0:T(128)S(1)} %copy-done.8, s32[8]{0:T(128)S(1)} %copy-done.9, bf16[8,1024,512]{2,1,0:T(8,128)(2,1)S(1)} %bitcast.20, f32[8,512]{1,0:T(8,128)S(1)} %add.27.sums, f32[16,2,32,512]{3,2,1,0:T(8,128)S(1)} %bitcast.25, ...), custom_call_target="tpu_custom_call" | custom-call | tf_op jit(solution)/shard_map/pallas_call | solution.py:27
  31.1 0.7 shard_map.117
  31.8 3.0 %collective-permute-start.8 = (f32[8,512]{1,0:T(8,128)S(1)}, f32[8,512]{1,0:T(8,128)S(1)}, u32[]{:S(2)}, u32[]{:S(2)}) collective-permute-start(f32[8,512]{1,0:T(8,128)S(1)} %get-tuple-element.46), channel_id=1, source_target_pairs={{0,1},{2,3},{1,0},{3,2},{4,5},{6,7},{5,4},{7,6},{8,9},{10,11},{9,8... | collective-permute-start | bytes 49160 | tf_op jit(solution)/shard_map/ppermute | solution.py:427
  34.7 0.5 collective-permute-start.10
  35.3 2.3 %collective-permute-start.11 = (f32[2,16,512]{2,1,0:T(8,128)S(1)}, f32[2,16,512]{2,1,0:T(8,128)S(1)}, u32[]{:S(2)}, u32[]{:S(2)}) collective-permute-start(f32[2,16,512]{2,1,0:T(8,128)S(1)} %get-tuple-element.51), channel_id=1, source_target_pairs={{4,8},{12,16},{20,24},{28,0},{8,4},{16,12},{24,20},{0,28},{5,9},{1... | collective-permute-start | bytes 196616 | tf_op jit(solution)/shard_map/ppermute | solution.py:427
  37.6 0.1 add_select_fusion.1
  37.7 0.5 collective-permute-start.9
  38.2 2.7 %collective-permute-done.9.from_dy = f32[8,512]{1,0:T(8,128)S(1)} collective-permute-done((f32[8,512]{1,0:T(8,128)S(1)}, f32[8,512]{1,0:T(8,128)S(1)}, u32[]{:S(2)}, u32[]{:S(2)}) %collective-permute-start.9) | collective-permute-done | bytes 16416 | tf_op jit(solution)/shard_map/ppermute | solution.py:427
  40.9 1.7 %shard_map.118 = (f32[2,32,512]{2,1,0:T(8,128)S(1)}, f32[8,128]{1,0:T(8,128)S(1)}) custom-call(s32[1]{0:T(128)S(6)} %copy.36.live, s32[8]{0:T(128)S(1)} %copy-done.8, s32[8]{0:T(128)S(1)} %copy-done.9, bf16[8,1024,512]{2,1,0:T(8,128)(2,1)S(1)} %bitcast.21, f32[8,512]{1,0:T(8,128)S(1)} %add.29.sums, f32[16,2,32,512]{3,2,1,0:T(8,128)S(1)} %bitcast.26, ...), custom_call_target="tpu_custom_call" | custom-call | tf_op jit(solution)/shard_map/pallas_call | solution.py:27
  42.6 0.7 shard_map.119
  43.3 3.2 %collective-permute-start.12 = (f32[8,512]{1,0:T(8,128)S(1)}, f32[8,512]{1,0:T(8,128)S(1)}, u32[]{:S(2)}, u32[]{:S(2)}) collective-permute-start(f32[8,512]{1,0:T(8,128)S(1)} %get-tuple-element.53), channel_id=1, source_target_pairs={{0,1},{2,3},{1,0},{3,2},{4,5},{6,7},{5,4},{7,6},{8,9},{10,11},{9,8... | collective-permute-start | bytes 49160 | tf_op jit(solution)/shard_map/ppermute | solution.py:427
  46.5 0.6 collective-permute-start.14
  47.1 1.7 %collective-permute-start.15 = (f32[2,16,512]{2,1,0:T(8,128)S(1)}, f32[2,16,512]{2,1,0:T(8,128)S(1)}, u32[]{:S(2)}, u32[]{:S(2)}) collective-permute-start(f32[2,16,512]{2,1,0:T(8,128)S(1)} %get-tuple-element.58), channel_id=1, source_target_pairs={{4,8},{12,16},{20,24},{28,0},{8,4},{16,12},{24,20},{0,28},{5,9},{1... | collective-permute-start | bytes 196616 | tf_op jit(solution)/shard_map/ppermute | solution.py:427
  48.9 0.1 add_select_fusion
  48.9 0.0 collective-permute-start.13
  48.9 8.7 %fusion.4 = f32[2,16,2,16]{1,3,0,2:T(8,128)S(1)} fusion(f32[16,2,2,16,512]{4,3,2,1,0:T(8,128)S(1)} %copy-done.3, f32[16,2,2,16,512,1]{4,3,2,1,0,5:T(8,128)S(1)} %bitcast.27), kind=kOutput, calls=%fused_computation.4 | convolution fusion | flops 201326592 | bytes 4198400 | tf_op jit(solution)/shard_map/icarl,jdarl->cidj/dot_general | solution.py:450
  57.6 0.1 copy.20
  57.7 0.1 reshape.26
  57.8 0.1 reshape.27
  57.9 0.0 copy-start.1
  57.9 3.4 %copy-done.1 = bf16[8,2,512,512]{3,2,1,0:T(8,128)(2,1)S(1)} copy-done((bf16[8,2,512,512]{3,2,1,0:T(8,128)(2,1)S(1)}, bf16[8,2,512,512]{3,2,1,0:T(8,128)(2,1)}, u32[]{:S(2)}) %copy-start.1) | copy-done | bytes 8388632
  61.3 1.7 %shard_map.120 = (f32[2,32,512]{2,1,0:T(8,128)S(1)}, f32[8,128]{1,0:T(8,128)S(1)}) custom-call(s32[1]{0:T(128)S(6)} %copy.36.live, s32[8]{0:T(128)S(1)} %copy-done.8, s32[8]{0:T(128)S(1)} %copy-done.9, bf16[8,1024,512]{2,1,0:T(8,128)(2,1)S(1)} %bitcast.22, f32[8,512]{1,0:T(8,128)S(1)} %add.31.sums, f32[16,2,32,512]{3,2,1,0:T(8,128)S(1)} %bitcast.28, ...), custom_call_target="tpu_custom_call" | custom-call | tf_op jit(solution)/shard_map/pallas_call | solution.py:27
  63.0 0.0 copy-start.11
  63.1 0.4 shard_map.121
  63.5 17.7 %all_to_all.5 = f32[32,16,128]{2,1,0:T(8,128)S(1)} all-to-all(f32[32,16,128]{2,1,0:T(8,128)S(1)} %broadcast_in_dim.2), channel_id=1, replica_groups=mesh['azim'=8,'dom'=4] {'azim','dom'}, dimensions={0} | all-to-all | bytes 524288 | tf_op jit(solution)/shard_map/all_to_all | solution.py:493
  81.3 2.4 %shard_map.122 = (f32[2,32,512]{2,1,0:T(8,128)}, f32[1,128]{1,0:T(1,128)S(1)}) custom-call(f32[2]{0:T(128)S(1)} %copy-done.11, f32[16,128]{1,0:T(8,128)S(1)} %reduce_sum.9.gram_s.gram, f32[16,128]{1,0:T(8,128)S(1)} %reduce_sum.9.gram_s.gram, f32[16,2,32,512]{3,2,1,0:T(8,128)S(1)} %bitcast.29, f32[2,32,512]{2,1,0:T(8,128)S(1)} %get-tuple-element.32.refs_0_.old.refs_7_, ...), custom_call_target="tpu_custom_call" | custom-call | tf_op jit(solution)/shard_map/pallas_call | solution.py:27
  83.7 0.5 slice_bitcast_fusion
  (37 shorter events, 0.2 us)
Async XLA Ops:
  0.6 14.5 %copy-start.9 = (s32[8]{0:T(128)S(1)}, s32[8]{0:T(128)}, u32[]{:S(2)}) copy-start(s32[8]{0:T(128)} %burners.7) | copy-start | bytes 100
  0.6 14.5 %copy-start.8 = (s32[8]{0:T(128)S(1)}, s32[8]{0:T(128)}, u32[]{:S(2)}) copy-start(s32[8]{0:T(128)} %lines.7) | copy-start | bytes 100
  0.7 1.6 %copy-start.2 = (f32[16,2,2,16,512]{4,3,2,1,0:T(8,128)S(1)}, f32[16,2,2,16,512]{4,3,2,1,0:T(8,128)}, u32[]{:S(2)}) copy-start(f32[16,2,2,16,512]{4,3,2,1,0:T(8,128)} %param.10) | copy-start | bytes 6291460
  2.3 0.7 copy-start.5
  2.9 0.7 copy-start.7
  3.6 0.7 copy-start.10
  4.2 10.9 %copy-start.3 = (f32[16,2,2,16,512]{4,3,2,1,0:T(8,128)S(1)}, f32[16,2,2,16,512]{4,3,2,1,0:T(8,128)}, u32[]{:S(2)}) copy-start(f32[16,2,2,16,512]{4,3,2,1,0:T(8,128)} %param.10) | copy-start | bytes 6291460
  5.1 6.7 %collective-permute-start = (f32[8,512]{1,0:T(8,128)S(1)}, f32[8,512]{1,0:T(8,128)S(1)}, u32[]{:S(2)}, u32[]{:S(2)}) collective-permute-start(f32[8,512]{1,0:T(8,128)S(1)} %get-tuple-element.33), channel_id=1, source_target_pairs={{0,1},{2,3},{1,0},{3,2},{4,5},{6,7},{5,4},{7,6},{8,9},{10,11},{9,8... | collective-permute-start | bytes 49160 | tf_op jit(solution)/shard_map/ppermute | solution.py:427
  5.7 14.6 %collective-permute-start.2 = (f32[2,16,512]{2,1,0:T(8,128)S(1)}, f32[2,16,512]{2,1,0:T(8,128)S(1)}, u32[]{:S(2)}, u32[]{:S(2)}) collective-permute-start(f32[2,16,512]{2,1,0:T(8,128)S(1)} %get-tuple-element.36), channel_id=1, source_target_pairs={{0,4},{8,12},{16,20},{24,28},{4,0},{12,8},{20,16},{28,24},{1,5},{9... | collective-permute-start | bytes 196616 | tf_op jit(solution)/shard_map/ppermute | solution.py:427
  8.3 12.0 %collective-permute-start.3 = (f32[2,16,512]{2,1,0:T(8,128)S(1)}, f32[2,16,512]{2,1,0:T(8,128)S(1)}, u32[]{:S(2)}, u32[]{:S(2)}) collective-permute-start(f32[2,16,512]{2,1,0:T(8,128)S(1)} %get-tuple-element.37), channel_id=1, source_target_pairs={{4,8},{12,16},{20,24},{28,0},{8,4},{16,12},{24,20},{0,28},{5,9},{1... | collective-permute-start | bytes 196616 | tf_op jit(solution)/shard_map/ppermute | solution.py:427
  11.9 3.3 %collective-permute-start.1 = (f32[8,512]{1,0:T(8,128)S(1)}, f32[8,512]{1,0:T(8,128)S(1)}, u32[]{:S(2)}, u32[]{:S(2)}) collective-permute-start(f32[8,512]{1,0:T(8,128)S(1)} %add_select_fusion.3), channel_id=1, source_target_pairs={{1,2},{3,0},{2,1},{0,3},{5,6},{7,4},{6,5},{4,7},{9,10},{11,8},{10,... | collective-permute-start | bytes 49160 | tf_op jit(solution)/shard_map/ppermute | solution.py:427
  15.2 3.4 %copy-start = (bf16[8,2,512,512]{3,2,1,0:T(8,128)(2,1)S(1)}, bf16[8,2,512,512]{3,2,1,0:T(8,128)(2,1)}, u32[]{:S(2)}) copy-start(bf16[8,2,512,512]{3,2,1,0:T(8,128)(2,1)} %param.14) | copy-start | bytes 25165828
  18.6 1.7 %copy-start.4 = (f32[2,16,512]{2,1,0:T(8,128)S(1)}, f32[2,16,512]{2,1,0:T(8,128)}, u32[]{:S(2)}) copy-start(f32[2,16,512]{2,1,0:T(8,128)} %param.13) | copy-start | bytes 196612
  18.6 1.7 %copy-start.6 = (s32[2]{0:T(128)S(1)}, s32[2]{0:T(128)}, u32[]{:S(2)}) copy-start(s32[2]{0:T(128)} %ref_part.7) | copy-start | bytes 28
  21.0 4.9 %collective-permute-start.4 = (f32[8,512]{1,0:T(8,128)S(1)}, f32[8,512]{1,0:T(8,128)S(1)}, u32[]{:S(2)}, u32[]{:S(2)}) collective-permute-start(f32[8,512]{1,0:T(8,128)S(1)} %get-tuple-element.39), channel_id=1, source_target_pairs={{0,1},{2,3},{1,0},{3,2},{4,5},{6,7},{5,4},{7,6},{8,9},{10,11},{9,8... | collective-permute-start | bytes 49160 | tf_op jit(solution)/shard_map/ppermute | solution.py:427
  24.1 7.0 %collective-permute-start.6 = (f32[2,16,512]{2,1,0:T(8,128)S(1)}, f32[2,16,512]{2,1,0:T(8,128)S(1)}, u32[]{:S(2)}, u32[]{:S(2)}) collective-permute-start(f32[2,16,512]{2,1,0:T(8,128)S(1)} %get-tuple-element.43), channel_id=1, source_target_pairs={{0,4},{8,12},{16,20},{24,28},{4,0},{12,8},{20,16},{28,24},{1,5},{9... | collective-permute-start | bytes 196616 | tf_op jit(solution)/shard_map/ppermute | solution.py:427
  24.1 7.0 %collective-permute-start.7 = (f32[2,16,512]{2,1,0:T(8,128)S(1)}, f32[2,16,512]{2,1,0:T(8,128)S(1)}, u32[]{:S(2)}, u32[]{:S(2)}) collective-permute-start(f32[2,16,512]{2,1,0:T(8,128)S(1)} %get-tuple-element.44), channel_id=1, source_target_pairs={{4,8},{12,16},{20,24},{28,0},{8,4},{16,12},{24,20},{0,28},{5,9},{1... | collective-permute-start | bytes 196616 | tf_op jit(solution)/shard_map/ppermute | solution.py:427
  26.0 3.3 %collective-permute-start.5 = (f32[8,512]{1,0:T(8,128)S(1)}, f32[8,512]{1,0:T(8,128)S(1)}, u32[]{:S(2)}, u32[]{:S(2)}) collective-permute-start(f32[8,512]{1,0:T(8,128)S(1)} %add_select_fusion.2), channel_id=1, source_target_pairs={{1,2},{3,0},{2,1},{0,3},{5,6},{7,4},{6,5},{4,7},{9,10},{11,8},{10,... | collective-permute-start | bytes 49160 | tf_op jit(solution)/shard_map/ppermute | solution.py:427
  31.8 5.8 %collective-permute-start.8 = (f32[8,512]{1,0:T(8,128)S(1)}, f32[8,512]{1,0:T(8,128)S(1)}, u32[]{:S(2)}, u32[]{:S(2)}) collective-permute-start(f32[8,512]{1,0:T(8,128)S(1)} %get-tuple-element.46), channel_id=1, source_target_pairs={{0,1},{2,3},{1,0},{3,2},{4,5},{6,7},{5,4},{7,6},{8,9},{10,11},{9,8... | collective-permute-start | bytes 49160 | tf_op jit(solution)/shard_map/ppermute | solution.py:427
  34.7 7.8 %collective-permute-start.10 = (f32[2,16,512]{2,1,0:T(8,128)S(1)}, f32[2,16,512]{2,1,0:T(8,128)S(1)}, u32[]{:S(2)}, u32[]{:S(2)}) collective-permute-start(f32[2,16,512]{2,1,0:T(8,128)S(1)} %get-tuple-element.50), channel_id=1, source_target_pairs={{0,4},{8,12},{16,20},{24,28},{4,0},{12,8},{20,16},{28,24},{1,5},{9... | collective-permute-start | bytes 196616 | tf_op jit(solution)/shard_map/ppermute | solution.py:427
  35.3 7.3 %collective-permute-start.11 = (f32[2,16,512]{2,1,0:T(8,128)S(1)}, f32[2,16,512]{2,1,0:T(8,128)S(1)}, u32[]{:S(2)}, u32[]{:S(2)}) collective-permute-start(f32[2,16,512]{2,1,0:T(8,128)S(1)} %get-tuple-element.51), channel_id=1, source_target_pairs={{4,8},{12,16},{20,24},{28,0},{8,4},{16,12},{24,20},{0,28},{5,9},{1... | collective-permute-start | bytes 196616 | tf_op jit(solution)/shard_map/ppermute | solution.py:427
  37.7 3.2 %collective-permute-start.9 = (f32[8,512]{1,0:T(8,128)S(1)}, f32[8,512]{1,0:T(8,128)S(1)}, u32[]{:S(2)}, u32[]{:S(2)}) collective-permute-start(f32[8,512]{1,0:T(8,128)S(1)} %add_select_fusion.1), channel_id=1, source_target_pairs={{1,2},{3,0},{2,1},{0,3},{5,6},{7,4},{6,5},{4,7},{9,10},{11,8},{10,... | collective-permute-start | bytes 49160 | tf_op jit(solution)/shard_map/ppermute | solution.py:427
  43.3 5.5 %collective-permute-start.12 = (f32[8,512]{1,0:T(8,128)S(1)}, f32[8,512]{1,0:T(8,128)S(1)}, u32[]{:S(2)}, u32[]{:S(2)}) collective-permute-start(f32[8,512]{1,0:T(8,128)S(1)} %get-tuple-element.53), channel_id=1, source_target_pairs={{0,1},{2,3},{1,0},{3,2},{4,5},{6,7},{5,4},{7,6},{8,9},{10,11},{9,8... | collective-permute-start | bytes 49160 | tf_op jit(solution)/shard_map/ppermute | solution.py:427
  46.5 16.5 %collective-permute-start.14 = (f32[2,16,512]{2,1,0:T(8,128)S(1)}, f32[2,16,512]{2,1,0:T(8,128)S(1)}, u32[]{:S(2)}, u32[]{:S(2)}) collective-permute-start(f32[2,16,512]{2,1,0:T(8,128)S(1)} %get-tuple-element.57), channel_id=1, source_target_pairs={{0,4},{8,12},{16,20},{24,28},{4,0},{12,8},{20,16},{28,24},{1,5},{9... | collective-permute-start | bytes 196616 | tf_op jit(solution)/shard_map/ppermute | solution.py:427
  47.1 15.9 %collective-permute-start.15 = (f32[2,16,512]{2,1,0:T(8,128)S(1)}, f32[2,16,512]{2,1,0:T(8,128)S(1)}, u32[]{:S(2)}, u32[]{:S(2)}) collective-permute-start(f32[2,16,512]{2,1,0:T(8,128)S(1)} %get-tuple-element.58), channel_id=1, source_target_pairs={{4,8},{12,16},{20,24},{28,0},{8,4},{16,12},{24,20},{0,28},{5,9},{1... | collective-permute-start | bytes 196616 | tf_op jit(solution)/shard_map/ppermute | solution.py:427
  48.9 8.9 %collective-permute-start.13 = (f32[8,512]{1,0:T(8,128)S(1)}, f32[8,512]{1,0:T(8,128)S(1)}, u32[]{:S(2)}, u32[]{:S(2)}) collective-permute-start(f32[8,512]{1,0:T(8,128)S(1)} %add_select_fusion), channel_id=1, source_target_pairs={{1,2},{3,0},{2,1},{0,3},{5,6},{7,4},{6,5},{4,7},{9,10},{11,8},{10,... | collective-permute-start | bytes 49160 | tf_op jit(solution)/shard_map/ppermute | solution.py:427
  57.9 3.4 %copy-start.1 = (bf16[8,2,512,512]{3,2,1,0:T(8,128)(2,1)S(1)}, bf16[8,2,512,512]{3,2,1,0:T(8,128)(2,1)}, u32[]{:S(2)}) copy-start(bf16[8,2,512,512]{3,2,1,0:T(8,128)(2,1)} %param.14) | copy-start | bytes 25165828
  63.0 18.2 %copy-start.11 = (f32[2]{0:T(128)S(1)}, f32[2]{0:T(128)}, u32[]{:S(2)}) copy-start(f32[2]{0:T(128)} %shift.1) | copy-start | bytes 28

commit v2 on v1

--- a/solution.py
+++ b/solution.py
@@ -10,6 +10,8 @@
 INNER_STEPS = 3
 EPSILON = 1e-06
 CENTRE = 7.125
+PARTS = 2
+START_LIMIT = 61 << 20
 HIGHEST = lax.Precision.HIGHEST
 VMEM = pltpu.VMEM
 SMEM = pltpu.SMEM
@@ -23,15 +25,22 @@
     return [pl.BlockSpec(memory_space=SMEM) for _ in range(count)]
 
 
-def call(kernel, outs, specs, args, scratch=(), cost=None, limit=16 << 20):
+def in_hbm(count):
+    return [pl.BlockSpec(memory_space=pltpu.HBM) for _ in range(count)]
+
+
+def call(kernel, outs, specs, args, scratch=(), cost=1, out_specs=None, limit=8 << 20):
+    estimate = pl.CostEstimate(flops=0, transcendentals=0, bytes_accessed=cost * 2_000_000)
+    if out_specs is None:
+        out_specs = jax.tree.map(lambda _: pl.BlockSpec(memory_space=VMEM), outs)
     return pl.pallas_call(
         kernel,
         out_shape=outs,
         in_specs=specs,
-        out_specs=jax.tree.map(lambda _: pl.BlockSpec(memory_space=VMEM), outs),
+        out_specs=out_specs,
         scratch_shapes=list(scratch),
         compiler_params=pltpu.CompilerParams(vmem_limit_bytes=limit),
-        cost_estimate=cost,
+        cost_estimate=estimate,
     )(*args)
 
 
@@ -52,7 +61,7 @@
             dom_x[at : at + 1, :] = field[c, pl.ds(x_row, 1), :]
             dom_y[at : at + 1, :] = field[c, pl.ds(y_row, 1), :]
     base = 2 * rows
-    for b in range(ref_part.shape[0]):
+    for b in range((dom_x.shape[0] - base) // 2):
         mine = ref_part[b] == part
         for c in range(2):
             at = base + 2 * b + c
@@ -61,51 +70,134 @@
             dom_y[at : at + 1, :] = jnp.zeros_like(line)
 
 
-def start_kernel(rows, depth, coef, ref_part, ref_line, basis, field, azim_x, azim_y, dom_x, dom_y):
+def start_kernel(
+    rows, depth, small, basis_in, field, azim_x, azim_y, dom_x, dom_y, basis, sems
+):
     count = basis.shape[0]
-    for a in range(rows):
-        span = slice(a * depth, (a + 1) * depth)
-        real = jnp.zeros((depth, basis.shape[3]), jnp.float32)
-        imag = real
-        for i in range(count):
+    copies = [pltpu.make_async_copy(basis_in.at[i], basis.at[i], sems.at[i]) for i in range(count)]
+    for copy in copies:
+        copy.start()
+    for i in range(count):
+        copies[i].wait()
+        one, two = small[i], small[count + i]
+        for a in range(rows):
+            span = slice(a * depth, (a + 1) * depth)
             re, im = basis[i, 0, span, :], basis[i, 1, span, :]
-            real = real + (coef[0, i] * re - coef[1, i] * im)
-            imag = imag + (coef[0, i] * im + coef[1, i] * re)
-        field[0, span, :] = real
-        field[1, span, :] = imag
-    write_edges(rows, depth, field, ref_part, ref_line, azim_x, azim_y, dom_x, dom_y)
-
-
-def flame_kernel(base, k, live, lines, burners, mats, sums, basis, *refs):
-    powers, (out, dots_out, source, held) = refs[: k + 1], refs[-4:]
+            real = one * re - two * im
+            imag = one * im + two * re
+            field[0, span, :] = real if i == 0 else field[0, span, :] + real
+            field[1, span, :] = imag if i == 0 else field[1, span, :] + imag
+    burners = (small.shape[0] - 2 * count) // 2
+    numbers = [small[2 * count + i].astype(jnp.int32) for i in range(2 * burners)]
+    write_edges(
+        rows, depth, field, numbers[:burners], numbers[burners:], azim_x, azim_y, dom_x, dom_y
+    )
+
+
+def basis_kernel(part, parts, basis, out, tiles):
+    half = basis.shape[0]
+    count = 2 * half
+    lines, width = basis.shape[2] // parts, basis.shape[3]
+    first = part * lines
+    for c in range(2):
+        for i in range(half):
+            for j in range(width // 128):
+                at = (c * half + i) * lines
+                tiles[j, at : at + lines, :] = basis[
+                    i, c, first : first + lines, j * 128 : (j + 1) * 128
+                ]
+
+    def one(line):
+        tall = jnp.concatenate(
+            [tiles.at[j][pl.ds(line, count, stride=lines), :] for j in range(width // 128)], axis=1
+        )
+        high = tall.astype(jnp.bfloat16)
+        low = (tall - high.astype(jnp.float32)).astype(jnp.bfloat16)
+        return jnp.concatenate([high, low], axis=0)
+
+    group = 4
+
+    def some(at, total):
+        both = jnp.concatenate([one(at * group + i) for i in range(group)], axis=1)
+        return total + lax.dot_general(
+            both, both, (((1,), (1,)), ((), ())), preferred_element_type=jnp.float32
+        )
+
+    zero = jnp.zeros((2 * count, 2 * count), jnp.float32)
+    total = lax.fori_loop(0, lines // group, some, zero)
+    total = total[:count] + total[count:]
+    total = jnp.concatenate([total, jnp.zeros((count, 128 - 2 * count), jnp.float32)], axis=1)
+    total = total + pltpu.roll(total, 128 - count, 1)
+    top, bottom = total[:half], total[half:]
+    crossed = pltpu.roll(top, 128 - half, 1)
+    lane = lax.broadcasted_iota(jnp.int32, (half, 128), 1)
+    table = jnp.where(
+        lane < half, top + pltpu.roll(bottom, 128 - half, 1) + crossed - bottom, 0.0
+    )
+    out[...] = jnp.zeros_like(out)
+    folds = 128 // half
+    for r in range(half // folds):
+        rows = [
+            pltpu.roll(table[r * folds + s : r * folds + s + 1], half * s, 1) if s
+            else table[r * folds : r * folds + 1]
+            for s in range(folds)
+        ]
+        out[5 + r : 6 + r, :] = total_of(rows)
+
+
+def dots_kernel(k, basis, *refs):
+    powers, (dots_out, held) = refs[: k + 1], refs[-2:]
     dots_in = refs[k + 1] if k else None
     add_dots(k, basis, powers[:-1], powers[-1], dots_in, dots_out, held)
+
+
+def flame_kernel(base, live, lines, burners, mats, sums, *refs):
+    out, source = refs[-2:]
     width = sums.shape[1]
-    count = (sums.shape[0] - base) // 2
-    for b in range(count):
-        for c in range(2):
-            row = sums[base + 2 * b + c : base + 2 * b + c + 1, :]
-            high = row.astype(jnp.bfloat16)
-            low = (row - high.astype(jnp.float32)).astype(jnp.bfloat16)
-            source[b, 2 * c : 2 * c + 1, :] = high
-            source[b, 2 * c + 1 : 2 * c + 2, :] = low
+    slots = mats.shape[0]
+    rows = sums.shape[0] - base
+    source[...] = jnp.zeros_like(source)
+    for i in range(rows):
+        row = sums[base + i : base + i + 1, :]
+        high = row.astype(jnp.bfloat16)
+        source[2 * i : 2 * i + 1, :] = high
+        source[2 * i + 1 : 2 * i + 2, :] = (row - high.astype(jnp.float32)).astype(jnp.bfloat16)
     out[...] = jnp.zeros_like(out)
-
-    def slot(s, carry):
-        product = lax.dot_general(
-            source[burners[s]],
-            mats[s],
-            (((1,), (1,)), ((), ())),
-            preferred_element_type=jnp.float32,
+    left = source[...]
+
+    def products(blocks):
+        return lax.dot_general(
+            left, blocks, (((1,), (1,)), ((), ())), preferred_element_type=jnp.float32
         )
-        by_re = product[0:1] + product[1:2]
-        by_im = product[2:3] + product[3:4]
+
+    def put(s, product):
+        chosen = product[0:4]
+        for b in range(1, rows // 2):
+            chosen = jnp.where(burners[s] == b, product[4 * b : 4 * b + 4], chosen)
+        by_re = chosen[0:1] + chosen[1:2]
+        by_im = chosen[2:3] + chosen[3:4]
         at = pl.ds(lines[s], 1)
         out[0, at, :] += by_re[:, :width] - by_im[:, width:]
         out[1, at, :] += by_im[:, :width] + by_re[:, width:]
-        return carry
-
-    lax.fori_loop(0, live[0], slot, 0)
+
+    few = 2
+
+    @pl.when(live[0] <= few)
+    def _():
+        def slot(s, carry):
+            put(s, products(mats[s]))
+            return carry
+
+        lax.fori_loop(0, live[0], slot, 0)
+
+    @pl.when(live[0] > few)
+    def _():
+        every = products(mats[...].reshape(slots * 2 * width, width))
+        for s in range(slots):
+
+            @pl.when(s < live[0])
+            def _():
+                put(s, every[:, 2 * width * s : 2 * width * (s + 1)])
 
 
 def step_kernel(
@@ -142,9 +234,11 @@
 
 
 def last_kernel(rows, depth, *refs):
-    first, powers, (dots_in, dots_out, field, held) = refs[:7], refs[7:-4], refs[-4:]
+    first, tables, powers = refs[:7], refs[7 : 7 + PARTS], refs[7 + PARTS : -4]
+    dots_in, dots_out, field, held = refs[-4:]
     step_kernel(rows, depth, None, None, *first, field, None, None, None, None)
     add_dots(len(powers), None, powers, field, dots_in, dots_out, held)
+    dots_out[...] += total_of(table[...] for table in tables)
 
 
 def folded(x):
@@ -334,8 +428,8 @@
         jnp.full(tile, CENTRE - shift[0], jnp.float32), jnp.full(tile, -shift[1], jnp.float32)
     )
     theta, update, update_sq = small_problem(table, mu)
-    lane = lax.broadcasted_iota(jnp.int32, (1, 128), 1)
-    ritz[...] = jnp.where(lane == 0, theta.re[0:1], theta.im[0:1])
+    ritz[0] = theta.re[0, 0]
+    ritz[1] = theta.im[0, 0]
 
     def lanes(x):
         return jnp.sum(x, axis=1, keepdims=True)
@@ -346,12 +440,15 @@
     def shifted(x, by):
         return pltpu.roll(x, 128 - by, 1)
 
-    packed = gram[8:16, :] * scale
-    folds = 128 // base
-    whole = jnp.concatenate([packed] + [shifted(packed, base * q) for q in range(1, folds)], axis=0)
-    top, bottom = whole[:count], whole[count:base]
-    g_re = top + shifted(bottom, count)
-    g_im = shifted(top, count) - bottom
+    folds = 128 // count
+    table = jnp.concatenate(
+        [
+            shifted(gram[5 + r : 6 + r, :], count * q) if q else gram[5 + r : 6 + r, :]
+            for r in range(count // folds)
+            for q in range(folds)
+        ],
+        axis=0,
+    )
     lane = lax.broadcasted_iota(jnp.int32, (count, 128), 1)
     same = lax.broadcasted_iota(jnp.int32, (count, 128), 0) == lane
     by_re = total_of(gram[k : k + 1, :] * v.re[0:1] for k, v in update.items()) * scale
@@ -359,15 +456,20 @@
     first_re = lanes(jnp.where(same, by_re - shifted(by_im, count), 0.0))
     first_im = lanes(jnp.where(same, by_im + shifted(by_re, count), 0.0))
 
+    table = jnp.where(lane < count, table, 0.0) * (0.5 * scale)
+
     def across(col):
         return sublanes(jnp.where(same, col, 0.0))
 
     def mixed(col_re, col_im):
-        row_re, row_im = across(col_re), across(col_im)
-        return (
-            lanes(g_re * row_re - g_im * row_im),
-            lanes(g_re * row_im + g_im * row_re),
-        )
+        def halves(col):
+            straight = lanes(table * across(col))
+            turned = lanes(jnp.where(same, sublanes(table * col), 0.0))
+            return straight + turned, straight - turned
+
+        re_re, im_re = halves(col_re)
+        re_im, im_im = halves(col_im)
+        return re_re - im_im, re_im + im_re
 
     mixed_re, mixed_im = mixed(first_re, first_im)
     second_re, second_im = first_re - mixed_re, first_im - mixed_im
@@ -418,7 +520,6 @@
     base = 2 * rows
     tall = base + 2 * reference_part.shape[0]
     basis = search_basis.reshape(count, 2, lines, width)
-    basis_rows = search_basis.reshape(count * 2 * lines, width)
     diag = stiffness_diag.reshape(lines, width)
     mats = flame_mats.reshape(slots, 2 * width, width)
 
@@ -441,14 +542,34 @@
         shape(tall, width),
         shape(tall, width),
     ]
-    here = functools.partial(start_kernel, rows, depth)
-    power, azim_x, azim_y, dom_x, dom_y = call(
-        here, fields, smem(3) + vmem(1), (coefficients, reference_part, reference_line, basis)
+    small = jnp.concatenate(
+        [
+            coefficients.reshape(-1),
+            reference_part.astype(jnp.float32),
+            reference_line.astype(jnp.float32),
+        ]
+    )
+    power, azim_x, azim_y, dom_x, dom_y, basis = call(
+        functools.partial(start_kernel, rows, depth),
+        [*fields, shape(count, 2, lines, width)],
+        smem(1) + in_hbm(1),
+        (small, basis),
+        [pltpu.SemaphoreType.DMA((count,))],
+        cost=4,
+        limit=START_LIMIT,
     )
     powers = [power]
     held = VMEM((2 * count + 16, 128), jnp.float32)
-    cross = jnp.einsum("icarl,jdarl->cidj", search_basis, search_basis, precision=HIGHEST)
-    folded_gram = cross.reshape(-1, 8, 2 * count).transpose(1, 0, 2).reshape(8, 8 * count)
+    tables = [
+        call(
+            functools.partial(basis_kernel, part, PARTS),
+            shape(8, 128),
+            vmem(1),
+            (basis,),
+            [VMEM((width // 128, count * 2 * (lines // PARTS), 128), jnp.float32)],
+        )
+        for part in range(PARTS)
+    ]
     is_sum = lax.broadcasted_iota(jnp.int32, (tall, width), 0) >= base
     for step in range(INNER_STEPS + 1):
         from_ay = exchange(azim_y, "azim", azim_odd)
@@ -462,13 +583,18 @@
             pairs = [(i, i ^ reach) for i in range(n_dom) if i < i ^ reach]
             sums = sums + exchange(sums, "dom", pairs)
             reach *= 2
-        given = (mats, sums, basis, *powers, *([dots] if step else []))
-        flame, dots = call(
-            functools.partial(flame_kernel, base, step),
-            [shape(2, lines, width), shape(8, 128)],
-            smem(3) + vmem(len(given)),
-            (flame_count, flame_line, flame_burner, *given),
-            [VMEM((reference_part.shape[0], 16, width), jnp.bfloat16), held],
+        given = (basis, *powers, *([dots] if step else []))
+        dots = call(
+            functools.partial(dots_kernel, step), shape(8, 128), vmem(len(given)), given, [held]
+        )
+        order = (dots, *tables[step - 1 : step]) if step else (dots,)
+        flame = call(
+            functools.partial(flame_kernel, base),
+            shape(2, lines, width),
+            smem(3) + vmem(2 + len(order)),
+            (flame_count, flame_line, flame_burner, mats, sums, *order),
+            [VMEM((16, width), jnp.bfloat16)],
+            cost=3,
         )
         received = (power, flame, diag, from_ax, from_ay, from_dx, from_dy)
         if step < INNER_STEPS:
@@ -482,23 +608,23 @@
             dots = call(
                 functools.partial(last_kernel, rows, depth),
                 shape(8, 128),
-                vmem(8 + len(powers)),
-                (*received, *powers, dots),
+                vmem(8 + len(tables) + len(powers)),
+                (*received, *tables, *powers, dots),
                 [VMEM((2, lines, width), jnp.float32), held],
             )
         powers.append(power)
     devices = n_azim * n_dom
-    packed = jnp.concatenate([dots, folded_gram], axis=0)
-    spread = jnp.broadcast_to(packed[None], (devices, *packed.shape))
+    spread = jnp.broadcast_to(dots[None], (devices, *dots.shape))
     gram = jnp.sum(lax.all_to_all(spread, ("azim", "dom"), 0, 0), axis=0)
     new_vector, ritz = call(
         functools.partial(end_kernel, rows, depth, scale),
-        [shape(2, lines, width), shape(1, 128)],
+        [shape(2, lines, width), shape(2)],
         smem(2) + vmem(2 + INNER_STEPS + 1),
         (target_shift, gram, gram, basis, *powers[: INNER_STEPS + 1]),
         [VMEM((2, count, 128), jnp.float32)],
-    )
-    return new_vector.reshape(2, rows, depth, width), ritz[0, :2]
+        out_specs=[pl.BlockSpec(memory_space=VMEM), pl.BlockSpec(memory_space=SMEM)],
+    )
+    return new_vector.reshape(2, rows, depth, width), ritz
 
 
 def solution(mesh):

time: 84.4 us -> 70.2 us (0.83)
  matrix products: 8.66 us -> 0 us
  blocking collectives: 17.7 us -> 12.5 us
  Pallas kernels: 12.6 us -> 17.1 us
  local copies, waits for them, and re-layouts: 11.2 us -> 6.94 us
  starting transfers between devices: 25.3 us -> 22.4 us
  other arithmetic: 0.35 us -> 3 us
    dot_general x1 -> x0, matrix products: 8.66 us -> none  [on_device(): jnp.einsum('icarl,jdarl->cidj', search_basis, search_basis, precision=HIG...]
    all_to_all x1, blocking collectives: 17.7 us -> 12.5 us  [on_device(): gram = jnp.sum(lax.all_to_all(spread, ('azim', 'dom'), 0, 0), axis=0)]
    pallas_call x10 -> x16, Pallas kernels: 12.6 us -> 17.1 us  [call(): pl.pallas_call(kernel, out_shape=outs, in_specs=specs, out_specs=out_spec...]
    unnamed x24, local copies, waits for them, and re-layouts: 10.4 us -> 6.16 us
    ppermute x16, starting transfers between devices: 25.3 us -> 22.4 us  [exchange(): return lax.ppermute(values, axis, both)]
    convert_element_type x0 -> x2, other arithmetic: none -> 1.31 us  [the longest x1 0.66 us: on_device(): reference_part.astype(jnp.float32)]
  transfers between devices with their start and end apart: 16 -> 16, of which waited for: 3 -> 6; matrix products, arithmetic and copies ran while one was open for 11% -> 2% of each run, Pallas kernels for 8% -> 12%
where the time goes in v2:
time: 70.2 us; the launch traced here: 69.5 us
  starting transfers between devices  22.4 us (32%)
  Pallas kernels  17.1 us (24%)
  blocking collectives  12.5 us (18%)
  local copies, waits for them, and re-layouts  6.94 us (10%)
  waiting for transfers between devices  6.07 us (9%)
  other arithmetic  3 us (4%)
  between operations  1.52 us (2%)
    ppermute x16, starting transfers between devices, exchange(): return lax.ppermute(values, axis, both)  22.4 us
    pallas_call x16, Pallas kernels, call(): pl.pallas_call(kernel, out_shape=outs, in_specs=specs, out_specs=out_spec...  17.1 us
    all_to_all x1, blocking collectives, on_device(): gram = jnp.sum(lax.all_to_all(spread, ('azim', 'dom'), 0, 0), axis=0)  12.5 us
    unnamed x24, local copies, waits for them, and re-layouts  6.16 us
    ppermute x16, waiting for transfers between devices, exchange(): return lax.ppermute(values, axis, both)  6.07 us
  transfers between devices with their start and end apart: 16, of which 6 were waited for; matrix products, arithmetic and copies ran while one was open for 2% of the time, Pallas kernels for 12%

profile of v2, /device:TPU:0, one launch (start us, length us, event | category | flops | bytes accessed | tf_op | source)
XLA Modules:
  0.0 69.5 jit_solution(16006795236604502163)
XLA Ops:
  0.6 0.8 %reshape.20 = f32[32]{0:T(128)S(1)} reshape(f32[2,16]{1,0:T(2,128)} %param.11) | data formatting | bytes 256 | tf_op jit(solution)/shard_map/reshape | solution.py:547
  1.4 0.7 convert_element_type.6
  2.0 0.7 convert_element_type.7
  2.7 0.6 pad_maximum_fusion.small
  3.3 3.9 %shard_map.113 = (f32[2,32,512]{2,1,0:T(8,128)}, f32[2,16,512]{2,1,0:T(8,128)}, f32[2,16,512]{2,1,0:T(8,128)}, f32[8,512]{1,0:T(8,128)}, f32[8,512]{1,0:T(8,128)}, /*index=5*/f32[16,2,32,512]{3,2,1,0:T(8,128)}) custom-call(f32[36]{0:T(128)} %pad_maximum_fusion.small, f32[16,2,32,512]{3,2,1,0:T(8,128)} %bitcast.12), custom_call_target="tpu_custom_call" | custom-call | bytes 8000000 | tf_op jit(solution)/shard_map/pallas_call | solution.py:36
  7.3 0.6 collective-permute-start
  7.8 2.6 %collective-permute-start.2 = (f32[2,16,512]{2,1,0:T(8,128)}, f32[2,16,512]{2,1,0:T(8,128)S(1)}, u32[]{:S(2)}, u32[]{:S(2)}) collective-permute-start(f32[2,16,512]{2,1,0:T(8,128)} %get-tuple-element.29), channel_id=1, source_target_pairs={{0,4},{8,12},{16,20},{24,28},{4,0},{12,8},{20,16},{28,24},{1,5},{9... | collective-permute-start | bytes 196616 | tf_op jit(solution)/shard_map/ppermute | solution.py:528
  10.4 3.5 %collective-permute-start.3 = (f32[2,16,512]{2,1,0:T(8,128)}, f32[2,16,512]{2,1,0:T(8,128)S(1)}, u32[]{:S(2)}, u32[]{:S(2)}) collective-permute-start(f32[2,16,512]{2,1,0:T(8,128)} %get-tuple-element.30), channel_id=1, source_target_pairs={{4,8},{12,16},{20,24},{28,0},{8,4},{16,12},{24,20},{0,28},{5,9},{1... | collective-permute-start | bytes 196616 | tf_op jit(solution)/shard_map/ppermute | solution.py:528
  13.9 0.8 %add_select_fusion.3 = f32[8,512]{1,0:T(8,128)S(1)} fusion(f32[8,512]{1,0:T(8,128)} %get-tuple-element.27, f32[8,512]{1,0:T(8,128)} %get-tuple-element.26, f32[8,512]{1,0:T(8,128)S(1)} %collective-permute-done.from_dx, pred[8]{0:T(512)(128)(4,1)S(1)} %iota_compare_fusion), kind=kLoop, calls=%fused_computation.3 | loop fusion | flops 8192 | bytes 65544 | tf_op jit(solution)/shard_map/jit(_where)/select_n | solution.py:577
  14.8 1.0 %collective-permute-start.1 = (f32[8,512]{1,0:T(8,128)S(1)}, f32[8,512]{1,0:T(8,128)S(1)}, u32[]{:S(2)}, u32[]{:S(2)}) collective-permute-start(f32[8,512]{1,0:T(8,128)S(1)} %add_select_fusion.3), channel_id=1, source_target_pairs={{1,2},{3,0},{2,1},{0,3},{5,6},{7,4},{6,5},{4,7},{9,10},{11,8},{10,... | collective-permute-start | bytes 49160 | tf_op jit(solution)/shard_map/ppermute | solution.py:528
  16.4 1.6 %copy-done.2 = f32[16,2,32,512]{3,2,1,0:T(8,128)S(1)} copy-done((f32[16,2,32,512]{3,2,1,0:T(8,128)S(1)}, f32[16,2,32,512]{3,2,1,0:T(8,128)}, u32[]{:S(2)}) %copy-start.2) | copy-done | bytes 2097176
  18.0 0.9 %copy-done.4 = f32[2,32,512]{2,1,0:T(8,128)S(1)} copy-done((f32[2,32,512]{2,1,0:T(8,128)S(1)}, f32[2,32,512]{2,1,0:T(8,128)}, u32[]{:S(2)}) %copy-start.4) | copy-done | bytes 131096
  18.9 0.7 %shard_map.114.refs_0_.refs_2_ = f32[8,128]{1,0:T(8,128)S(1)} custom-call(f32[16,2,32,512]{3,2,1,0:T(8,128)S(1)} %copy-done.2, f32[2,32,512]{2,1,0:T(8,128)S(1)} %copy-done.4), custom_call_target="tpu_custom_call" | custom-call | bytes 2000000 | tf_op jit(solution)/shard_map/pallas_call | solution.py:36
  19.7 3.4 %copy-done = bf16[8,2,512,512]{3,2,1,0:T(8,128)(2,1)S(1)} copy-done((bf16[8,2,512,512]{3,2,1,0:T(8,128)(2,1)S(1)}, bf16[8,2,512,512]{3,2,1,0:T(8,128)(2,1)}, u32[]{:S(2)}) %copy-start) | copy-done | bytes 8388632
  23.1 0.6 shard_map.115.flame
  23.7 0.3 copy-done.5
  24.0 0.7 %shard_map.116 = (f32[2,32,512]{2,1,0:T(8,128)S(1)}, f32[2,16,512]{2,1,0:T(8,128)S(1)}, f32[2,16,512]{2,1,0:T(8,128)S(1)}, f32[8,512]{1,0:T(8,128)S(1)}, f32[8,512]{1,0:T(8,128)S(1)}) custom-call(s32[2]{0:T(128)S(1)} %copy-done.9, s32[2]{0:T(128)S(1)} %copy-done.10, f32[2,32,512]{2,1,0:T(8,128)S(1)} %copy-done.5, f32[2,32,512]{2,1,0:T(8,128)S(1)} %shard_map.115.flame, ...), custom_call_target="tpu_custom_call" | custom-call | bytes 2000000 | tf_op jit(solution)/shard_map/pallas_call | solution.py:36
  24.7 0.7 %collective-permute-start.4 = (f32[8,512]{1,0:T(8,128)S(1)}, f32[8,512]{1,0:T(8,128)S(1)}, u32[]{:S(2)}, u32[]{:S(2)}) collective-permute-start(f32[8,512]{1,0:T(8,128)S(1)} %get-tuple-element.32), channel_id=1, source_target_pairs={{0,1},{2,3},{1,0},{3,2},{4,5},{6,7},{5,4},{7,6},{8,9},{10,11},{9,8... | collective-permute-start | bytes 49160 | tf_op jit(solution)/shard_map/ppermute | solution.py:528
  25.4 1.7 %collective-permute-start.6 = (f32[2,16,512]{2,1,0:T(8,128)S(1)}, f32[2,16,512]{2,1,0:T(8,128)S(1)}, u32[]{:S(2)}, u32[]{:S(2)}) collective-permute-start(f32[2,16,512]{2,1,0:T(8,128)S(1)} %get-tuple-element.34), channel_id=1, source_target_pairs={{0,4},{8,12},{16,20},{24,28},{4,0},{12,8},{20,16},{28,24},{1,5},{9... | collective-permute-start | bytes 196616 | tf_op jit(solution)/shard_map/ppermute | solution.py:528
  27.1 2.4 %collective-permute-start.7 = (f32[2,16,512]{2,1,0:T(8,128)S(1)}, f32[2,16,512]{2,1,0:T(8,128)S(1)}, u32[]{:S(2)}, u32[]{:S(2)}) collective-permute-start(f32[2,16,512]{2,1,0:T(8,128)S(1)} %get-tuple-element.35), channel_id=1, source_target_pairs={{4,8},{12,16},{20,24},{28,0},{8,4},{16,12},{24,20},{0,28},{5,9},{1... | collective-permute-start | bytes 196616 | tf_op jit(solution)/shard_map/ppermute | solution.py:528
  29.5 0.1 add_select_fusion.2
  29.6 1.5 %shard_map.118.refs_1_.refs_7_ = f32[8,128]{1,0:T(8,128)S(1)} custom-call(f32[16,2,32,512]{3,2,1,0:T(8,128)S(1)} %copy-done.3), custom_call_target="tpu_custom_call" | custom-call | bytes 2000000 | tf_op jit(solution)/shard_map/pallas_call | solution.py:36
  31.1 0.8 %shard_map.117.refs_0_.refs_3_ = f32[8,128]{1,0:T(8,128)S(1)} custom-call(f32[16,2,32,512]{3,2,1,0:T(8,128)S(1)} %copy-done.3, f32[2,32,512]{2,1,0:T(8,128)S(1)} %copy-done.5, f32[2,32,512]{2,1,0:T(8,128)S(1)} %get-tuple-element.31.refs_1_.old.refs_10_, f32[8,128]{1,0:T(8,128)S(1)} %shard_map.114.refs_0_.refs_2_), custom_call_target="tpu_custom_call" | custom-call | bytes 2000000 | tf_op jit(solution)/shard_map/pallas_call | solution.py:36
  31.9 0.9 %collective-permute-done.5.from_dy = f32[8,512]{1,0:T(8,128)S(1)} collective-permute-done((f32[8,512]{1,0:T(8,128)S(1)}, f32[8,512]{1,0:T(8,128)S(1)}, u32[]{:S(2)}, u32[]{:S(2)}) %collective-permute-start.5) | collective-permute-done | bytes 16416 | tf_op jit(solution)/shard_map/ppermute | solution.py:528
  32.8 0.6 shard_map.119.flame
  33.4 0.7 collective-permute-done.7.from_ay
  34.1 0.7 %shard_map.120 = (f32[2,32,512]{2,1,0:T(8,128)S(1)}, f32[2,16,512]{2,1,0:T(8,128)S(1)}, f32[2,16,512]{2,1,0:T(8,128)S(1)}, f32[8,512]{1,0:T(8,128)S(1)}, f32[8,512]{1,0:T(8,128)S(1)}) custom-call(s32[2]{0:T(128)S(1)} %copy-done.9, s32[2]{0:T(128)S(1)} %copy-done.10, f32[2,32,512]{2,1,0:T(8,128)S(1)} %get-tuple-element.31.refs_1_.old.refs_10_, ...), custom_call_target="tpu_custom_call" | custom-call | bytes 2000000 | tf_op jit(solution)/shard_map/pallas_call | solution.py:36
  34.9 2.1 %collective-permute-start.10 = (f32[2,16,512]{2,1,0:T(8,128)S(1)}, f32[2,16,512]{2,1,0:T(8,128)S(1)}, u32[]{:S(2)}, u32[]{:S(2)}) collective-permute-start(f32[2,16,512]{2,1,0:T(8,128)S(1)} %get-tuple-element.39), channel_id=1, source_target_pairs={{0,4},{8,12},{16,20},{24,28},{4,0},{12,8},{20,16},{28,24},{1,5},{9... | collective-permute-start | bytes 196616 | tf_op jit(solution)/shard_map/ppermute | solution.py:528
  37.0 2.1 %collective-permute-start.11 = (f32[2,16,512]{2,1,0:T(8,128)S(1)}, f32[2,16,512]{2,1,0:T(8,128)S(1)}, u32[]{:S(2)}, u32[]{:S(2)}) collective-permute-start(f32[2,16,512]{2,1,0:T(8,128)S(1)} %get-tuple-element.40), channel_id=1, source_target_pairs={{4,8},{12,16},{20,24},{28,0},{8,4},{16,12},{24,20},{0,28},{5,9},{1... | collective-permute-start | bytes 196616 | tf_op jit(solution)/shard_map/ppermute | solution.py:528
  39.1 0.1 add_select_fusion.1
  39.2 0.7 collective-permute-start.9
  39.8 1.5 %shard_map.122.refs_1_.refs_8_ = f32[8,128]{1,0:T(8,128)S(1)} custom-call(f32[16,2,32,512]{3,2,1,0:T(8,128)S(1)} %copy-done.3), custom_call_target="tpu_custom_call" | custom-call | bytes 2000000 | tf_op jit(solution)/shard_map/pallas_call | solution.py:36
  41.3 0.8 %shard_map.121.refs_0_.refs_4_ = f32[8,128]{1,0:T(8,128)S(1)} custom-call(f32[16,2,32,512]{3,2,1,0:T(8,128)S(1)} %copy-done.3, f32[2,32,512]{2,1,0:T(8,128)S(1)} %copy-done.5, f32[2,32,512]{2,1,0:T(8,128)S(1)} %get-tuple-element.31.refs_1_.old.refs_10_, f32[2,32,512]{2,1,0:T(8,128)S(1)} %get-tuple-element.36.refs_2_.old.refs_11_, ...), custom_call_target="tpu_custom_call" | custom-call | bytes 2000000 | tf_op jit(solution)/shard_map/pallas_call | solution.py:36
  42.1 0.3 collective-permute-done.9.from_dy
  42.3 0.6 shard_map.123.flame
  43.0 1.0 %collective-permute-done.11.from_ay = f32[2,16,512]{2,1,0:T(8,128)S(1)} collective-permute-done((f32[2,16,512]{2,1,0:T(8,128)S(1)}, f32[2,16,512]{2,1,0:T(8,128)S(1)}, u32[]{:S(2)}, u32[]{:S(2)}) %collective-permute-start.11) | collective-permute-done | bytes 65568 | tf_op jit(solution)/shard_map/ppermute | solution.py:528
  44.0 0.7 %shard_map.124 = (f32[2,32,512]{2,1,0:T(8,128)S(1)}, f32[2,16,512]{2,1,0:T(8,128)S(1)}, f32[2,16,512]{2,1,0:T(8,128)S(1)}, f32[8,512]{1,0:T(8,128)S(1)}, f32[8,512]{1,0:T(8,128)S(1)}) custom-call(s32[2]{0:T(128)S(1)} %copy-done.9, s32[2]{0:T(128)S(1)} %copy-done.10, f32[2,32,512]{2,1,0:T(8,128)S(1)} %get-tuple-element.36.refs_2_.old.refs_11_, ...), custom_call_target="tpu_custom_call" | custom-call | bytes 2000000 | tf_op jit(solution)/shard_map/pallas_call | solution.py:36
  44.8 2.5 %collective-permute-start.14 = (f32[2,16,512]{2,1,0:T(8,128)S(1)}, f32[2,16,512]{2,1,0:T(8,128)S(1)}, u32[]{:S(2)}, u32[]{:S(2)}) collective-permute-start(f32[2,16,512]{2,1,0:T(8,128)S(1)} %get-tuple-element.44), channel_id=1, source_target_pairs={{0,4},{8,12},{16,20},{24,28},{4,0},{12,8},{20,16},{28,24},{1,5},{9... | collective-permute-start | bytes 196616 | tf_op jit(solution)/shard_map/ppermute | solution.py:528
  47.3 1.8 %collective-permute-start.15 = (f32[2,16,512]{2,1,0:T(8,128)S(1)}, f32[2,16,512]{2,1,0:T(8,128)S(1)}, u32[]{:S(2)}, u32[]{:S(2)}) collective-permute-start(f32[2,16,512]{2,1,0:T(8,128)S(1)} %get-tuple-element.45), channel_id=1, source_target_pairs={{4,8},{12,16},{20,24},{28,0},{8,4},{16,12},{24,20},{0,28},{5,9},{1... | collective-permute-start | bytes 196616 | tf_op jit(solution)/shard_map/ppermute | solution.py:528
  49.1 0.1 add_select_fusion
  49.2 0.5 collective-permute-start.13
  49.7 0.8 %shard_map.125.refs_0_.refs_13_ = f32[8,128]{1,0:T(8,128)S(1)} custom-call(f32[16,2,32,512]{3,2,1,0:T(8,128)S(1)} %copy-done.3, f32[2,32,512]{2,1,0:T(8,128)S(1)} %copy-done.5, f32[2,32,512]{2,1,0:T(8,128)S(1)} %get-tuple-element.31.refs_1_.old.refs_10_, f32[2,32,512]{2,1,0:T(8,128)S(1)} %get-tuple-element.36.refs_2_.old.refs_11_, ...), custom_call_target="tpu_custom_call" | custom-call | bytes 2000000 | tf_op jit(solution)/shard_map/pallas_call | solution.py:36
  50.5 1.9 %collective-permute-done.13.refs_6_ = f32[8,512]{1,0:T(8,128)S(1)} collective-permute-done((f32[8,512]{1,0:T(8,128)S(1)}, f32[8,512]{1,0:T(8,128)S(1)}, u32[]{:S(2)}, u32[]{:S(2)}) %collective-permute-start.13) | collective-permute-done | bytes 16416 | tf_op jit(solution)/shard_map/ppermute | solution.py:528
  52.4 0.6 shard_map.126.refs_1_
  53.0 1.3 %collective-permute-done.15.refs_4_ = f32[2,16,512]{2,1,0:T(8,128)S(1)} collective-permute-done((f32[2,16,512]{2,1,0:T(8,128)S(1)}, f32[2,16,512]{2,1,0:T(8,128)S(1)}, u32[]{:S(2)}, u32[]{:S(2)}) %collective-permute-start.15) | collective-permute-done | bytes 65568 | tf_op jit(solution)/shard_map/ppermute | solution.py:528
  54.3 0.4 shard_map.127
  54.7 12.5 %all_to_all.5 = f32[32,8,128]{2,1,0:T(8,128)S(1)} all-to-all(f32[32,8,128]{2,1,0:T(8,128)S(1)} %broadcast_in_dim.2), channel_id=1, replica_groups=mesh['azim'=8,'dom'=4] {'azim','dom'}, dimensions={0} | all-to-all | bytes 262144 | tf_op jit(solution)/shard_map/all_to_all | solution.py:618
  67.2 2.3 %shard_map.128 = (f32[2,32,512]{2,1,0:T(8,128)}, f32[2]{0:T(128)}) custom-call(f32[2]{0:T(128)S(1)} %copy-done.11, f32[8,128]{1,0:T(8,128)S(1)} %reduce_sum.9.gram_s.gram, f32[8,128]{1,0:T(8,128)S(1)} %reduce_sum.9.gram_s.gram, f32[16,2,32,512]{3,2,1,0:T(8,128)S(1)} %copy-done.3, f32[2,32,512]{2,1,0:T(8,128)S(1)} %copy-done.5, ...), custom_call_target="tpu_custom_call" | custom-call | bytes 2000000 | tf_op jit(solution)/shard_map/pallas_call | solution.py:36
  (40 shorter events, 0.3 us)
Async XLA Ops:
  3.3 16.3 %copy-start.7 = (s32[8]{0:T(128)S(1)}, s32[8]{0:T(128)}, u32[]{:S(2)}) copy-start(s32[8]{0:T(128)} %lines.7) | copy-start | bytes 100
  3.3 16.4 %copy-start.8 = (s32[8]{0:T(128)S(1)}, s32[8]{0:T(128)}, u32[]{:S(2)}) copy-start(s32[8]{0:T(128)} %burners.7) | copy-start | bytes 100
  7.3 6.7 %collective-permute-start = (f32[8,512]{1,0:T(8,128)}, f32[8,512]{1,0:T(8,128)S(1)}, u32[]{:S(2)}, u32[]{:S(2)}) collective-permute-start(f32[8,512]{1,0:T(8,128)} %get-tuple-element.26), channel_id=1, source_target_pairs={{0,1},{2,3},{1,0},{3,2},{4,5},{6,7},{5,4},{7,6},{8,9},{10,11},{9,8... | collective-permute-start | bytes 49160 | tf_op jit(solution)/shard_map/ppermute | solution.py:528
  7.8 15.8 %collective-permute-start.2 = (f32[2,16,512]{2,1,0:T(8,128)}, f32[2,16,512]{2,1,0:T(8,128)S(1)}, u32[]{:S(2)}, u32[]{:S(2)}) collective-permute-start(f32[2,16,512]{2,1,0:T(8,128)} %get-tuple-element.29), channel_id=1, source_target_pairs={{0,4},{8,12},{16,20},{24,28},{4,0},{12,8},{20,16},{28,24},{1,5},{9... | collective-permute-start | bytes 196616 | tf_op jit(solution)/shard_map/ppermute | solution.py:528
  10.4 13.3 %collective-permute-start.3 = (f32[2,16,512]{2,1,0:T(8,128)}, f32[2,16,512]{2,1,0:T(8,128)S(1)}, u32[]{:S(2)}, u32[]{:S(2)}) collective-permute-start(f32[2,16,512]{2,1,0:T(8,128)} %get-tuple-element.30), channel_id=1, source_target_pairs={{4,8},{12,16},{20,24},{28,0},{8,4},{16,12},{24,20},{0,28},{5,9},{1... | collective-permute-start | bytes 196616 | tf_op jit(solution)/shard_map/ppermute | solution.py:528
  14.8 4.9 %collective-permute-start.1 = (f32[8,512]{1,0:T(8,128)S(1)}, f32[8,512]{1,0:T(8,128)S(1)}, u32[]{:S(2)}, u32[]{:S(2)}) collective-permute-start(f32[8,512]{1,0:T(8,128)S(1)} %add_select_fusion.3), channel_id=1, source_target_pairs={{1,2},{3,0},{2,1},{0,3},{5,6},{7,4},{6,5},{4,7},{9,10},{11,8},{10,... | collective-permute-start | bytes 49160 | tf_op jit(solution)/shard_map/ppermute | solution.py:528
  16.4 1.6 %copy-start.2 = (f32[16,2,32,512]{3,2,1,0:T(8,128)S(1)}, f32[16,2,32,512]{3,2,1,0:T(8,128)}, u32[]{:S(2)}) copy-start(f32[16,2,32,512]{3,2,1,0:T(8,128)} %get-tuple-element.28.basis) | copy-start | bytes 6291460
  18.0 0.9 %copy-start.4 = (f32[2,32,512]{2,1,0:T(8,128)S(1)}, f32[2,32,512]{2,1,0:T(8,128)}, u32[]{:S(2)}) copy-start(f32[2,32,512]{2,1,0:T(8,128)} %get-tuple-element.25.refs_0_.old.refs_9_) | copy-start | bytes 393220
  18.9 4.8 %copy-start.6 = (f32[2,16,512]{2,1,0:T(8,128)S(1)}, f32[2,16,512]{2,1,0:T(8,128)}, u32[]{:S(2)}) copy-start(f32[2,16,512]{2,1,0:T(8,128)} %param.13) | copy-start | bytes 196612
  18.9 10.7 %copy-start.3 = (f32[16,2,32,512]{3,2,1,0:T(8,128)S(1)}, f32[16,2,32,512]{3,2,1,0:T(8,128)}, u32[]{:S(2)}) copy-start(f32[16,2,32,512]{3,2,1,0:T(8,128)} %get-tuple-element.28.basis) | copy-start | bytes 6291460
  19.7 3.4 %copy-start = (bf16[8,2,512,512]{3,2,1,0:T(8,128)(2,1)S(1)}, bf16[8,2,512,512]{3,2,1,0:T(8,128)(2,1)}, u32[]{:S(2)}) copy-start(bf16[8,2,512,512]{3,2,1,0:T(8,128)(2,1)} %param.14) | copy-start | bytes 25165828
  23.0 0.9 %copy-start.5 = (f32[2,32,512]{2,1,0:T(8,128)S(1)}, f32[2,32,512]{2,1,0:T(8,128)}, u32[]{:S(2)}) copy-start(f32[2,32,512]{2,1,0:T(8,128)} %get-tuple-element.25.refs_0_.old.refs_9_) | copy-start | bytes 393220
  23.0 0.9 %copy-start.9 = (s32[2]{0:T(128)S(1)}, s32[2]{0:T(128)}, u32[]{:S(2)}) copy-start(s32[2]{0:T(128)} %ref_part.5) | copy-start | bytes 28
  23.0 0.9 %copy-start.10 = (s32[2]{0:T(128)S(1)}, s32[2]{0:T(128)}, u32[]{:S(2)}) copy-start(s32[2]{0:T(128)} %ref_line.5) | copy-start | bytes 28
  23.0 9.7 %copy-start.1 = (bf16[8,2,512,512]{3,2,1,0:T(8,128)(2,1)S(1)}, bf16[8,2,512,512]{3,2,1,0:T(8,128)(2,1)}, u32[]{:S(2)}) copy-start(bf16[8,2,512,512]{3,2,1,0:T(8,128)(2,1)} %param.14) | copy-start | bytes 25165828
  24.7 4.8 %collective-permute-start.4 = (f32[8,512]{1,0:T(8,128)S(1)}, f32[8,512]{1,0:T(8,128)S(1)}, u32[]{:S(2)}, u32[]{:S(2)}) collective-permute-start(f32[8,512]{1,0:T(8,128)S(1)} %get-tuple-element.32), channel_id=1, source_target_pairs={{0,1},{2,3},{1,0},{3,2},{4,5},{6,7},{5,4},{7,6},{8,9},{10,11},{9,8... | collective-permute-start | bytes 49160 | tf_op jit(solution)/shard_map/ppermute | solution.py:528
  25.4 8.0 %collective-permute-start.6 = (f32[2,16,512]{2,1,0:T(8,128)S(1)}, f32[2,16,512]{2,1,0:T(8,128)S(1)}, u32[]{:S(2)}, u32[]{:S(2)}) collective-permute-start(f32[2,16,512]{2,1,0:T(8,128)S(1)} %get-tuple-element.34), channel_id=1, source_target_pairs={{0,4},{8,12},{16,20},{24,28},{4,0},{12,8},{20,16},{28,24},{1,5},{9... | collective-permute-start | bytes 196616 | tf_op jit(solution)/shard_map/ppermute | solution.py:528
  27.1 7.0 %collective-permute-start.7 = (f32[2,16,512]{2,1,0:T(8,128)S(1)}, f32[2,16,512]{2,1,0:T(8,128)S(1)}, u32[]{:S(2)}, u32[]{:S(2)}) collective-permute-start(f32[2,16,512]{2,1,0:T(8,128)S(1)} %get-tuple-element.35), channel_id=1, source_target_pairs={{4,8},{12,16},{20,24},{28,0},{8,4},{16,12},{24,20},{0,28},{5,9},{1... | collective-permute-start | bytes 196616 | tf_op jit(solution)/shard_map/ppermute | solution.py:528
  29.6 3.2 %collective-permute-start.5 = (f32[8,512]{1,0:T(8,128)S(1)}, f32[8,512]{1,0:T(8,128)S(1)}, u32[]{:S(2)}, u32[]{:S(2)}) collective-permute-start(f32[8,512]{1,0:T(8,128)S(1)} %add_select_fusion.2), channel_id=1, source_target_pairs={{1,2},{3,0},{2,1},{0,3},{5,6},{7,4},{6,5},{4,7},{9,10},{11,8},{10,... | collective-permute-start | bytes 49160 | tf_op jit(solution)/shard_map/ppermute | solution.py:528
  34.8 4.3 %collective-permute-start.8 = (f32[8,512]{1,0:T(8,128)S(1)}, f32[8,512]{1,0:T(8,128)S(1)}, u32[]{:S(2)}, u32[]{:S(2)}) collective-permute-start(f32[8,512]{1,0:T(8,128)S(1)} %get-tuple-element.37), channel_id=1, source_target_pairs={{0,1},{2,3},{1,0},{3,2},{4,5},{6,7},{5,4},{7,6},{8,9},{10,11},{9,8... | collective-permute-start | bytes 49160 | tf_op jit(solution)/shard_map/ppermute | solution.py:528
  34.9 8.1 %collective-permute-start.10 = (f32[2,16,512]{2,1,0:T(8,128)S(1)}, f32[2,16,512]{2,1,0:T(8,128)S(1)}, u32[]{:S(2)}, u32[]{:S(2)}) collective-permute-start(f32[2,16,512]{2,1,0:T(8,128)S(1)} %get-tuple-element.39), channel_id=1, source_target_pairs={{0,4},{8,12},{16,20},{24,28},{4,0},{12,8},{20,16},{28,24},{1,5},{9... | collective-permute-start | bytes 196616 | tf_op jit(solution)/shard_map/ppermute | solution.py:528
  37.0 7.0 %collective-permute-start.11 = (f32[2,16,512]{2,1,0:T(8,128)S(1)}, f32[2,16,512]{2,1,0:T(8,128)S(1)}, u32[]{:S(2)}, u32[]{:S(2)}) collective-permute-start(f32[2,16,512]{2,1,0:T(8,128)S(1)} %get-tuple-element.40), channel_id=1, source_target_pairs={{4,8},{12,16},{20,24},{28,0},{8,4},{16,12},{24,20},{0,28},{5,9},{1... | collective-permute-start | bytes 196616 | tf_op jit(solution)/shard_map/ppermute | solution.py:528
  39.2 3.2 %collective-permute-start.9 = (f32[8,512]{1,0:T(8,128)S(1)}, f32[8,512]{1,0:T(8,128)S(1)}, u32[]{:S(2)}, u32[]{:S(2)}) collective-permute-start(f32[8,512]{1,0:T(8,128)S(1)} %add_select_fusion.1), channel_id=1, source_target_pairs={{1,2},{3,0},{2,1},{0,3},{5,6},{7,4},{6,5},{4,7},{9,10},{11,8},{10,... | collective-permute-start | bytes 49160 | tf_op jit(solution)/shard_map/ppermute | solution.py:528
  44.7 4.4 %collective-permute-start.12 = (f32[8,512]{1,0:T(8,128)S(1)}, f32[8,512]{1,0:T(8,128)S(1)}, u32[]{:S(2)}, u32[]{:S(2)}) collective-permute-start(f32[8,512]{1,0:T(8,128)S(1)} %get-tuple-element.42), channel_id=1, source_target_pairs={{0,1},{2,3},{1,0},{3,2},{4,5},{6,7},{5,4},{7,6},{8,9},{10,11},{9,8... | collective-permute-start | bytes 49160 | tf_op jit(solution)/shard_map/ppermute | solution.py:528
  44.8 8.2 %collective-permute-start.14 = (f32[2,16,512]{2,1,0:T(8,128)S(1)}, f32[2,16,512]{2,1,0:T(8,128)S(1)}, u32[]{:S(2)}, u32[]{:S(2)}) collective-permute-start(f32[2,16,512]{2,1,0:T(8,128)S(1)} %get-tuple-element.44), channel_id=1, source_target_pairs={{0,4},{8,12},{16,20},{24,28},{4,0},{12,8},{20,16},{28,24},{1,5},{9... | collective-permute-start | bytes 196616 | tf_op jit(solution)/shard_map/ppermute | solution.py:528
  47.3 7.0 %collective-permute-start.15 = (f32[2,16,512]{2,1,0:T(8,128)S(1)}, f32[2,16,512]{2,1,0:T(8,128)S(1)}, u32[]{:S(2)}, u32[]{:S(2)}) collective-permute-start(f32[2,16,512]{2,1,0:T(8,128)S(1)} %get-tuple-element.45), channel_id=1, source_target_pairs={{4,8},{12,16},{20,24},{28,0},{8,4},{16,12},{24,20},{0,28},{5,9},{1... | collective-permute-start | bytes 196616 | tf_op jit(solution)/shard_map/ppermute | solution.py:528
  49.2 3.2 %collective-permute-start.13 = (f32[8,512]{1,0:T(8,128)S(1)}, f32[8,512]{1,0:T(8,128)S(1)}, u32[]{:S(2)}, u32[]{:S(2)}) collective-permute-start(f32[8,512]{1,0:T(8,128)S(1)} %add_select_fusion), channel_id=1, source_target_pairs={{1,2},{3,0},{2,1},{0,3},{5,6},{7,4},{6,5},{4,7},{9,10},{11,8},{10,... | collective-permute-start | bytes 49160 | tf_op jit(solution)/shard_map/ppermute | solution.py:528
  52.4 14.8 %copy-start.11 = (f32[2]{0:T(128)S(1)}, f32[2]{0:T(128)}, u32[]{:S(2)}) copy-start(f32[2]{0:T(128)} %shift.1) | copy-start | bytes 28

commit v3 on v2

--- a/solution.py
+++ b/solution.py
@@ -11,7 +11,6 @@
 EPSILON = 1e-06
 CENTRE = 7.125
 PARTS = 2
-START_LIMIT = 61 << 20
 HIGHEST = lax.Precision.HIGHEST
 VMEM = pltpu.VMEM
 SMEM = pltpu.SMEM
@@ -27,6 +26,10 @@
 
 def in_hbm(count):
     return [pl.BlockSpec(memory_space=pltpu.HBM) for _ in range(count)]
+
+
+def held_in_hbm(*arrays):
+    return [pltpu.with_memory_space_constraint(a, pltpu.HBM) for a in arrays]
 
 
 def call(kernel, outs, specs, args, scratch=(), cost=1, out_specs=None, limit=8 << 20):
@@ -61,7 +64,7 @@
             dom_x[at : at + 1, :] = field[c, pl.ds(x_row, 1), :]
             dom_y[at : at + 1, :] = field[c, pl.ds(y_row, 1), :]
     base = 2 * rows
-    for b in range((dom_x.shape[0] - base) // 2):
+    for b in range(ref_part.shape[0]):
         mine = ref_part[b] == part
         for c in range(2):
             at = base + 2 * b + c
@@ -71,27 +74,37 @@
 
 
 def start_kernel(
-    rows, depth, small, basis_in, field, azim_x, azim_y, dom_x, dom_y, basis, sems
+    rows, depth, coef_in, part_in, line_in, basis_in,
+    field, azim_x, azim_y, dom_x, dom_y, basis, coef, ref_part, ref_line, small_sems, sems,
 ):
     count = basis.shape[0]
-    copies = [pltpu.make_async_copy(basis_in.at[i], basis.at[i], sems.at[i]) for i in range(count)]
-    for copy in copies:
+    pairs = ((coef_in, coef), (part_in, ref_part), (line_in, ref_line))
+    small = [pltpu.make_async_copy(a, b, small_sems.at[i]) for i, (a, b) in enumerate(pairs)]
+    group = count // sems.shape[0]
+    large = [
+        pltpu.make_async_copy(
+            basis_in.at[pl.ds(i * group, group)], basis.at[pl.ds(i * group, group)], sems.at[i]
+        )
+        for i in range(sems.shape[0])
+    ]
+    for copy in small + large:
         copy.start()
-    for i in range(count):
-        copies[i].wait()
-        one, two = small[i], small[count + i]
+    for copy in small:
+        copy.wait()
+    for at, copy in enumerate(large):
+        copy.wait()
         for a in range(rows):
             span = slice(a * depth, (a + 1) * depth)
-            re, im = basis[i, 0, span, :], basis[i, 1, span, :]
-            real = one * re - two * im
-            imag = one * im + two * re
-            field[0, span, :] = real if i == 0 else field[0, span, :] + real
-            field[1, span, :] = imag if i == 0 else field[1, span, :] + imag
-    burners = (small.shape[0] - 2 * count) // 2
-    numbers = [small[2 * count + i].astype(jnp.int32) for i in range(2 * burners)]
-    write_edges(
-        rows, depth, field, numbers[:burners], numbers[burners:], azim_x, azim_y, dom_x, dom_y
-    )
+            real = imag = None
+            for i in range(at * group, (at + 1) * group):
+                re, im = basis[i, 0, span, :], basis[i, 1, span, :]
+                one = coef[0, i] * re - coef[1, i] * im
+                two = coef[0, i] * im + coef[1, i] * re
+                real = one if real is None else real + one
+                imag = two if imag is None else imag + two
+            field[0, span, :] = real if at == 0 else field[0, span, :] + real
+            field[1, span, :] = imag if at == 0 else field[1, span, :] + imag
+    write_edges(rows, depth, field, ref_part, ref_line, azim_x, azim_y, dom_x, dom_y)
 
 
 def basis_kernel(part, parts, basis, out, tiles):
@@ -151,10 +164,20 @@
     add_dots(k, basis, powers[:-1], powers[-1], dots_in, dots_out, held)
 
 
-def flame_kernel(base, live, lines, burners, mats, sums, *refs):
+def first_dots_kernel(basis, power, mats_in, dots_out, mats, held, sems):
+    half = mats.shape[0]
+    copies = [pltpu.make_async_copy(mats_in.at[s], mats.at[s], sems.at[s]) for s in range(half)]
+    for copy in copies:
+        copy.start()
+    add_dots(0, basis, [], power, None, dots_out, held)
+    for copy in copies:
+        copy.wait()
+
+
+def flame_kernel(base, live, lines, burners, sums, lower, upper, *refs, ready=None):
     out, source = refs[-2:]
     width = sums.shape[1]
-    slots = mats.shape[0]
+    half = lower.shape[0]
     rows = sums.shape[0] - base
     source[...] = jnp.zeros_like(source)
     for i in range(rows):
@@ -180,24 +203,50 @@
         out[0, at, :] += by_re[:, :width] - by_im[:, width:]
         out[1, at, :] += by_im[:, :width] + by_re[:, width:]
 
-    few = 2
+    def put_all(first, blocks):
+        every = products(blocks[...].reshape(half * 2 * width, width))
+        for s in range(half):
+
+            @pl.when(first + s < live[0])
+            def _():
+                put(first + s, every[:, 2 * width * s : 2 * width * (s + 1)])
+
+    few = half // 2
 
     @pl.when(live[0] <= few)
     def _():
         def slot(s, carry):
-            put(s, products(mats[s]))
+            put(s, products(lower[s]))
             return carry
 
         lax.fori_loop(0, live[0], slot, 0)
 
     @pl.when(live[0] > few)
     def _():
-        every = products(mats[...].reshape(slots * 2 * width, width))
-        for s in range(slots):
-
-            @pl.when(s < live[0])
-            def _():
-                put(s, every[:, 2 * width * s : 2 * width * (s + 1)])
+        put_all(0, lower)
+
+    if ready is not None:
+        ready()
+
+    @pl.when(live[0] > half)
+    def _():
+        put_all(half, upper)
+
+
+def first_flame_kernel(base, live, lines, burners, sums, lower, mats_in, order, out, upper, *refs):
+    source, sems = refs
+    half = lower.shape[0]
+    copies = [
+        pltpu.make_async_copy(mats_in.at[half + s], upper.at[s], sems.at[s]) for s in range(half)
+    ]
+    for copy in copies:
+        copy.start()
+
+    def ready():
+        for copy in copies:
+            copy.wait()
+
+    flame_kernel(base, live, lines, burners, sums, lower, upper, order, out, source, ready=ready)
 
 
 def step_kernel(
@@ -542,21 +591,19 @@
         shape(tall, width),
         shape(tall, width),
     ]
-    small = jnp.concatenate(
-        [
-            coefficients.reshape(-1),
-            reference_part.astype(jnp.float32),
-            reference_line.astype(jnp.float32),
-        ]
-    )
     power, azim_x, azim_y, dom_x, dom_y, basis = call(
         functools.partial(start_kernel, rows, depth),
         [*fields, shape(count, 2, lines, width)],
-        smem(1) + in_hbm(1),
-        (small, basis),
-        [pltpu.SemaphoreType.DMA((count,))],
+        in_hbm(4),
+        held_in_hbm(coefficients, reference_part, reference_line, basis),
+        [
+            SMEM(coefficients.shape, jnp.float32),
+            SMEM(reference_part.shape, jnp.int32),
+            SMEM(reference_line.shape, jnp.int32),
+            pltpu.SemaphoreType.DMA((3,)),
+            pltpu.SemaphoreType.DMA((4,)),
+        ],
         cost=4,
-        limit=START_LIMIT,
     )
     powers = [power]
     held = VMEM((2 * count + 16, 128), jnp.float32)
@@ -583,19 +630,42 @@
             pairs = [(i, i ^ reach) for i in range(n_dom) if i < i ^ reach]
             sums = sums + exchange(sums, "dom", pairs)
             reach *= 2
-        given = (basis, *powers, *([dots] if step else []))
-        dots = call(
-            functools.partial(dots_kernel, step), shape(8, 128), vmem(len(given)), given, [held]
-        )
-        order = (dots, *tables[step - 1 : step]) if step else (dots,)
-        flame = call(
-            functools.partial(flame_kernel, base),
-            shape(2, lines, width),
-            smem(3) + vmem(2 + len(order)),
-            (flame_count, flame_line, flame_burner, mats, sums, *order),
-            [VMEM((16, width), jnp.bfloat16)],
-            cost=3,
-        )
+        numbers = (flame_count, flame_line, flame_burner)
+        source = VMEM((16, width), jnp.bfloat16)
+        half = slots // 2
+        blocks = jax.ShapeDtypeStruct((half, 2 * width, width), mats.dtype)
+        if step == 0:
+            (mats,) = held_in_hbm(mats)
+            dots, lower = call(
+                first_dots_kernel,
+                [shape(8, 128), blocks],
+                vmem(2) + in_hbm(1),
+                (basis, power, mats),
+                [held, pltpu.SemaphoreType.DMA((half,))],
+                cost=2,
+            )
+            flame, upper = call(
+                functools.partial(first_flame_kernel, base),
+                [shape(2, lines, width), blocks],
+                smem(3) + vmem(2) + in_hbm(1) + vmem(1),
+                (*numbers, sums, lower, mats, dots),
+                [source, pltpu.SemaphoreType.DMA((half,))],
+                cost=3,
+            )
+        else:
+            given = (basis, *powers, dots)
+            dots = call(
+                functools.partial(dots_kernel, step), shape(8, 128), vmem(len(given)), given, [held]
+            )
+            order = (dots, *tables[step - 1 : step])
+            flame = call(
+                functools.partial(flame_kernel, base),
+                shape(2, lines, width),
+                smem(3) + vmem(3 + len(order)),
+                (*numbers, sums, lower, upper, *order),
+                [source],
+                cost=3,
+            )
         received = (power, flame, diag, from_ax, from_ay, from_dx, from_dy)
         if step < INNER_STEPS:
             power, azim_x, azim_y, dom_x, dom_y = call(

time: 70.2 us -> 61.3 us (0.87)
  Pallas kernels: 17.1 us -> 27.5 us
  local copies, waits for them, and re-layouts: 6.94 us -> 0.06 us
  starting transfers between devices: 22.4 us -> 15.7 us
  other arithmetic: 3 us -> 0.35 us
  waiting for transfers between devices: 6.07 us -> 4.32 us
  blocking collectives: 12.5 us -> 11.4 us
    pallas_call x16, Pallas kernels: 17.1 us -> 27.5 us  [call(): pl.pallas_call(kernel, out_shape=outs, in_specs=specs, out_specs=out_spec...]
    ppermute x16, starting transfers between devices: 22.4 us -> 15.7 us  [exchange(): return lax.ppermute(values, axis, both)]
    unnamed x24 -> x12, local copies, waits for them, and re-layouts: 6.16 us -> 0.04 us
    ppermute x16, waiting for transfers between devices: 6.07 us -> 4.32 us  [exchange(): return lax.ppermute(values, axis, both)]
    convert_element_type x2 -> x0, other arithmetic: 1.31 us -> none  [the longest x1 0.66 us: on_device(): reference_part.astype(jnp.float32)]
    all_to_all x1, blocking collectives: 12.5 us -> 11.4 us  [on_device(): gram = jnp.sum(lax.all_to_all(spread, ('azim', 'dom'), 0, 0), axis=0)]
    reshape x1 -> x0, local copies, waits for them, and re-layouts: 0.76 us -> none  [on_device(): coefficients.reshape(-1)]
    select_n x4, other arithmetic: 1.02 us -> 0.29 us  [on_device(): dom_y = jnp.where(is_sum, dom_x + from_dx, dom_y)]
  transfers between devices with their start and end apart: 16 -> 16, of which waited for: 6 -> 3; matrix products, arithmetic and copies ran while one was open for 2% -> 1% of each run, Pallas kernels for 12% -> 34%
where the time goes in v3:
time: 61.3 us; the launch traced here: 61 us
  Pallas kernels  27.5 us (45%)
  starting transfers between devices  15.7 us (26%)
  blocking collectives  11.4 us (19%)
  waiting for transfers between devices  4.32 us (7%)
  between operations  1.59 us (3%)
    pallas_call x16, Pallas kernels, call(): pl.pallas_call(kernel, out_shape=outs, in_specs=specs, out_specs=out_spec...  27.5 us
    ppermute x16, starting transfers between devices, exchange(): return lax.ppermute(values, axis, both)  15.7 us
    all_to_all x1, blocking collectives, on_device(): gram = jnp.sum(lax.all_to_all(spread, ('azim', 'dom'), 0, 0), axis=0)  11.4 us
    ppermute x16, waiting for transfers between devices, exchange(): return lax.ppermute(values, axis, both)  4.32 us
  transfers between devices with their start and end apart: 16, of which 3 were waited for; matrix products, arithmetic and copies ran while one was open for 1% of the time, Pallas kernels for 34%

profile of v3, /device:TPU:0, one launch (start us, length us, event | category | flops | bytes accessed | tf_op | source)
XLA Modules:
  0.0 61.0 jit_solution(4009018344203181450)
XLA Ops:
  0.6 1.7 %shard_map.113 = (f32[2,32,512]{2,1,0:T(8,128)S(1)}, f32[2,16,512]{2,1,0:T(8,128)S(1)}, f32[2,16,512]{2,1,0:T(8,128)S(1)}, f32[8,512]{1,0:T(8,128)S(1)}, f32[8,5...) custom-call(f32[2,16]{1,0:T(2,128)} %coef_in.1, s32[2]{0:T(128)} %ref_part.5, s32[2]{0:T(128)} %ref_line.5, ...), custom_call_target="tpu_custom_call" | custom-call | bytes 8000000 | tf_op jit(solution)/shard_map/pallas_call | solution.py:39
  2.3 0.6 collective-permute-start
  2.9 2.6 %collective-permute-start.2 = (f32[2,16,512]{2,1,0:T(8,128)S(1)}, f32[2,16,512]{2,1,0:T(8,128)S(1)}, u32[]{:S(2)}, u32[]{:S(2)}) collective-permute-start(f32[2,16,512]{2,1,0:T(8,128)S(1)} %get-tuple-element.36), channel_id=1, source_target_pairs={{0,4},{8,12},{16,20},{24,28},{4,0},{12,8},{20,16},{28,24},{1,5},{9... | collective-permute-start | bytes 196616 | tf_op jit(solution)/shard_map/ppermute | solution.py:577
  5.5 3.5 %collective-permute-start.3 = (f32[2,16,512]{2,1,0:T(8,128)S(1)}, f32[2,16,512]{2,1,0:T(8,128)S(1)}, u32[]{:S(2)}, u32[]{:S(2)}) collective-permute-start(f32[2,16,512]{2,1,0:T(8,128)S(1)} %get-tuple-element.37), channel_id=1, source_target_pairs={{4,8},{12,16},{20,24},{28,0},{8,4},{16,12},{24,20},{0,28},{5,9},{1... | collective-permute-start | bytes 196616 | tf_op jit(solution)/shard_map/ppermute | solution.py:577
  9.0 0.0 collective-permute-done.from_dx
  9.0 0.1 add_select_fusion.3
  9.1 1.0 %collective-permute-start.1 = (f32[8,512]{1,0:T(8,128)S(1)}, f32[8,512]{1,0:T(8,128)S(1)}, u32[]{:S(2)}, u32[]{:S(2)}) collective-permute-start(f32[8,512]{1,0:T(8,128)S(1)} %add_select_fusion.3), channel_id=1, source_target_pairs={{1,2},{3,0},{2,1},{0,3},{5,6},{7,4},{6,5},{4,7},{9,10},{11,8},{10,... | collective-permute-start | bytes 49160 | tf_op jit(solution)/shard_map/ppermute | solution.py:577
  10.7 0.0 copy-start.1
  10.7 0.0 copy-start.2
  10.7 2.2 %shard_map.114 = (f32[8,128]{1,0:T(8,128)S(1)}, bf16[4,1024,512]{2,1,0:T(8,128)(2,1)S(1)}) custom-call(f32[16,2,32,512]{3,2,1,0:T(8,128)S(1)} %get-tuple-element.32.basis, f32[2,32,512]{2,1,0:T(8,128)S(1)} %get-tuple-element.29.power.old.refs_0_.refs_9_, bf16[8,1024,512]{2,1,0:T(8,128)(2,1)} %bitcast.8), custom_call_target="tpu_custom_call" | custom-call | bytes 4000000 | tf_op jit(solution)/shard_map/pallas_call | solution.py:39
  13.0 0.0 collective-permute-done.1.from_dy
  13.0 0.0 copy-start
  13.0 0.0 copy-start.3
  13.0 0.0 copy-start.4
  13.0 4.0 %shard_map.115 = (f32[2,32,512]{2,1,0:T(8,128)S(1)}, bf16[4,1024,512]{2,1,0:T(8,128)(2,1)S(1)}) custom-call(s32[1]{0:T(128)S(6)} %copy.12.live, s32[8]{0:T(128)S(1)} %copy-done.1, s32[8]{0:T(128)S(1)} %copy-done.2, f32[8,512]{1,0:T(8,128)S(1)} %add.25.sums, bf16[4,1024,512]{2,1,0:T(8,128)(2,1)S(1)} %get-tuple-element.33.lower, ...), custom_call_target="tpu_custom_call" | custom-call | bytes 6000000 | tf_op jit(solution)/shard_map/pallas_call | solution.py:39
  17.1 0.0 collective-permute-done.2.from_ax
  17.1 0.7 %shard_map.116 = (f32[2,32,512]{2,1,0:T(8,128)S(1)}, f32[2,16,512]{2,1,0:T(8,128)S(1)}, f32[2,16,512]{2,1,0:T(8,128)S(1)}, f32[8,512]{1,0:T(8,128)S(1)}, f32[8,512]{1,0:T(8,128)S(1)}) custom-call(s32[2]{0:T(128)S(1)} %copy-done.3, s32[2]{0:T(128)S(1)} %copy-done.4, f32[2,32,512]{2,1,0:T(8,128)S(1)} %get-tuple-element.29.power.old.refs_0_.refs_9_, ...), custom_call_target="tpu_custom_call" | custom-call | bytes 2000000 | tf_op jit(solution)/shard_map/pallas_call | solution.py:39
  17.9 0.1 collective-permute-start.4
  17.9 0.1 collective-permute-start.6
  18.1 2.4 %collective-permute-start.7 = (f32[2,16,512]{2,1,0:T(8,128)S(1)}, f32[2,16,512]{2,1,0:T(8,128)S(1)}, u32[]{:S(2)}, u32[]{:S(2)}) collective-permute-start(f32[2,16,512]{2,1,0:T(8,128)S(1)} %get-tuple-element.43), channel_id=1, source_target_pairs={{4,8},{12,16},{20,24},{28,0},{8,4},{16,12},{24,20},{0,28},{5,9},{1... | collective-permute-start | bytes 196616 | tf_op jit(solution)/shard_map/ppermute | solution.py:577
  20.5 0.1 add_select_fusion.2
  20.5 0.0 collective-permute-start.5
  20.6 1.5 %shard_map.118.refs_1_.refs_7_ = f32[8,128]{1,0:T(8,128)S(1)} custom-call(f32[16,2,32,512]{3,2,1,0:T(8,128)S(1)} %get-tuple-element.32.basis), custom_call_target="tpu_custom_call" | custom-call | bytes 2000000 | tf_op jit(solution)/shard_map/pallas_call | solution.py:39
  22.0 0.8 %shard_map.117.refs_0_.refs_3_ = f32[8,128]{1,0:T(8,128)S(1)} custom-call(f32[16,2,32,512]{3,2,1,0:T(8,128)S(1)} %get-tuple-element.32.basis, f32[2,32,512]{2,1,0:T(8,128)S(1)} %get-tuple-element.29.power.old.refs_0_.refs_9_, f32[2,32,512]{2,1,0:T(8,128)S(1)} %get-tuple-element.38.refs_1_.old.refs_10_, f32[8,128]{1,0:T(8,128)S(1)} %get-tuple-element.34.order.refs_2_), custom_call_target="tpu_custom_call" | custom-call | bytes 2000000 | tf_op jit(solution)/shard_map/pallas_call | solution.py:39
  22.8 0.9 %collective-permute-done.5.from_dy = f32[8,512]{1,0:T(8,128)S(1)} collective-permute-done((f32[8,512]{1,0:T(8,128)S(1)}, f32[8,512]{1,0:T(8,128)S(1)}, u32[]{:S(2)}, u32[]{:S(2)}) %collective-permute-start.5) | collective-permute-done | bytes 16416 | tf_op jit(solution)/shard_map/ppermute | solution.py:577
  23.7 3.2 %shard_map.119.flame = f32[2,32,512]{2,1,0:T(8,128)S(1)} custom-call(s32[1]{0:T(128)S(6)} %copy.12.live, s32[8]{0:T(128)S(1)} %copy-done.1, s32[8]{0:T(128)S(1)} %copy-done.2, f32[8,512]{1,0:T(8,128)S(1)} %add.27.sums, bf16[4,1024,512]{2,1,0:T(8,128)(2,1)S(1)} %get-tuple-element.33.lower, bf16[4,1024,512]{2,1,0:T(8,128)(2,1)S(1)} %get-tuple-element.41.upper, ...), custom_call_target="tpu_custom_call" | custom-call | bytes 6000000 | tf_op jit(solution)/shard_map/pallas_call | solution.py:39
  26.9 0.7 %shard_map.120 = (f32[2,32,512]{2,1,0:T(8,128)S(1)}, f32[2,16,512]{2,1,0:T(8,128)S(1)}, f32[2,16,512]{2,1,0:T(8,128)S(1)}, f32[8,512]{1,0:T(8,128)S(1)}, f32[8,512]{1,0:T(8,128)S(1)}) custom-call(s32[2]{0:T(128)S(1)} %copy-done.3, s32[2]{0:T(128)S(1)} %copy-done.4, f32[2,32,512]{2,1,0:T(8,128)S(1)} %get-tuple-element.38.refs_1_.old.refs_10_, ...), custom_call_target="tpu_custom_call" | custom-call | bytes 2000000 | tf_op jit(solution)/shard_map/pallas_call | solution.py:39
  27.6 0.1 collective-permute-start.8
  27.7 0.3 collective-permute-start.10
  28.0 2.3 %collective-permute-start.11 = (f32[2,16,512]{2,1,0:T(8,128)S(1)}, f32[2,16,512]{2,1,0:T(8,128)S(1)}, u32[]{:S(2)}, u32[]{:S(2)}) collective-permute-start(f32[2,16,512]{2,1,0:T(8,128)S(1)} %get-tuple-element.48), channel_id=1, source_target_pairs={{4,8},{12,16},{20,24},{28,0},{8,4},{16,12},{24,20},{0,28},{5,9},{1... | collective-permute-start | bytes 196616 | tf_op jit(solution)/shard_map/ppermute | solution.py:577
  30.4 0.1 add_select_fusion.1
  30.5 0.0 collective-permute-start.9
  30.5 1.5 %shard_map.122.refs_1_.refs_8_ = f32[8,128]{1,0:T(8,128)S(1)} custom-call(f32[16,2,32,512]{3,2,1,0:T(8,128)S(1)} %get-tuple-element.32.basis), custom_call_target="tpu_custom_call" | custom-call | bytes 2000000 | tf_op jit(solution)/shard_map/pallas_call | solution.py:39
  32.0 0.8 %shard_map.121.refs_0_.refs_4_ = f32[8,128]{1,0:T(8,128)S(1)} custom-call(f32[16,2,32,512]{3,2,1,0:T(8,128)S(1)} %get-tuple-element.32.basis, f32[2,32,512]{2,1,0:T(8,128)S(1)} %get-tuple-element.29.power.old.refs_0_.refs_9_, f32[2,32,512]{2,1,0:T(8,128)S(1)} %get-tuple-element.38.refs_1_.old.refs_10_, ...), custom_call_target="tpu_custom_call" | custom-call | bytes 2000000 | tf_op jit(solution)/shard_map/pallas_call | solution.py:39
  32.7 1.0 %collective-permute-done.9.from_dy = f32[8,512]{1,0:T(8,128)S(1)} collective-permute-done((f32[8,512]{1,0:T(8,128)S(1)}, f32[8,512]{1,0:T(8,128)S(1)}, u32[]{:S(2)}, u32[]{:S(2)}) %collective-permute-start.9) | collective-permute-done | bytes 16416 | tf_op jit(solution)/shard_map/ppermute | solution.py:577
  33.8 3.2 %shard_map.123.flame = f32[2,32,512]{2,1,0:T(8,128)S(1)} custom-call(s32[1]{0:T(128)S(6)} %copy.12.live, s32[8]{0:T(128)S(1)} %copy-done.1, s32[8]{0:T(128)S(1)} %copy-done.2, f32[8,512]{1,0:T(8,128)S(1)} %add.29.sums, bf16[4,1024,512]{2,1,0:T(8,128)(2,1)S(1)} %get-tuple-element.33.lower, bf16[4,1024,512]{2,1,0:T(8,128)(2,1)S(1)} %get-tuple-element.41.upper, ...), custom_call_target="tpu_custom_call" | custom-call | bytes 6000000 | tf_op jit(solution)/shard_map/pallas_call | solution.py:39
  36.9 0.7 %shard_map.124 = (f32[2,32,512]{2,1,0:T(8,128)S(1)}, f32[2,16,512]{2,1,0:T(8,128)S(1)}, f32[2,16,512]{2,1,0:T(8,128)S(1)}, f32[8,512]{1,0:T(8,128)S(1)}, f32[8,512]{1,0:T(8,128)S(1)}) custom-call(s32[2]{0:T(128)S(1)} %copy-done.3, s32[2]{0:T(128)S(1)} %copy-done.4, f32[2,32,512]{2,1,0:T(8,128)S(1)} %get-tuple-element.44.refs_2_.old.refs_11_, ...), custom_call_target="tpu_custom_call" | custom-call | bytes 2000000 | tf_op jit(solution)/shard_map/pallas_call | solution.py:39
  37.7 0.1 collective-permute-start.12
  37.7 0.8 %collective-permute-start.14 = (f32[2,16,512]{2,1,0:T(8,128)S(1)}, f32[2,16,512]{2,1,0:T(8,128)S(1)}, u32[]{:S(2)}, u32[]{:S(2)}) collective-permute-start(f32[2,16,512]{2,1,0:T(8,128)S(1)} %get-tuple-element.52), channel_id=1, source_target_pairs={{0,4},{8,12},{16,20},{24,28},{4,0},{12,8},{20,16},{28,24},{1,5},{9... | collective-permute-start | bytes 196616 | tf_op jit(solution)/shard_map/ppermute | solution.py:577
  38.5 1.8 %collective-permute-start.15 = (f32[2,16,512]{2,1,0:T(8,128)S(1)}, f32[2,16,512]{2,1,0:T(8,128)S(1)}, u32[]{:S(2)}, u32[]{:S(2)}) collective-permute-start(f32[2,16,512]{2,1,0:T(8,128)S(1)} %get-tuple-element.53), channel_id=1, source_target_pairs={{4,8},{12,16},{20,24},{28,0},{8,4},{16,12},{24,20},{0,28},{5,9},{1... | collective-permute-start | bytes 196616 | tf_op jit(solution)/shard_map/ppermute | solution.py:577
  40.3 0.1 add_select_fusion
  40.4 0.0 collective-permute-start.13
  40.4 0.8 %shard_map.125.refs_0_.refs_13_ = f32[8,128]{1,0:T(8,128)S(1)} custom-call(f32[16,2,32,512]{3,2,1,0:T(8,128)S(1)} %get-tuple-element.32.basis, f32[2,32,512]{2,1,0:T(8,128)S(1)} %get-tuple-element.29.power.old.refs_0_.refs_9_, f32[2,32,512]{2,1,0:T(8,128)S(1)} %get-tuple-element.38.refs_1_.old.refs_10_, ...), custom_call_target="tpu_custom_call" | custom-call | bytes 2000000 | tf_op jit(solution)/shard_map/pallas_call | solution.py:39
  41.2 2.4 %collective-permute-done.13.refs_6_ = f32[8,512]{1,0:T(8,128)S(1)} collective-permute-done((f32[8,512]{1,0:T(8,128)S(1)}, f32[8,512]{1,0:T(8,128)S(1)}, u32[]{:S(2)}, u32[]{:S(2)}) %collective-permute-start.13) | collective-permute-done | bytes 16416 | tf_op jit(solution)/shard_map/ppermute | solution.py:577
  43.5 3.2 %shard_map.126.refs_1_ = f32[2,32,512]{2,1,0:T(8,128)S(1)} custom-call(s32[1]{0:T(128)S(6)} %copy.12.live, s32[8]{0:T(128)S(1)} %copy-done.1, s32[8]{0:T(128)S(1)} %copy-done.2, f32[8,512]{1,0:T(8,128)S(1)} %add.31.sums, bf16[4,1024,512]{2,1,0:T(8,128)(2,1)S(1)} %get-tuple-element.33.lower, bf16[4,1024,512]{2,1,0:T(8,128)(2,1)S(1)} %get-tuple-element.41.upper, ...), custom_call_target="tpu_custom_call" | custom-call | bytes 6000000 | tf_op jit(solution)/shard_map/pallas_call | solution.py:39
  46.7 0.4 shard_map.127
  47.1 11.4 %all_to_all.5 = f32[32,8,128]{2,1,0:T(8,128)S(1)} all-to-all(f32[32,8,128]{2,1,0:T(8,128)S(1)} %broadcast_in_dim.2), channel_id=1, replica_groups=mesh['azim'=8,'dom'=4] {'azim','dom'}, dimensions={0} | all-to-all | bytes 262144 | tf_op jit(solution)/shard_map/all_to_all | solution.py:688
  58.6 2.3 %shard_map.128 = (f32[2,32,512]{2,1,0:T(8,128)}, f32[2]{0:T(128)}) custom-call(f32[2]{0:T(128)S(1)} %copy-done.5, f32[8,128]{1,0:T(8,128)S(1)} %reduce_sum.9.gram_s.gram, f32[8,128]{1,0:T(8,128)S(1)} %reduce_sum.9.gram_s.gram, f32[16,2,32,512]{3,2,1,0:T(8,128)S(1)} %get-tuple-element.32.basis, f32[2,32,512]{2,1,0:T(8,128)S(1)} %get-tuple-element.29.power.old.refs_0_.refs_9_, ...), custom_call_target="tpu_custom_call" | custom-call | bytes 2000000 | tf_op jit(solution)/shard_map/pallas_call | solution.py:39
  (24 shorter events, 0.1 us)
Async XLA Ops:
  2.3 6.7 %collective-permute-start = (f32[8,512]{1,0:T(8,128)S(1)}, f32[8,512]{1,0:T(8,128)S(1)}, u32[]{:S(2)}, u32[]{:S(2)}) collective-permute-start(f32[8,512]{1,0:T(8,128)S(1)} %get-tuple-element.30), channel_id=1, source_target_pairs={{0,1},{2,3},{1,0},{3,2},{4,5},{6,7},{5,4},{7,6},{8,9},{10,11},{9,8... | collective-permute-start | bytes 49160 | tf_op jit(solution)/shard_map/ppermute | solution.py:577
  2.9 14.2 %collective-permute-start.2 = (f32[2,16,512]{2,1,0:T(8,128)S(1)}, f32[2,16,512]{2,1,0:T(8,128)S(1)}, u32[]{:S(2)}, u32[]{:S(2)}) collective-permute-start(f32[2,16,512]{2,1,0:T(8,128)S(1)} %get-tuple-element.36), channel_id=1, source_target_pairs={{0,4},{8,12},{16,20},{24,28},{4,0},{12,8},{20,16},{28,24},{1,5},{9... | collective-permute-start | bytes 196616 | tf_op jit(solution)/shard_map/ppermute | solution.py:577
  5.5 11.6 %collective-permute-start.3 = (f32[2,16,512]{2,1,0:T(8,128)S(1)}, f32[2,16,512]{2,1,0:T(8,128)S(1)}, u32[]{:S(2)}, u32[]{:S(2)}) collective-permute-start(f32[2,16,512]{2,1,0:T(8,128)S(1)} %get-tuple-element.37), channel_id=1, source_target_pairs={{4,8},{12,16},{20,24},{28,0},{8,4},{16,12},{24,20},{0,28},{5,9},{1... | collective-permute-start | bytes 196616 | tf_op jit(solution)/shard_map/ppermute | solution.py:577
  9.1 3.9 %collective-permute-start.1 = (f32[8,512]{1,0:T(8,128)S(1)}, f32[8,512]{1,0:T(8,128)S(1)}, u32[]{:S(2)}, u32[]{:S(2)}) collective-permute-start(f32[8,512]{1,0:T(8,128)S(1)} %add_select_fusion.3), channel_id=1, source_target_pairs={{1,2},{3,0},{2,1},{0,3},{5,6},{7,4},{6,5},{4,7},{9,10},{11,8},{10,... | collective-permute-start | bytes 49160 | tf_op jit(solution)/shard_map/ppermute | solution.py:577
  10.7 2.3 %copy-start.1 = (s32[8]{0:T(128)S(1)}, s32[8]{0:T(128)}, u32[]{:S(2)}) copy-start(s32[8]{0:T(128)} %lines.7) | copy-start | bytes 100
  10.7 2.3 %copy-start.2 = (s32[8]{0:T(128)S(1)}, s32[8]{0:T(128)}, u32[]{:S(2)}) copy-start(s32[8]{0:T(128)} %burners.7) | copy-start | bytes 100
  13.0 4.1 %copy-start = (f32[2,16,512]{2,1,0:T(8,128)S(1)}, f32[2,16,512]{2,1,0:T(8,128)}, u32[]{:S(2)}) copy-start(f32[2,16,512]{2,1,0:T(8,128)} %param.13) | copy-start | bytes 196612
  13.0 4.1 %copy-start.3 = (s32[2]{0:T(128)S(1)}, s32[2]{0:T(128)}, u32[]{:S(2)}) copy-start(s32[2]{0:T(128)} %ref_part.5) | copy-start | bytes 28
  13.0 4.1 %copy-start.4 = (s32[2]{0:T(128)S(1)}, s32[2]{0:T(128)}, u32[]{:S(2)}) copy-start(s32[2]{0:T(128)} %ref_line.5) | copy-start | bytes 28
  17.9 2.6 %collective-permute-start.4 = (f32[8,512]{1,0:T(8,128)S(1)}, f32[8,512]{1,0:T(8,128)S(1)}, u32[]{:S(2)}, u32[]{:S(2)}) collective-permute-start(f32[8,512]{1,0:T(8,128)S(1)} %get-tuple-element.39), channel_id=1, source_target_pairs={{0,1},{2,3},{1,0},{3,2},{4,5},{6,7},{5,4},{7,6},{8,9},{10,11},{9,8... | collective-permute-start | bytes 49160 | tf_op jit(solution)/shard_map/ppermute | solution.py:577
  17.9 8.9 %collective-permute-start.6 = (f32[2,16,512]{2,1,0:T(8,128)S(1)}, f32[2,16,512]{2,1,0:T(8,128)S(1)}, u32[]{:S(2)}, u32[]{:S(2)}) collective-permute-start(f32[2,16,512]{2,1,0:T(8,128)S(1)} %get-tuple-element.42), channel_id=1, source_target_pairs={{0,4},{8,12},{16,20},{24,28},{4,0},{12,8},{20,16},{28,24},{1,5},{9... | collective-permute-start | bytes 196616 | tf_op jit(solution)/shard_map/ppermute | solution.py:577
  18.1 8.8 %collective-permute-start.7 = (f32[2,16,512]{2,1,0:T(8,128)S(1)}, f32[2,16,512]{2,1,0:T(8,128)S(1)}, u32[]{:S(2)}, u32[]{:S(2)}) collective-permute-start(f32[2,16,512]{2,1,0:T(8,128)S(1)} %get-tuple-element.43), channel_id=1, source_target_pairs={{4,8},{12,16},{20,24},{28,0},{8,4},{16,12},{24,20},{0,28},{5,9},{1... | collective-permute-start | bytes 196616 | tf_op jit(solution)/shard_map/ppermute | solution.py:577
  20.5 3.2 %collective-permute-start.5 = (f32[8,512]{1,0:T(8,128)S(1)}, f32[8,512]{1,0:T(8,128)S(1)}, u32[]{:S(2)}, u32[]{:S(2)}) collective-permute-start(f32[8,512]{1,0:T(8,128)S(1)} %add_select_fusion.2), channel_id=1, source_target_pairs={{1,2},{3,0},{2,1},{0,3},{5,6},{7,4},{6,5},{4,7},{9,10},{11,8},{10,... | collective-permute-start | bytes 49160 | tf_op jit(solution)/shard_map/ppermute | solution.py:577
  27.6 2.8 %collective-permute-start.8 = (f32[8,512]{1,0:T(8,128)S(1)}, f32[8,512]{1,0:T(8,128)S(1)}, u32[]{:S(2)}, u32[]{:S(2)}) collective-permute-start(f32[8,512]{1,0:T(8,128)S(1)} %get-tuple-element.45), channel_id=1, source_target_pairs={{0,1},{2,3},{1,0},{3,2},{4,5},{6,7},{5,4},{7,6},{8,9},{10,11},{9,8... | collective-permute-start | bytes 49160 | tf_op jit(solution)/shard_map/ppermute | solution.py:577
  27.7 9.2 %collective-permute-start.10 = (f32[2,16,512]{2,1,0:T(8,128)S(1)}, f32[2,16,512]{2,1,0:T(8,128)S(1)}, u32[]{:S(2)}, u32[]{:S(2)}) collective-permute-start(f32[2,16,512]{2,1,0:T(8,128)S(1)} %get-tuple-element.47), channel_id=1, source_target_pairs={{0,4},{8,12},{16,20},{24,28},{4,0},{12,8},{20,16},{28,24},{1,5},{9... | collective-permute-start | bytes 196616 | tf_op jit(solution)/shard_map/ppermute | solution.py:577
  28.0 8.9 %collective-permute-start.11 = (f32[2,16,512]{2,1,0:T(8,128)S(1)}, f32[2,16,512]{2,1,0:T(8,128)S(1)}, u32[]{:S(2)}, u32[]{:S(2)}) collective-permute-start(f32[2,16,512]{2,1,0:T(8,128)S(1)} %get-tuple-element.48), channel_id=1, source_target_pairs={{4,8},{12,16},{20,24},{28,0},{8,4},{16,12},{24,20},{0,28},{5,9},{1... | collective-permute-start | bytes 196616 | tf_op jit(solution)/shard_map/ppermute | solution.py:577
  30.5 3.3 %collective-permute-start.9 = (f32[8,512]{1,0:T(8,128)S(1)}, f32[8,512]{1,0:T(8,128)S(1)}, u32[]{:S(2)}, u32[]{:S(2)}) collective-permute-start(f32[8,512]{1,0:T(8,128)S(1)} %add_select_fusion.1), channel_id=1, source_target_pairs={{1,2},{3,0},{2,1},{0,3},{5,6},{7,4},{6,5},{4,7},{9,10},{11,8},{10,... | collective-permute-start | bytes 49160 | tf_op jit(solution)/shard_map/ppermute | solution.py:577
  37.7 2.6 %collective-permute-start.12 = (f32[8,512]{1,0:T(8,128)S(1)}, f32[8,512]{1,0:T(8,128)S(1)}, u32[]{:S(2)}, u32[]{:S(2)}) collective-permute-start(f32[8,512]{1,0:T(8,128)S(1)} %get-tuple-element.50), channel_id=1, source_target_pairs={{0,1},{2,3},{1,0},{3,2},{4,5},{6,7},{5,4},{7,6},{8,9},{10,11},{9,8... | collective-permute-start | bytes 49160 | tf_op jit(solution)/shard_map/ppermute | solution.py:577
  37.7 9.0 %collective-permute-start.14 = (f32[2,16,512]{2,1,0:T(8,128)S(1)}, f32[2,16,512]{2,1,0:T(8,128)S(1)}, u32[]{:S(2)}, u32[]{:S(2)}) collective-permute-start(f32[2,16,512]{2,1,0:T(8,128)S(1)} %get-tuple-element.52), channel_id=1, source_target_pairs={{0,4},{8,12},{16,20},{24,28},{4,0},{12,8},{20,16},{28,24},{1,5},{9... | collective-permute-start | bytes 196616 | tf_op jit(solution)/shard_map/ppermute | solution.py:577
  38.5 8.2 %collective-permute-start.15 = (f32[2,16,512]{2,1,0:T(8,128)S(1)}, f32[2,16,512]{2,1,0:T(8,128)S(1)}, u32[]{:S(2)}, u32[]{:S(2)}) collective-permute-start(f32[2,16,512]{2,1,0:T(8,128)S(1)} %get-tuple-element.53), channel_id=1, source_target_pairs={{4,8},{12,16},{20,24},{28,0},{8,4},{16,12},{24,20},{0,28},{5,9},{1... | collective-permute-start | bytes 196616 | tf_op jit(solution)/shard_map/ppermute | solution.py:577
  40.4 3.2 %collective-permute-start.13 = (f32[8,512]{1,0:T(8,128)S(1)}, f32[8,512]{1,0:T(8,128)S(1)}, u32[]{:S(2)}, u32[]{:S(2)}) collective-permute-start(f32[8,512]{1,0:T(8,128)S(1)} %add_select_fusion), channel_id=1, source_target_pairs={{1,2},{3,0},{2,1},{0,3},{5,6},{7,4},{6,5},{4,7},{9,10},{11,8},{10,... | collective-permute-start | bytes 49160 | tf_op jit(solution)/shard_map/ppermute | solution.py:577
  43.5 15.1 %copy-start.5 = (f32[2]{0:T(128)S(1)}, f32[2]{0:T(128)}, u32[]{:S(2)}) copy-start(f32[2]{0:T(128)} %shift.1) | copy-start | bytes 28

commit v4 on v3

--- a/solution.py
+++ b/solution.py
@@ -7,10 +7,10 @@
 from jax.experimental.pallas import tpu as pltpu
 from jax.sharding import PartitionSpec as P
 
+
 INNER_STEPS = 3
 EPSILON = 1e-06
 CENTRE = 7.125
-PARTS = 2
 HIGHEST = lax.Precision.HIGHEST
 VMEM = pltpu.VMEM
 SMEM = pltpu.SMEM
@@ -32,7 +32,7 @@
     return [pltpu.with_memory_space_constraint(a, pltpu.HBM) for a in arrays]
 
 
-def call(kernel, outs, specs, args, scratch=(), cost=1, out_specs=None, limit=8 << 20):
+def call(kernel, outs, specs, args, scratch=(), cost=1, out_specs=None, aliases={}, limit=8 << 20):
     estimate = pl.CostEstimate(flops=0, transcendentals=0, bytes_accessed=cost * 2_000_000)
     if out_specs is None:
         out_specs = jax.tree.map(lambda _: pl.BlockSpec(memory_space=VMEM), outs)
@@ -42,6 +42,7 @@
         in_specs=specs,
         out_specs=out_specs,
         scratch_shapes=list(scratch),
+        input_output_aliases=aliases,
         compiler_params=pltpu.CompilerParams(vmem_limit_bytes=limit),
         cost_estimate=estimate,
     )(*args)
@@ -107,7 +108,7 @@
     write_edges(rows, depth, field, ref_part, ref_line, azim_x, azim_y, dom_x, dom_y)
 
 
-def basis_kernel(part, parts, basis, out, tiles):
+def basis_products(part, parts, basis, tiles):
     half = basis.shape[0]
     count = 2 * half
     lines, width = basis.shape[2] // parts, basis.shape[3]
@@ -128,7 +129,7 @@
         low = (tall - high.astype(jnp.float32)).astype(jnp.bfloat16)
         return jnp.concatenate([high, low], axis=0)
 
-    group = 4
+    group = min(4, lines)
 
     def some(at, total):
         both = jnp.concatenate([one(at * group + i) for i in range(group)], axis=1)
@@ -147,37 +148,48 @@
     table = jnp.where(
         lane < half, top + pltpu.roll(bottom, 128 - half, 1) + crossed - bottom, 0.0
     )
-    out[...] = jnp.zeros_like(out)
     folds = 128 // half
+    packed = []
     for r in range(half // folds):
         rows = [
             pltpu.roll(table[r * folds + s : r * folds + s + 1], half * s, 1) if s
             else table[r * folds : r * folds + 1]
             for s in range(folds)
         ]
-        out[5 + r : 6 + r, :] = total_of(rows)
+        packed.append(total_of(rows))
+    return packed
+
+
+def add_basis_products(part, basis, tiles, dots):
+    for r, row in enumerate(basis_products(part, INNER_STEPS + 1, basis, tiles)):
+        dots[2 + r : 3 + r, :] += row
 
 
 def dots_kernel(k, basis, *refs):
-    powers, (dots_out, held) = refs[: k + 1], refs[-2:]
-    dots_in = refs[k + 1] if k else None
-    add_dots(k, basis, powers[:-1], powers[-1], dots_in, dots_out, held)
-
-
-def first_dots_kernel(basis, power, mats_in, dots_out, mats, held, sems):
-    half = mats.shape[0]
+    powers, (dots_out, held, tiles) = refs[: k + 1], refs[-3:]
+    add_dots(k, basis, powers[:-1], powers[-1], refs[k + 1], dots_out, held)
+    add_basis_products(k, basis, tiles, dots_out)
+
+
+def first_dots_kernel(
+    basis, power, count, mats_in, dots_out, mats, count_out, held, tiles, sems
+):
+    half = sems.shape[0]
     copies = [pltpu.make_async_copy(mats_in.at[s], mats.at[s], sems.at[s]) for s in range(half)]
     for copy in copies:
         copy.start()
     add_dots(0, basis, [], power, None, dots_out, held)
+    add_basis_products(0, basis, tiles, dots_out)
+    count_out[...] = jnp.broadcast_to(count[...], count_out.shape)
     for copy in copies:
         copy.wait()
 
 
-def flame_kernel(base, live, lines, burners, sums, lower, upper, *refs, ready=None):
+def flame_kernel(base, live, lines, burners, sums, mats, *refs, ready=None):
     out, source = refs[-2:]
     width = sums.shape[1]
-    half = lower.shape[0]
+    slots = mats.shape[0]
+    half = slots // 2
     rows = sums.shape[0] - base
     source[...] = jnp.zeros_like(source)
     for i in range(rows):
@@ -203,41 +215,49 @@
         out[0, at, :] += by_re[:, :width] - by_im[:, width:]
         out[1, at, :] += by_im[:, :width] + by_re[:, width:]
 
-    def put_all(first, blocks):
-        every = products(blocks[...].reshape(half * 2 * width, width))
-        for s in range(half):
-
-            @pl.when(first + s < live[0])
+    def put_all(first, number):
+        blocks = mats[first : first + number]
+        every = products(blocks.reshape(number * 2 * width, width))
+        for s in range(number):
+
+            @pl.when(first + s < live[0, 0])
             def _():
                 put(first + s, every[:, 2 * width * s : 2 * width * (s + 1)])
 
     few = half // 2
 
-    @pl.when(live[0] <= few)
+    @pl.when(live[0, 0] <= few)
     def _():
         def slot(s, carry):
-            put(s, products(lower[s]))
+            put(s, products(mats[s]))
             return carry
 
-        lax.fori_loop(0, live[0], slot, 0)
-
-    @pl.when(live[0] > few)
-    def _():
-        put_all(0, lower)
-
-    if ready is not None:
+        lax.fori_loop(0, live[0, 0], slot, 0)
+
+    if ready is None:
+
+        @pl.when(live[0, 0] > few)
+        def _():
+            put_all(0, slots)
+    else:
+
+        @pl.when(live[0, 0] > few)
+        def _():
+            put_all(0, half)
+
         ready()
 
-    @pl.when(live[0] > half)
-    def _():
-        put_all(half, upper)
-
-
-def first_flame_kernel(base, live, lines, burners, sums, lower, mats_in, order, out, upper, *refs):
+        @pl.when(live[0, 0] > half)
+        def _():
+            put_all(half, half)
+
+
+def first_flame_kernel(base, live, lines, burners, sums, given, mats_in, order, out, mats, *refs):
     source, sems = refs
-    half = lower.shape[0]
+    half = sems.shape[0]
     copies = [
-        pltpu.make_async_copy(mats_in.at[half + s], upper.at[s], sems.at[s]) for s in range(half)
+        pltpu.make_async_copy(mats_in.at[half + s], mats.at[half + s], sems.at[s])
+        for s in range(half)
     ]
     for copy in copies:
         copy.start()
@@ -246,7 +266,7 @@
         for copy in copies:
             copy.wait()
 
-    flame_kernel(base, live, lines, burners, sums, lower, upper, order, out, source, ready=ready)
+    flame_kernel(base, live, lines, burners, sums, mats, order, out, source, ready=ready)
 
 
 def step_kernel(
@@ -283,11 +303,9 @@
 
 
 def last_kernel(rows, depth, *refs):
-    first, tables, powers = refs[:7], refs[7 : 7 + PARTS], refs[7 + PARTS : -4]
-    dots_in, dots_out, field, held = refs[-4:]
+    first, powers, (dots_in, dots_out, field, held) = refs[:7], refs[7:-4], refs[-4:]
     step_kernel(rows, depth, None, None, *first, field, None, None, None, None)
     add_dots(len(powers), None, powers, field, dots_in, dots_out, held)
-    dots_out[...] += total_of(table[...] for table in tables)
 
 
 def folded(x):
@@ -304,6 +322,10 @@
             for i in range(0, len(terms), 2)
         ]
     return terms[0]
+
+
+def place_of(k):
+    return (0, 16) if k == INNER_STEPS + 1 else (k // 2, 64 * (k % 2))
 
 
 def add_dots(k, basis, powers, current, dots_in, dots_out, held):
@@ -329,10 +351,11 @@
         jnp.ones((8, 128), jnp.float32), held[...], (((1,), (1,)), ((), ())),
         precision=HIGHEST, preferred_element_type=jnp.float32,
     )
-    at = lax.broadcasted_iota(jnp.int32, row.shape, 0)
-    wide = row.shape[1]
-    dots_out[...] = jnp.zeros_like(dots_out)
-    dots_out[:, :wide] = jnp.where(at == k, row, 0.0 if dots_in is None else dots_in[:, :wide])
+    row = jnp.concatenate([row, jnp.zeros((8, 128 - row.shape[1]), jnp.float32)], axis=1)
+    at, lane = place_of(k)
+    row = pltpu.roll(row, lane, 1) if lane else row
+    dots_out[...] = jnp.zeros_like(dots_out) if dots_in is None else dots_in[...]
+    dots_out[at : at + 1, :] += row[0:1]
 
 
 class Cx:
@@ -469,8 +492,10 @@
     table = [[None] * size for _ in range(size)]
     for i in range(size):
         for j in range(i, size):
-            im = splat(j, base + 8 + i) if i != j else jnp.zeros(tile, jnp.float32)
-            table[i][j] = Cx(splat(j, base + i), im)
+            at, first = place_of(j)
+            first += base + i
+            im = splat(at, first + 8) if i != j else jnp.zeros(tile, jnp.float32)
+            table[i][j] = Cx(splat(at, first), im)
             if i != j:
                 table[j][i] = table[i][j].conj()
     mu = Cx(
@@ -492,7 +517,7 @@
     folds = 128 // count
     table = jnp.concatenate(
         [
-            shifted(gram[5 + r : 6 + r, :], count * q) if q else gram[5 + r : 6 + r, :]
+            shifted(gram[2 + r : 3 + r, :], count * q) if q else gram[2 + r : 3 + r, :]
             for r in range(count // folds)
             for q in range(folds)
         ],
@@ -500,8 +525,13 @@
     )
     lane = lax.broadcasted_iota(jnp.int32, (count, 128), 1)
     same = lax.broadcasted_iota(jnp.int32, (count, 128), 0) == lane
-    by_re = total_of(gram[k : k + 1, :] * v.re[0:1] for k, v in update.items()) * scale
-    by_im = total_of(gram[k : k + 1, :] * v.im[0:1] for k, v in update.items()) * scale
+
+    def of_power(k):
+        at, first = place_of(k)
+        return shifted(gram[at : at + 1, :], first) if first else gram[at : at + 1, :]
+
+    by_re = total_of(of_power(k) * v.re[0:1] for k, v in update.items()) * scale
+    by_im = total_of(of_power(k) * v.im[0:1] for k, v in update.items()) * scale
     first_re = lanes(jnp.where(same, by_re - shifted(by_im, count), 0.0))
     first_im = lanes(jnp.where(same, by_im + shifted(by_re, count), 0.0))
 
@@ -607,62 +637,59 @@
     )
     powers = [power]
     held = VMEM((2 * count + 16, 128), jnp.float32)
-    tables = [
-        call(
-            functools.partial(basis_kernel, part, PARTS),
-            shape(8, 128),
-            vmem(1),
-            (basis,),
-            [VMEM((width // 128, count * 2 * (lines // PARTS), 128), jnp.float32)],
-        )
-        for part in range(PARTS)
-    ]
+    tiles = VMEM((width // 128, count * 2 * (lines // (INNER_STEPS + 1)), 128), jnp.float32)
     is_sum = lax.broadcasted_iota(jnp.int32, (tall, width), 0) >= base
     for step in range(INNER_STEPS + 1):
+        from_dx = exchange(dom_x, "dom", dom_even)
+        from_ax = exchange(azim_x, "azim", azim_even)
         from_ay = exchange(azim_y, "azim", azim_odd)
-        from_dx = exchange(dom_x, "dom", dom_even)
         dom_y = jnp.where(is_sum, dom_x + from_dx, dom_y)
         from_dy = exchange(dom_y, "dom", dom_odd)
-        from_ax = exchange(azim_x, "azim", azim_even)
         sums = dom_y + from_dy
         reach = 4
         while reach < n_dom:
             pairs = [(i, i ^ reach) for i in range(n_dom) if i < i ^ reach]
             sums = sums + exchange(sums, "dom", pairs)
             reach *= 2
-        numbers = (flame_count, flame_line, flame_burner)
+        half = slots // 2
+        blocks = jax.ShapeDtypeStruct(mats.shape, mats.dtype)
         source = VMEM((16, width), jnp.bfloat16)
-        half = slots // 2
-        blocks = jax.ShapeDtypeStruct((half, 2 * width, width), mats.dtype)
         if step == 0:
-            (mats,) = held_in_hbm(mats)
-            dots, lower = call(
+            (mats_in,) = held_in_hbm(mats)
+            dots, mats, live = call(
                 first_dots_kernel,
-                [shape(8, 128), blocks],
-                vmem(2) + in_hbm(1),
-                (basis, power, mats),
-                [held, pltpu.SemaphoreType.DMA((half,))],
+                [shape(4, 128), blocks, jax.ShapeDtypeStruct((8, 128), jnp.int32)],
+                vmem(3) + in_hbm(1),
+                (basis, power, flame_count.reshape(1, 1), mats_in),
+                [held, tiles, pltpu.SemaphoreType.DMA((half,))],
                 cost=2,
-            )
-            flame, upper = call(
-                functools.partial(first_flame_kernel, base),
-                [shape(2, lines, width), blocks],
-                smem(3) + vmem(2) + in_hbm(1) + vmem(1),
-                (*numbers, sums, lower, mats, dots),
-                [source, pltpu.SemaphoreType.DMA((half,))],
-                cost=3,
             )
         else:
             given = (basis, *powers, dots)
             dots = call(
-                functools.partial(dots_kernel, step), shape(8, 128), vmem(len(given)), given, [held]
+                functools.partial(dots_kernel, step),
+                shape(4, 128),
+                vmem(len(given)),
+                given,
+                [held, tiles],
             )
-            order = (dots, *tables[step - 1 : step])
+        numbers = (live, flame_line, flame_burner)
+        if step == 0:
+            flame, mats = call(
+                functools.partial(first_flame_kernel, base),
+                [shape(2, lines, width), blocks],
+                smem(3) + vmem(2) + in_hbm(1) + vmem(1),
+                (*numbers, sums, mats, mats_in, dots),
+                [source, pltpu.SemaphoreType.DMA((half,))],
+                cost=3,
+                aliases={4: 1},
+            )
+        else:
             flame = call(
                 functools.partial(flame_kernel, base),
                 shape(2, lines, width),
-                smem(3) + vmem(3 + len(order)),
-                (*numbers, sums, lower, upper, *order),
+                smem(3) + vmem(3),
+                (*numbers, sums, mats, dots),
                 [source],
                 cost=3,
             )
@@ -677,9 +704,9 @@
         else:
             dots = call(
                 functools.partial(last_kernel, rows, depth),
-                shape(8, 128),
-                vmem(8 + len(tables) + len(powers)),
-                (*received, *tables, *powers, dots),
+                shape(4, 128),
+                vmem(8 + len(powers)),
+                (*received, *powers, dots),
                 [VMEM((2, lines, width), jnp.float32), held],
             )
         powers.append(power)

time: 61.3 us -> 60 us (0.979)
  Pallas kernels: 27.5 us -> 19.3 us
  starting transfers between devices: 15.7 us -> 20.1 us
  waiting for transfers between devices: 4.32 us -> 6.29 us
  blocking collectives: 11.4 us -> 12.1 us
    pallas_call x16 -> x14, Pallas kernels: 27.5 us -> 19.3 us  [call(): pl.pallas_call(kernel, out_shape=outs, in_specs=specs, out_specs=out_spec...]
    ppermute x16, starting transfers between devices: 15.7 us -> 20.1 us  [exchange(): return lax.ppermute(values, axis, both)]
    ppermute x16, waiting for transfers between devices: 4.32 us -> 6.29 us  [exchange(): return lax.ppermute(values, axis, both)]
    all_to_all x1, blocking collectives: 11.4 us -> 12.1 us  [on_device(): gram = jnp.sum(lax.all_to_all(spread, ('azim', 'dom'), 0, 0), axis=0)]
  transfers between devices with their start and end apart: 16 -> 16, of which waited for: 3 -> 5; matrix products, arithmetic and copies ran while one was open for 1% -> 1% of each run, Pallas kernels for 34% -> 21%
where the time goes in v4:
time: 60 us; the launch traced here: 59.8 us
  starting transfers between devices  20.1 us (34%)
  Pallas kernels  19.3 us (32%)
  blocking collectives  12.1 us (20%)
  waiting for transfers between devices  6.29 us (10%)
  between operations  1.58 us (3%)
    ppermute x16, starting transfers between devices, exchange(): return lax.ppermute(values, axis, both)  20.1 us
    pallas_call x14, Pallas kernels, call(): pl.pallas_call(kernel, out_shape=outs, in_specs=specs, out_specs=out_spec...  19.3 us
    all_to_all x1, blocking collectives, on_device(): gram = jnp.sum(lax.all_to_all(spread, ('azim', 'dom'), 0, 0), axis=0)  12.1 us
    ppermute x16, waiting for transfers between devices, exchange(): return lax.ppermute(values, axis, both)  6.29 us
  transfers between devices with their start and end apart: 16, of which 5 were waited for; matrix products, arithmetic and copies ran while one was open for 1% of the time, Pallas kernels for 21%

profile of v4, /device:TPU:0, one launch (start us, length us, event | category | flops | bytes accessed | tf_op | source)
XLA Modules:
  0.0 59.8 jit_solution(4143209264665867211)
XLA Ops:
  0.7 1.7 %shard_map.113 = (f32[2,32,512]{2,1,0:T(8,128)S(1)}, f32[2,16,512]{2,1,0:T(8,128)S(1)}, f32[2,16,512]{2,1,0:T(8,128)S(1)}, f32[8,512]{1,0:T(8,128)S(1)}, f32[8,5...) custom-call(f32[2,16]{1,0:T(2,128)} %coef_in.1, s32[2]{0:T(128)} %ref_part.5, s32[2]{0:T(128)} %ref_line.5, ...), custom_call_target="tpu_custom_call" | custom-call | bytes 8000000 | tf_op jit(solution)/shard_map/pallas_call | solution.py:39
  2.3 0.6 collective-permute-start
  2.9 2.6 %collective-permute-start.2 = (f32[2,16,512]{2,1,0:T(8,128)S(1)}, f32[2,16,512]{2,1,0:T(8,128)S(1)}, u32[]{:S(2)}, u32[]{:S(2)}) collective-permute-start(f32[2,16,512]{2,1,0:T(8,128)S(1)} %get-tuple-element.38), channel_id=1, source_target_pairs={{0,4},{8,12},{16,20},{24,28},{4,0},{12,8},{20,16},{28,24},{1,5},{9... | collective-permute-start | bytes 196616 | tf_op jit(solution)/shard_map/ppermute | solution.py:607
  5.5 3.5 %collective-permute-start.3 = (f32[2,16,512]{2,1,0:T(8,128)S(1)}, f32[2,16,512]{2,1,0:T(8,128)S(1)}, u32[]{:S(2)}, u32[]{:S(2)}) collective-permute-start(f32[2,16,512]{2,1,0:T(8,128)S(1)} %get-tuple-element.39), channel_id=1, source_target_pairs={{4,8},{12,16},{20,24},{28,0},{8,4},{16,12},{24,20},{0,28},{5,9},{1... | collective-permute-start | bytes 196616 | tf_op jit(solution)/shard_map/ppermute | solution.py:607
  9.0 0.1 add_select_fusion.3
  9.1 1.0 %collective-permute-start.1 = (f32[8,512]{1,0:T(8,128)S(1)}, f32[8,512]{1,0:T(8,128)S(1)}, u32[]{:S(2)}, u32[]{:S(2)}) collective-permute-start(f32[8,512]{1,0:T(8,128)S(1)} %add_select_fusion.3), channel_id=1, source_target_pairs={{1,2},{3,0},{2,1},{0,3},{5,6},{7,4},{6,5},{4,7},{9,10},{11,8},{10,... | collective-permute-start | bytes 49160 | tf_op jit(solution)/shard_map/ppermute | solution.py:607
  10.7 2.2 %shard_map.114 = (f32[4,128]{1,0:T(4,128)S(1)}, bf16[8,1024,512]{2,1,0:T(8,128)(2,1)S(1)}, s32[8,128]{1,0:T(8,128)S(1)}) custom-call(f32[16,2,32,512]{3,2,1,0:T(8,128)S(1)} %get-tuple-element.31.basis, f32[2,32,512]{2,1,0:T(8,128)S(1)} %get-tuple-element.30.power.old.refs_0_.refs_7_, s32[1,1]{1,0:T(1,128)} %bitcast.5.count, bf16[8,1024,512]{2,1,0:T(8,128)(2,1)} %bitcast.10), custom_call_target="tpu_custom_call" | custom-call | bytes 4000000 | tf_op jit(solution)/shard_map/pallas_call | solution.py:39
  13.0 0.0 copy-start
  13.0 0.0 copy-start.3
  13.0 0.0 copy-start.4
  13.0 2.8 %shard_map.115 = (f32[2,32,512]{2,1,0:T(8,128)S(1)}, bf16[8,1024,512]{2,1,0:T(8,128)(2,1)S(1)}) custom-call(s32[8,128]{1,0:T(8,128)S(1)} %get-tuple-element.32.live, s32[8]{0:T(128)S(1)} %copy-done.1, s32[8]{0:T(128)S(1)} %copy-done.2, f32[8,512]{1,0:T(8,128)S(1)} %add.25.sums, ...), custom_call_target="tpu_custom_call", output_to_operand_aliasing={{1}: (4, {})} | custom-call | bytes 6000000 | tf_op jit(solution)/shard_map/pallas_call | solution.py:39
  15.9 0.7 %shard_map.116 = (f32[2,32,512]{2,1,0:T(8,128)S(1)}, f32[2,16,512]{2,1,0:T(8,128)S(1)}, f32[2,16,512]{2,1,0:T(8,128)S(1)}, f32[8,512]{1,0:T(8,128)S(1)}, f32[8,512]{1,0:T(8,128)S(1)}) custom-call(s32[2]{0:T(128)S(1)} %copy-done.3, s32[2]{0:T(128)S(1)} %copy-done.4, f32[2,32,512]{2,1,0:T(8,128)S(1)} %get-tuple-element.30.power.old.refs_0_.refs_7_, ...), custom_call_target="tpu_custom_call" | custom-call | bytes 2000000 | tf_op jit(solution)/shard_map/pallas_call | solution.py:39
  16.6 2.0 %collective-permute-start.4 = (f32[8,512]{1,0:T(8,128)S(1)}, f32[8,512]{1,0:T(8,128)S(1)}, u32[]{:S(2)}, u32[]{:S(2)}) collective-permute-start(f32[8,512]{1,0:T(8,128)S(1)} %get-tuple-element.41), channel_id=1, source_target_pairs={{0,1},{2,3},{1,0},{3,2},{4,5},{6,7},{5,4},{7,6},{8,9},{10,11},{9,8... | collective-permute-start | bytes 49160 | tf_op jit(solution)/shard_map/ppermute | solution.py:607
  18.6 0.0 collective-permute-start.6
  18.6 0.6 %collective-permute-start.7 = (f32[2,16,512]{2,1,0:T(8,128)S(1)}, f32[2,16,512]{2,1,0:T(8,128)S(1)}, u32[]{:S(2)}, u32[]{:S(2)}) collective-permute-start(f32[2,16,512]{2,1,0:T(8,128)S(1)} %get-tuple-element.45), channel_id=1, source_target_pairs={{4,8},{12,16},{20,24},{28,0},{8,4},{16,12},{24,20},{0,28},{5,9},{1... | collective-permute-start | bytes 196616 | tf_op jit(solution)/shard_map/ppermute | solution.py:607
  19.3 0.2 collective-permute-done.4.from_dx
  19.5 0.1 add_select_fusion.2
  19.5 0.9 %collective-permute-start.5 = (f32[8,512]{1,0:T(8,128)S(1)}, f32[8,512]{1,0:T(8,128)S(1)}, u32[]{:S(2)}, u32[]{:S(2)}) collective-permute-start(f32[8,512]{1,0:T(8,128)S(1)} %add_select_fusion.2), channel_id=1, source_target_pairs={{1,2},{3,0},{2,1},{0,3},{5,6},{7,4},{6,5},{4,7},{9,10},{11,8},{10,... | collective-permute-start | bytes 49160 | tf_op jit(solution)/shard_map/ppermute | solution.py:607
  20.4 1.5 %shard_map.117.refs_0_.refs_3_ = f32[4,128]{1,0:T(4,128)S(1)} custom-call(f32[16,2,32,512]{3,2,1,0:T(8,128)S(1)} %get-tuple-element.31.basis, f32[2,32,512]{2,1,0:T(8,128)S(1)} %get-tuple-element.30.power.old.refs_0_.refs_7_, f32[2,32,512]{2,1,0:T(8,128)S(1)} %get-tuple-element.40.refs_1_.old.refs_8_, f32[4,128]{1,0:T(4,128)S(1)} %get-tuple-element.36.order.refs_2_), custom_call_target="tpu_custom_call" | custom-call | bytes 2000000 | tf_op jit(solution)/shard_map/pallas_call | solution.py:39
  22.0 0.7 %collective-permute-done.5.from_dy = f32[8,512]{1,0:T(8,128)S(1)} collective-permute-done((f32[8,512]{1,0:T(8,128)S(1)}, f32[8,512]{1,0:T(8,128)S(1)}, u32[]{:S(2)}, u32[]{:S(2)}) %collective-permute-start.5) | collective-permute-done | bytes 16416 | tf_op jit(solution)/shard_map/ppermute | solution.py:607
  22.7 1.0 %shard_map.118.flame = f32[2,32,512]{2,1,0:T(8,128)S(1)} custom-call(s32[8,128]{1,0:T(8,128)S(1)} %get-tuple-element.32.live, s32[8]{0:T(128)S(1)} %copy-done.1, s32[8]{0:T(128)S(1)} %copy-done.2, f32[8,512]{1,0:T(8,128)S(1)} %add.27.sums, bf16[8,1024,512]{2,1,0:T(8,128)(2,1)S(1)} %get-tuple-element.43.mats, f32[4,128]{1,0:T(4,128)S(1)} %shard_map.117.refs_0_.refs_3_), custom_call_target="tpu_custom_call" | custom-call | bytes 6000000 | tf_op jit(solution)/shard_map/pallas_call | solution.py:39
  23.8 0.0 collective-permute-done.6.from_ax
  23.8 1.8 %collective-permute-done.7.from_ay = f32[2,16,512]{2,1,0:T(8,128)S(1)} collective-permute-done((f32[2,16,512]{2,1,0:T(8,128)S(1)}, f32[2,16,512]{2,1,0:T(8,128)S(1)}, u32[]{:S(2)}, u32[]{:S(2)}) %collective-permute-start.7) | collective-permute-done | bytes 65568 | tf_op jit(solution)/shard_map/ppermute | solution.py:607
  25.6 0.7 %shard_map.119 = (f32[2,32,512]{2,1,0:T(8,128)S(1)}, f32[2,16,512]{2,1,0:T(8,128)S(1)}, f32[2,16,512]{2,1,0:T(8,128)S(1)}, f32[8,512]{1,0:T(8,128)S(1)}, f32[8,512]{1,0:T(8,128)S(1)}) custom-call(s32[2]{0:T(128)S(1)} %copy-done.3, s32[2]{0:T(128)S(1)} %copy-done.4, f32[2,32,512]{2,1,0:T(8,128)S(1)} %get-tuple-element.40.refs_1_.old.refs_8_, ...), custom_call_target="tpu_custom_call" | custom-call | bytes 2000000 | tf_op jit(solution)/shard_map/pallas_call | solution.py:39
  26.3 0.7 %collective-permute-start.8 = (f32[8,512]{1,0:T(8,128)S(1)}, f32[8,512]{1,0:T(8,128)S(1)}, u32[]{:S(2)}, u32[]{:S(2)}) collective-permute-start(f32[8,512]{1,0:T(8,128)S(1)} %get-tuple-element.47), channel_id=1, source_target_pairs={{0,1},{2,3},{1,0},{3,2},{4,5},{6,7},{5,4},{7,6},{8,9},{10,11},{9,8... | collective-permute-start | bytes 49160 | tf_op jit(solution)/shard_map/ppermute | solution.py:607
  27.0 1.4 %collective-permute-start.10 = (f32[2,16,512]{2,1,0:T(8,128)S(1)}, f32[2,16,512]{2,1,0:T(8,128)S(1)}, u32[]{:S(2)}, u32[]{:S(2)}) collective-permute-start(f32[2,16,512]{2,1,0:T(8,128)S(1)} %get-tuple-element.49), channel_id=1, source_target_pairs={{0,4},{8,12},{16,20},{24,28},{4,0},{12,8},{20,16},{28,24},{1,5},{9... | collective-permute-start | bytes 196616 | tf_op jit(solution)/shard_map/ppermute | solution.py:607
  28.4 0.3 collective-permute-start.11
  28.7 0.0 collective-permute-done.8.from_dx
  28.7 0.1 add_select_fusion.1
  28.8 2.1 %collective-permute-start.9 = (f32[8,512]{1,0:T(8,128)S(1)}, f32[8,512]{1,0:T(8,128)S(1)}, u32[]{:S(2)}, u32[]{:S(2)}) collective-permute-start(f32[8,512]{1,0:T(8,128)S(1)} %add_select_fusion.1), channel_id=1, source_target_pairs={{1,2},{3,0},{2,1},{0,3},{5,6},{7,4},{6,5},{4,7},{9,10},{11,8},{10,... | collective-permute-start | bytes 49160 | tf_op jit(solution)/shard_map/ppermute | solution.py:607
  30.9 1.5 %shard_map.120.refs_0_.refs_4_ = f32[4,128]{1,0:T(4,128)S(1)} custom-call(f32[16,2,32,512]{3,2,1,0:T(8,128)S(1)} %get-tuple-element.31.basis, f32[2,32,512]{2,1,0:T(8,128)S(1)} %get-tuple-element.30.power.old.refs_0_.refs_7_, f32[2,32,512]{2,1,0:T(8,128)S(1)} %get-tuple-element.40.refs_1_.old.refs_8_, ...), custom_call_target="tpu_custom_call" | custom-call | bytes 2000000 | tf_op jit(solution)/shard_map/pallas_call | solution.py:39
  32.4 1.0 %shard_map.121.flame = f32[2,32,512]{2,1,0:T(8,128)S(1)} custom-call(s32[8,128]{1,0:T(8,128)S(1)} %get-tuple-element.32.live, s32[8]{0:T(128)S(1)} %copy-done.1, s32[8]{0:T(128)S(1)} %copy-done.2, f32[8,512]{1,0:T(8,128)S(1)} %add.29.sums, bf16[8,1024,512]{2,1,0:T(8,128)(2,1)S(1)} %get-tuple-element.43.mats, f32[4,128]{1,0:T(4,128)S(1)} %shard_map.120.refs_0_.refs_4_), custom_call_target="tpu_custom_call" | custom-call | bytes 6000000 | tf_op jit(solution)/shard_map/pallas_call | solution.py:39
  33.4 0.0 copy-start.5
  33.5 0.0 collective-permute-done.10.from_ax
  33.5 1.9 %collective-permute-done.11.from_ay = f32[2,16,512]{2,1,0:T(8,128)S(1)} collective-permute-done((f32[2,16,512]{2,1,0:T(8,128)S(1)}, f32[2,16,512]{2,1,0:T(8,128)S(1)}, u32[]{:S(2)}, u32[]{:S(2)}) %collective-permute-start.11) | collective-permute-done | bytes 65568 | tf_op jit(solution)/shard_map/ppermute | solution.py:607
  35.4 0.7 %shard_map.122 = (f32[2,32,512]{2,1,0:T(8,128)S(1)}, f32[2,16,512]{2,1,0:T(8,128)S(1)}, f32[2,16,512]{2,1,0:T(8,128)S(1)}, f32[8,512]{1,0:T(8,128)S(1)}, f32[8,512]{1,0:T(8,128)S(1)}) custom-call(s32[2]{0:T(128)S(1)} %copy-done.3, s32[2]{0:T(128)S(1)} %copy-done.4, f32[2,32,512]{2,1,0:T(8,128)S(1)} %get-tuple-element.46.refs_2_.old.refs_9_, ...), custom_call_target="tpu_custom_call" | custom-call | bytes 2000000 | tf_op jit(solution)/shard_map/pallas_call | solution.py:39
  36.1 0.9 %collective-permute-start.12 = (f32[8,512]{1,0:T(8,128)S(1)}, f32[8,512]{1,0:T(8,128)S(1)}, u32[]{:S(2)}, u32[]{:S(2)}) collective-permute-start(f32[8,512]{1,0:T(8,128)S(1)} %get-tuple-element.52), channel_id=1, source_target_pairs={{0,1},{2,3},{1,0},{3,2},{4,5},{6,7},{5,4},{7,6},{8,9},{10,11},{9,8... | collective-permute-start | bytes 49160 | tf_op jit(solution)/shard_map/ppermute | solution.py:607
  37.0 0.9 %collective-permute-start.14 = (f32[2,16,512]{2,1,0:T(8,128)S(1)}, f32[2,16,512]{2,1,0:T(8,128)S(1)}, u32[]{:S(2)}, u32[]{:S(2)}) collective-permute-start(f32[2,16,512]{2,1,0:T(8,128)S(1)} %get-tuple-element.54), channel_id=1, source_target_pairs={{0,4},{8,12},{16,20},{24,28},{4,0},{12,8},{20,16},{28,24},{1,5},{9... | collective-permute-start | bytes 196616 | tf_op jit(solution)/shard_map/ppermute | solution.py:607
  37.9 0.6 %collective-permute-start.15 = (f32[2,16,512]{2,1,0:T(8,128)S(1)}, f32[2,16,512]{2,1,0:T(8,128)S(1)}, u32[]{:S(2)}, u32[]{:S(2)}) collective-permute-start(f32[2,16,512]{2,1,0:T(8,128)S(1)} %get-tuple-element.55), channel_id=1, source_target_pairs={{4,8},{12,16},{20,24},{28,0},{8,4},{16,12},{24,20},{0,28},{5,9},{1... | collective-permute-start | bytes 196616 | tf_op jit(solution)/shard_map/ppermute | solution.py:607
  38.5 0.0 collective-permute-done.12.refs_5_
  38.5 0.1 add_select_fusion
  38.6 2.0 %collective-permute-start.13 = (f32[8,512]{1,0:T(8,128)S(1)}, f32[8,512]{1,0:T(8,128)S(1)}, u32[]{:S(2)}, u32[]{:S(2)}) collective-permute-start(f32[8,512]{1,0:T(8,128)S(1)} %add_select_fusion), channel_id=1, source_target_pairs={{1,2},{3,0},{2,1},{0,3},{5,6},{7,4},{6,5},{4,7},{9,10},{11,8},{10,... | collective-permute-start | bytes 49160 | tf_op jit(solution)/shard_map/ppermute | solution.py:607
  40.6 1.6 %shard_map.123.refs_0_.refs_11_ = f32[4,128]{1,0:T(4,128)S(1)} custom-call(f32[16,2,32,512]{3,2,1,0:T(8,128)S(1)} %get-tuple-element.31.basis, f32[2,32,512]{2,1,0:T(8,128)S(1)} %get-tuple-element.30.power.old.refs_0_.refs_7_, f32[2,32,512]{2,1,0:T(8,128)S(1)} %get-tuple-element.40.refs_1_.old.refs_8_, ...), custom_call_target="tpu_custom_call" | custom-call | bytes 2000000 | tf_op jit(solution)/shard_map/pallas_call | solution.py:39
  42.2 1.0 %shard_map.124.refs_1_ = f32[2,32,512]{2,1,0:T(8,128)S(1)} custom-call(s32[8,128]{1,0:T(8,128)S(1)} %get-tuple-element.32.live, s32[8]{0:T(128)S(1)} %copy-done.1, s32[8]{0:T(128)S(1)} %copy-done.2, f32[8,512]{1,0:T(8,128)S(1)} %add.31.sums, bf16[8,1024,512]{2,1,0:T(8,128)(2,1)S(1)} %get-tuple-element.43.mats, f32[4,128]{1,0:T(4,128)S(1)} %shard_map.123.refs_0_.refs_11_), custom_call_target="tpu_custom_call" | custom-call | bytes 6000000 | tf_op jit(solution)/shard_map/pallas_call | solution.py:39
  43.3 1.6 %collective-permute-done.15.refs_4_ = f32[2,16,512]{2,1,0:T(8,128)S(1)} collective-permute-done((f32[2,16,512]{2,1,0:T(8,128)S(1)}, f32[2,16,512]{2,1,0:T(8,128)S(1)}, u32[]{:S(2)}, u32[]{:S(2)}) %collective-permute-start.15) | collective-permute-done | bytes 65568 | tf_op jit(solution)/shard_map/ppermute | solution.py:607
  44.8 0.5 shard_map.125
  45.3 12.1 %all_to_all.5 = f32[32,4,128]{2,1,0:T(4,128)S(1)} all-to-all(f32[32,4,128]{2,1,0:T(4,128)S(1)} %broadcast_in_dim.2), channel_id=1, replica_groups=mesh['azim'=8,'dom'=4] {'azim','dom'}, dimensions={0} | all-to-all | bytes 131072 | tf_op jit(solution)/shard_map/all_to_all | solution.py:715
  57.5 2.3 %shard_map.126 = (f32[2,32,512]{2,1,0:T(8,128)}, f32[2]{0:T(128)}) custom-call(f32[2]{0:T(128)S(1)} %copy-done.5, f32[4,128]{1,0:T(4,128)S(1)} %reduce_sum.9.gram_s.gram, f32[4,128]{1,0:T(4,128)S(1)} %reduce_sum.9.gram_s.gram, f32[16,2,32,512]{3,2,1,0:T(8,128)S(1)} %get-tuple-element.31.basis, f32[2,32,512]{2,1,0:T(8,128)S(1)} %get-tuple-element.30.power.old.refs_0_.refs_7_, ...), custom_call_target="tpu_custom_call" | custom-call | bytes 2000000 | tf_op jit(solution)/shard_map/pallas_call | solution.py:39
  (22 shorter events, 0.1 us)
Async XLA Ops:
  0.6 12.3 %copy-start.2 = (s32[8]{0:T(128)S(1)}, s32[8]{0:T(128)}, u32[]{:S(2)}) copy-start(s32[8]{0:T(128)} %burners.7) | copy-start | bytes 100
  0.6 12.3 %copy-start.1 = (s32[8]{0:T(128)S(1)}, s32[8]{0:T(128)}, u32[]{:S(2)}) copy-start(s32[8]{0:T(128)} %lines.7) | copy-start | bytes 100
  2.3 6.7 %collective-permute-start = (f32[8,512]{1,0:T(8,128)S(1)}, f32[8,512]{1,0:T(8,128)S(1)}, u32[]{:S(2)}, u32[]{:S(2)}) collective-permute-start(f32[8,512]{1,0:T(8,128)S(1)} %get-tuple-element.33), channel_id=1, source_target_pairs={{0,1},{2,3},{1,0},{3,2},{4,5},{6,7},{5,4},{7,6},{8,9},{10,11},{9,8... | collective-permute-start | bytes 49160 | tf_op jit(solution)/shard_map/ppermute | solution.py:607
  2.9 13.0 %collective-permute-start.2 = (f32[2,16,512]{2,1,0:T(8,128)S(1)}, f32[2,16,512]{2,1,0:T(8,128)S(1)}, u32[]{:S(2)}, u32[]{:S(2)}) collective-permute-start(f32[2,16,512]{2,1,0:T(8,128)S(1)} %get-tuple-element.38), channel_id=1, source_target_pairs={{0,4},{8,12},{16,20},{24,28},{4,0},{12,8},{20,16},{28,24},{1,5},{9... | collective-permute-start | bytes 196616 | tf_op jit(solution)/shard_map/ppermute | solution.py:607
  5.5 10.4 %collective-permute-start.3 = (f32[2,16,512]{2,1,0:T(8,128)S(1)}, f32[2,16,512]{2,1,0:T(8,128)S(1)}, u32[]{:S(2)}, u32[]{:S(2)}) collective-permute-start(f32[2,16,512]{2,1,0:T(8,128)S(1)} %get-tuple-element.39), channel_id=1, source_target_pairs={{4,8},{12,16},{20,24},{28,0},{8,4},{16,12},{24,20},{0,28},{5,9},{1... | collective-permute-start | bytes 196616 | tf_op jit(solution)/shard_map/ppermute | solution.py:607
  9.1 3.8 %collective-permute-start.1 = (f32[8,512]{1,0:T(8,128)S(1)}, f32[8,512]{1,0:T(8,128)S(1)}, u32[]{:S(2)}, u32[]{:S(2)}) collective-permute-start(f32[8,512]{1,0:T(8,128)S(1)} %add_select_fusion.3), channel_id=1, source_target_pairs={{1,2},{3,0},{2,1},{0,3},{5,6},{7,4},{6,5},{4,7},{9,10},{11,8},{10,... | collective-permute-start | bytes 49160 | tf_op jit(solution)/shard_map/ppermute | solution.py:607
  13.0 2.9 %copy-start = (f32[2,16,512]{2,1,0:T(8,128)S(1)}, f32[2,16,512]{2,1,0:T(8,128)}, u32[]{:S(2)}) copy-start(f32[2,16,512]{2,1,0:T(8,128)} %param.13) | copy-start | bytes 196612
  13.0 2.9 %copy-start.3 = (s32[2]{0:T(128)S(1)}, s32[2]{0:T(128)}, u32[]{:S(2)}) copy-start(s32[2]{0:T(128)} %ref_part.5) | copy-start | bytes 28
  13.0 2.9 %copy-start.4 = (s32[2]{0:T(128)S(1)}, s32[2]{0:T(128)}, u32[]{:S(2)}) copy-start(s32[2]{0:T(128)} %ref_line.5) | copy-start | bytes 28
  16.6 2.8 %collective-permute-start.4 = (f32[8,512]{1,0:T(8,128)S(1)}, f32[8,512]{1,0:T(8,128)S(1)}, u32[]{:S(2)}, u32[]{:S(2)}) collective-permute-start(f32[8,512]{1,0:T(8,128)S(1)} %get-tuple-element.41), channel_id=1, source_target_pairs={{0,1},{2,3},{1,0},{3,2},{4,5},{6,7},{5,4},{7,6},{8,9},{10,11},{9,8... | collective-permute-start | bytes 49160 | tf_op jit(solution)/shard_map/ppermute | solution.py:607
  18.6 5.1 %collective-permute-start.6 = (f32[2,16,512]{2,1,0:T(8,128)S(1)}, f32[2,16,512]{2,1,0:T(8,128)S(1)}, u32[]{:S(2)}, u32[]{:S(2)}) collective-permute-start(f32[2,16,512]{2,1,0:T(8,128)S(1)} %get-tuple-element.44), channel_id=1, source_target_pairs={{0,4},{8,12},{16,20},{24,28},{4,0},{12,8},{20,16},{28,24},{1,5},{9... | collective-permute-start | bytes 196616 | tf_op jit(solution)/shard_map/ppermute | solution.py:607
  18.6 7.0 %collective-permute-start.7 = (f32[2,16,512]{2,1,0:T(8,128)S(1)}, f32[2,16,512]{2,1,0:T(8,128)S(1)}, u32[]{:S(2)}, u32[]{:S(2)}) collective-permute-start(f32[2,16,512]{2,1,0:T(8,128)S(1)} %get-tuple-element.45), channel_id=1, source_target_pairs={{4,8},{12,16},{20,24},{28,0},{8,4},{16,12},{24,20},{0,28},{5,9},{1... | collective-permute-start | bytes 196616 | tf_op jit(solution)/shard_map/ppermute | solution.py:607
  19.5 3.2 %collective-permute-start.5 = (f32[8,512]{1,0:T(8,128)S(1)}, f32[8,512]{1,0:T(8,128)S(1)}, u32[]{:S(2)}, u32[]{:S(2)}) collective-permute-start(f32[8,512]{1,0:T(8,128)S(1)} %add_select_fusion.2), channel_id=1, source_target_pairs={{1,2},{3,0},{2,1},{0,3},{5,6},{7,4},{6,5},{4,7},{9,10},{11,8},{10,... | collective-permute-start | bytes 49160 | tf_op jit(solution)/shard_map/ppermute | solution.py:607
  26.3 2.4 %collective-permute-start.8 = (f32[8,512]{1,0:T(8,128)S(1)}, f32[8,512]{1,0:T(8,128)S(1)}, u32[]{:S(2)}, u32[]{:S(2)}) collective-permute-start(f32[8,512]{1,0:T(8,128)S(1)} %get-tuple-element.47), channel_id=1, source_target_pairs={{0,1},{2,3},{1,0},{3,2},{4,5},{6,7},{5,4},{7,6},{8,9},{10,11},{9,8... | collective-permute-start | bytes 49160 | tf_op jit(solution)/shard_map/ppermute | solution.py:607
  27.0 6.5 %collective-permute-start.10 = (f32[2,16,512]{2,1,0:T(8,128)S(1)}, f32[2,16,512]{2,1,0:T(8,128)S(1)}, u32[]{:S(2)}, u32[]{:S(2)}) collective-permute-start(f32[2,16,512]{2,1,0:T(8,128)S(1)} %get-tuple-element.49), channel_id=1, source_target_pairs={{0,4},{8,12},{16,20},{24,28},{4,0},{12,8},{20,16},{28,24},{1,5},{9... | collective-permute-start | bytes 196616 | tf_op jit(solution)/shard_map/ppermute | solution.py:607
  28.4 7.0 %collective-permute-start.11 = (f32[2,16,512]{2,1,0:T(8,128)S(1)}, f32[2,16,512]{2,1,0:T(8,128)S(1)}, u32[]{:S(2)}, u32[]{:S(2)}) collective-permute-start(f32[2,16,512]{2,1,0:T(8,128)S(1)} %get-tuple-element.50), channel_id=1, source_target_pairs={{4,8},{12,16},{20,24},{28,0},{8,4},{16,12},{24,20},{0,28},{5,9},{1... | collective-permute-start | bytes 196616 | tf_op jit(solution)/shard_map/ppermute | solution.py:607
  28.8 3.6 %collective-permute-start.9 = (f32[8,512]{1,0:T(8,128)S(1)}, f32[8,512]{1,0:T(8,128)S(1)}, u32[]{:S(2)}, u32[]{:S(2)}) collective-permute-start(f32[8,512]{1,0:T(8,128)S(1)} %add_select_fusion.1), channel_id=1, source_target_pairs={{1,2},{3,0},{2,1},{0,3},{5,6},{7,4},{6,5},{4,7},{9,10},{11,8},{10,... | collective-permute-start | bytes 49160 | tf_op jit(solution)/shard_map/ppermute | solution.py:607
  33.4 24.0 %copy-start.5 = (f32[2]{0:T(128)S(1)}, f32[2]{0:T(128)}, u32[]{:S(2)}) copy-start(f32[2]{0:T(128)} %shift.1) | copy-start | bytes 28
  36.1 2.4 %collective-permute-start.12 = (f32[8,512]{1,0:T(8,128)S(1)}, f32[8,512]{1,0:T(8,128)S(1)}, u32[]{:S(2)}, u32[]{:S(2)}) collective-permute-start(f32[8,512]{1,0:T(8,128)S(1)} %get-tuple-element.52), channel_id=1, source_target_pairs={{0,1},{2,3},{1,0},{3,2},{4,5},{6,7},{5,4},{7,6},{8,9},{10,11},{9,8... | collective-permute-start | bytes 49160 | tf_op jit(solution)/shard_map/ppermute | solution.py:607
  37.0 6.3 %collective-permute-start.14 = (f32[2,16,512]{2,1,0:T(8,128)S(1)}, f32[2,16,512]{2,1,0:T(8,128)S(1)}, u32[]{:S(2)}, u32[]{:S(2)}) collective-permute-start(f32[2,16,512]{2,1,0:T(8,128)S(1)} %get-tuple-element.54), channel_id=1, source_target_pairs={{0,4},{8,12},{16,20},{24,28},{4,0},{12,8},{20,16},{28,24},{1,5},{9... | collective-permute-start | bytes 196616 | tf_op jit(solution)/shard_map/ppermute | solution.py:607
  37.9 7.0 %collective-permute-start.15 = (f32[2,16,512]{2,1,0:T(8,128)S(1)}, f32[2,16,512]{2,1,0:T(8,128)S(1)}, u32[]{:S(2)}, u32[]{:S(2)}) collective-permute-start(f32[2,16,512]{2,1,0:T(8,128)S(1)} %get-tuple-element.55), channel_id=1, source_target_pairs={{4,8},{12,16},{20,24},{28,0},{8,4},{16,12},{24,20},{0,28},{5,9},{1... | collective-permute-start | bytes 196616 | tf_op jit(solution)/shard_map/ppermute | solution.py:607
  38.6 3.6 %collective-permute-start.13 = (f32[8,512]{1,0:T(8,128)S(1)}, f32[8,512]{1,0:T(8,128)S(1)}, u32[]{:S(2)}, u32[]{:S(2)}) collective-permute-start(f32[8,512]{1,0:T(8,128)S(1)} %add_select_fusion), channel_id=1, source_target_pairs={{1,2},{3,0},{2,1},{0,3},{5,6},{7,4},{6,5},{4,7},{9,10},{11,8},{10,... | collective-permute-start | bytes 49160 | tf_op jit(solution)/shard_map/ppermute | solution.py:607

commit v5 on v4

--- a/solution.py
+++ b/solution.py
@@ -74,9 +74,17 @@
             dom_y[at : at + 1, :] = jnp.zeros_like(line)
 
 
+def bring(source, target, first, sems):
+    return [
+        pltpu.make_async_copy(source.at[first + s], target.at[first + s], sems.at[s])
+        for s in range(sems.shape[0])
+    ]
+
+
 def start_kernel(
-    rows, depth, coef_in, part_in, line_in, basis_in,
-    field, azim_x, azim_y, dom_x, dom_y, basis, coef, ref_part, ref_line, small_sems, sems,
+    rows, depth, coef_in, part_in, line_in, basis_in, mats_in,
+    field, azim_x, azim_y, dom_x, dom_y, basis, mats,
+    coef, ref_part, ref_line, small_sems, sems, block_sems,
 ):
     count = basis.shape[0]
     pairs = ((coef_in, coef), (part_in, ref_part), (line_in, ref_line))
@@ -88,7 +96,8 @@
         )
         for i in range(sems.shape[0])
     ]
-    for copy in small + large:
+    blocks = bring(mats_in, mats, 0, block_sems)
+    for copy in small + large + blocks:
         copy.start()
     for copy in small:
         copy.wait()
@@ -106,6 +115,8 @@
             field[0, span, :] = real if at == 0 else field[0, span, :] + real
             field[1, span, :] = imag if at == 0 else field[1, span, :] + imag
     write_edges(rows, depth, field, ref_part, ref_line, azim_x, azim_y, dom_x, dom_y)
+    for copy in blocks:
+        copy.wait()
 
 
 def basis_products(part, parts, basis, tiles):
@@ -172,10 +183,9 @@
 
 
 def first_dots_kernel(
-    basis, power, count, mats_in, dots_out, mats, count_out, held, tiles, sems
+    first, basis, power, count, given, mats_in, dots_out, mats, count_out, held, tiles, sems
 ):
-    half = sems.shape[0]
-    copies = [pltpu.make_async_copy(mats_in.at[s], mats.at[s], sems.at[s]) for s in range(half)]
+    copies = bring(mats_in, mats, first, sems)
     for copy in copies:
         copy.start()
     add_dots(0, basis, [], power, None, dots_out, held)
@@ -189,7 +199,6 @@
     out, source = refs[-2:]
     width = sums.shape[1]
     slots = mats.shape[0]
-    half = slots // 2
     rows = sums.shape[0] - base
     source[...] = jnp.zeros_like(source)
     for i in range(rows):
@@ -224,7 +233,7 @@
             def _():
                 put(first + s, every[:, 2 * width * s : 2 * width * (s + 1)])
 
-    few = half // 2
+    few = 2
 
     @pl.when(live[0, 0] <= few)
     def _():
@@ -240,25 +249,23 @@
         def _():
             put_all(0, slots)
     else:
+        there, wait = ready
 
         @pl.when(live[0, 0] > few)
         def _():
-            put_all(0, half)
-
-        ready()
-
-        @pl.when(live[0, 0] > half)
+            put_all(0, there)
+
+        wait()
+
+        @pl.when(live[0, 0] > there)
         def _():
-            put_all(half, half)
-
-
-def first_flame_kernel(base, live, lines, burners, sums, given, mats_in, order, out, mats, *refs):
-    source, sems = refs
-    half = sems.shape[0]
-    copies = [
-        pltpu.make_async_copy(mats_in.at[half + s], mats.at[half + s], sems.at[s])
-        for s in range(half)
-    ]
+            put_all(there, slots - there)
+
+
+def first_flame_kernel(
+    base, first, live, lines, burners, sums, given, mats_in, order, out, mats, source, sems
+):
+    copies = bring(mats_in, mats, first, sems)
     for copy in copies:
         copy.start()
 
@@ -266,7 +273,7 @@
         for copy in copies:
             copy.wait()
 
-    flame_kernel(base, live, lines, burners, sums, mats, order, out, source, ready=ready)
+    flame_kernel(base, live, lines, burners, sums, mats, order, out, source, ready=(first, ready))
 
 
 def step_kernel(
@@ -621,17 +628,21 @@
         shape(tall, width),
         shape(tall, width),
     ]
-    power, azim_x, azim_y, dom_x, dom_y, basis = call(
+    (mats_in,) = held_in_hbm(mats)
+    blocks = jax.ShapeDtypeStruct(mats.shape, mats.dtype)
+    second, third = max(2, slots // 4), max(2, slots * 5 // 8)
+    power, azim_x, azim_y, dom_x, dom_y, basis, mats = call(
         functools.partial(start_kernel, rows, depth),
-        [*fields, shape(count, 2, lines, width)],
-        in_hbm(4),
-        held_in_hbm(coefficients, reference_part, reference_line, basis),
+        [*fields, shape(count, 2, lines, width), blocks],
+        in_hbm(5),
+        [*held_in_hbm(coefficients, reference_part, reference_line, basis), mats_in],
         [
             SMEM(coefficients.shape, jnp.float32),
             SMEM(reference_part.shape, jnp.int32),
             SMEM(reference_line.shape, jnp.int32),
             pltpu.SemaphoreType.DMA((3,)),
             pltpu.SemaphoreType.DMA((4,)),
+            pltpu.SemaphoreType.DMA((second,)),
         ],
         cost=4,
     )
@@ -651,18 +662,16 @@
             pairs = [(i, i ^ reach) for i in range(n_dom) if i < i ^ reach]
             sums = sums + exchange(sums, "dom", pairs)
             reach *= 2
-        half = slots // 2
-        blocks = jax.ShapeDtypeStruct(mats.shape, mats.dtype)
         source = VMEM((16, width), jnp.bfloat16)
         if step == 0:
-            (mats_in,) = held_in_hbm(mats)
             dots, mats, live = call(
-                first_dots_kernel,
+                functools.partial(first_dots_kernel, second),
                 [shape(4, 128), blocks, jax.ShapeDtypeStruct((8, 128), jnp.int32)],
-                vmem(3) + in_hbm(1),
-                (basis, power, flame_count.reshape(1, 1), mats_in),
-                [held, tiles, pltpu.SemaphoreType.DMA((half,))],
+                vmem(4) + in_hbm(1),
+                (basis, power, flame_count.reshape(1, 1), mats, mats_in),
+                [held, tiles, pltpu.SemaphoreType.DMA((third - second,))],
                 cost=2,
+                aliases={3: 1},
             )
         else:
             given = (basis, *powers, dots)
@@ -676,11 +685,11 @@
         numbers = (live, flame_line, flame_burner)
         if step == 0:
             flame, mats = call(
-                functools.partial(first_flame_kernel, base),
+                functools.partial(first_flame_kernel, base, third),
                 [shape(2, lines, width), blocks],
                 smem(3) + vmem(2) + in_hbm(1) + vmem(1),
                 (*numbers, sums, mats, mats_in, dots),
-                [source, pltpu.SemaphoreType.DMA((half,))],
+                [source, pltpu.SemaphoreType.DMA((slots - third,))],
                 cost=3,
                 aliases={4: 1},
             )

time: 60 us -> 59.9 us (level)
  waiting for transfers between devices: 6.29 us -> 5.59 us
    ppermute x16, waiting for transfers between devices: 6.29 us -> 5.59 us  [exchange(): return lax.ppermute(values, axis, both)]
  transfers between devices with their start and end apart: 16 -> 16, of which waited for: 5 -> 4; matrix products, arithmetic and copies ran while one was open for 1% -> 1% of each run, Pallas kernels for 21% -> 20%
where the time goes in v5:
time: 59.9 us; the launch traced here: 59.7 us
  starting transfers between devices  20.6 us (34%)
  Pallas kernels  19.2 us (32%)
  blocking collectives  12.3 us (21%)
  waiting for transfers between devices  5.59 us (9%)
  between operations  1.57 us (3%)
    ppermute x16, starting transfers between devices, exchange(): return lax.ppermute(values, axis, both)  20.6 us
    pallas_call x14, Pallas kernels, call(): pl.pallas_call(kernel, out_shape=outs, in_specs=specs, out_specs=out_spec...  19.2 us
    all_to_all x1, blocking collectives, on_device(): gram = jnp.sum(lax.all_to_all(spread, ('azim', 'dom'), 0, 0), axis=0)  12.3 us
    ppermute x16, waiting for transfers between devices, exchange(): return lax.ppermute(values, axis, both)  5.59 us
  transfers between devices with their start and end apart: 16, of which 4 were waited for; matrix products, arithmetic and copies ran while one was open for 1% of the time, Pallas kernels for 20%

profile of v5, /device:TPU:0, one launch (start us, length us, event | category | flops | bytes accessed | tf_op | source)
XLA Modules:
  0.0 59.7 jit_solution(5709252032077741916)
XLA Ops:
  0.6 2.3 %shard_map.113 = (f32[2,32,512]{2,1,0:T(8,128)S(1)}, f32[2,16,512]{2,1,0:T(8,128)S(1)}, f32[2,16,512]{2,1,0:T(8,128)S(1)}, f32[8,512]{1,0:T(8,128)S(1)}, f32[8,5...) custom-call(f32[2,16]{1,0:T(2,128)} %coef_in.1, s32[2]{0:T(128)} %ref_part.5, ...), custom_call_target="tpu_custom_call" | custom-call | bytes 8000000 | tf_op jit(solution)/shard_map/pallas_call | solution.py:39
  2.9 0.6 collective-permute-start
  3.5 2.6 %collective-permute-start.2 = (f32[2,16,512]{2,1,0:T(8,128)S(1)}, f32[2,16,512]{2,1,0:T(8,128)S(1)}, u32[]{:S(2)}, u32[]{:S(2)}) collective-permute-start(f32[2,16,512]{2,1,0:T(8,128)S(1)} %get-tuple-element.40), channel_id=1, source_target_pairs={{0,4},{8,12},{16,20},{24,28},{4,0},{12,8},{20,16},{28,24},{1,5},{9... | collective-permute-start | bytes 196616 | tf_op jit(solution)/shard_map/ppermute | solution.py:614
  6.0 3.5 %collective-permute-start.3 = (f32[2,16,512]{2,1,0:T(8,128)S(1)}, f32[2,16,512]{2,1,0:T(8,128)S(1)}, u32[]{:S(2)}, u32[]{:S(2)}) collective-permute-start(f32[2,16,512]{2,1,0:T(8,128)S(1)} %get-tuple-element.41), channel_id=1, source_target_pairs={{4,8},{12,16},{20,24},{28,0},{8,4},{16,12},{24,20},{0,28},{5,9},{1... | collective-permute-start | bytes 196616 | tf_op jit(solution)/shard_map/ppermute | solution.py:614
  9.6 0.1 add_select_fusion.3
  9.7 1.0 %collective-permute-start.1 = (f32[8,512]{1,0:T(8,128)S(1)}, f32[8,512]{1,0:T(8,128)S(1)}, u32[]{:S(2)}, u32[]{:S(2)}) collective-permute-start(f32[8,512]{1,0:T(8,128)S(1)} %add_select_fusion.3), channel_id=1, source_target_pairs={{1,2},{3,0},{2,1},{0,3},{5,6},{7,4},{6,5},{4,7},{9,10},{11,8},{10,... | collective-permute-start | bytes 49160 | tf_op jit(solution)/shard_map/ppermute | solution.py:614
  11.3 0.0 copy-start.1
  11.3 0.0 copy-start.2
  11.3 1.9 %shard_map.114 = (f32[4,128]{1,0:T(4,128)S(1)}, bf16[8,1024,512]{2,1,0:T(8,128)(2,1)S(1)}, s32[8,128]{1,0:T(8,128)S(1)}) custom-call(f32[16,2,32,512]{3,2,1,0:T(8,128)S(1)} %get-tuple-element.32.basis, f32[2,32,512]{2,1,0:T(8,128)S(1)} %get-tuple-element.31.power.old.refs_0_.refs_7_, s32[1,1]{1,0:T(1,128)} %bitcast.5.count, ...), custom_call_target="tpu_custom_call", output_to_operand_aliasing={{1}: (3, {})} | custom-call | bytes 4000000 | tf_op jit(solution)/shard_map/pallas_call | solution.py:39
  13.3 0.0 copy-start
  13.3 0.0 copy-start.3
  13.3 0.0 copy-start.4
  13.3 2.5 %shard_map.115 = (f32[2,32,512]{2,1,0:T(8,128)S(1)}, bf16[8,1024,512]{2,1,0:T(8,128)(2,1)S(1)}) custom-call(s32[8,128]{1,0:T(8,128)S(1)} %get-tuple-element.34.live, s32[8]{0:T(128)S(1)} %copy-done.1, s32[8]{0:T(128)S(1)} %copy-done.2, f32[8,512]{1,0:T(8,128)S(1)} %add.25.sums, ...), custom_call_target="tpu_custom_call", output_to_operand_aliasing={{1}: (4, {})} | custom-call | bytes 6000000 | tf_op jit(solution)/shard_map/pallas_call | solution.py:39
  15.8 0.0 collective-permute-done.3.from_ay
  15.8 0.7 %shard_map.116 = (f32[2,32,512]{2,1,0:T(8,128)S(1)}, f32[2,16,512]{2,1,0:T(8,128)S(1)}, f32[2,16,512]{2,1,0:T(8,128)S(1)}, f32[8,512]{1,0:T(8,128)S(1)}, f32[8,512]{1,0:T(8,128)S(1)}) custom-call(s32[2]{0:T(128)S(1)} %copy-done.3, s32[2]{0:T(128)S(1)} %copy-done.4, f32[2,32,512]{2,1,0:T(8,128)S(1)} %get-tuple-element.31.power.old.refs_0_.refs_7_, ...), custom_call_target="tpu_custom_call" | custom-call | bytes 2000000 | tf_op jit(solution)/shard_map/pallas_call | solution.py:39
  16.6 1.7 %collective-permute-start.4 = (f32[8,512]{1,0:T(8,128)S(1)}, f32[8,512]{1,0:T(8,128)S(1)}, u32[]{:S(2)}, u32[]{:S(2)}) collective-permute-start(f32[8,512]{1,0:T(8,128)S(1)} %get-tuple-element.43), channel_id=1, source_target_pairs={{0,1},{2,3},{1,0},{3,2},{4,5},{6,7},{5,4},{7,6},{8,9},{10,11},{9,8... | collective-permute-start | bytes 49160 | tf_op jit(solution)/shard_map/ppermute | solution.py:614
  18.3 0.9 %collective-permute-start.7 = (f32[2,16,512]{2,1,0:T(8,128)S(1)}, f32[2,16,512]{2,1,0:T(8,128)S(1)}, u32[]{:S(2)}, u32[]{:S(2)}) collective-permute-start(f32[2,16,512]{2,1,0:T(8,128)S(1)} %get-tuple-element.47), channel_id=1, source_target_pairs={{4,8},{12,16},{20,24},{28,0},{8,4},{16,12},{24,20},{0,28},{5,9},{1... | collective-permute-start | bytes 196616 | tf_op jit(solution)/shard_map/ppermute | solution.py:614
  19.2 0.0 collective-permute-done.4.from_dx
  19.2 0.1 add_select_fusion.2
  19.3 1.1 %collective-permute-start.5 = (f32[8,512]{1,0:T(8,128)S(1)}, f32[8,512]{1,0:T(8,128)S(1)}, u32[]{:S(2)}, u32[]{:S(2)}) collective-permute-start(f32[8,512]{1,0:T(8,128)S(1)} %add_select_fusion.2), channel_id=1, source_target_pairs={{1,2},{3,0},{2,1},{0,3},{5,6},{7,4},{6,5},{4,7},{9,10},{11,8},{10,... | collective-permute-start | bytes 49160 | tf_op jit(solution)/shard_map/ppermute | solution.py:614
  20.4 1.5 %shard_map.117.refs_0_.refs_3_ = f32[4,128]{1,0:T(4,128)S(1)} custom-call(f32[16,2,32,512]{3,2,1,0:T(8,128)S(1)} %get-tuple-element.32.basis, f32[2,32,512]{2,1,0:T(8,128)S(1)} %get-tuple-element.31.power.old.refs_0_.refs_7_, f32[2,32,512]{2,1,0:T(8,128)S(1)} %get-tuple-element.42.refs_1_.old.refs_8_, f32[4,128]{1,0:T(4,128)S(1)} %get-tuple-element.38.order.refs_2_), custom_call_target="tpu_custom_call" | custom-call | bytes 2000000 | tf_op jit(solution)/shard_map/pallas_call | solution.py:39
  21.9 0.5 collective-permute-done.5.from_dy
  22.4 1.0 %shard_map.118.flame = f32[2,32,512]{2,1,0:T(8,128)S(1)} custom-call(s32[8,128]{1,0:T(8,128)S(1)} %get-tuple-element.34.live, s32[8]{0:T(128)S(1)} %copy-done.1, s32[8]{0:T(128)S(1)} %copy-done.2, f32[8,512]{1,0:T(8,128)S(1)} %add.27.sums, bf16[8,1024,512]{2,1,0:T(8,128)(2,1)S(1)} %get-tuple-element.45.mats, f32[4,128]{1,0:T(4,128)S(1)} %shard_map.117.refs_0_.refs_3_), custom_call_target="tpu_custom_call" | custom-call | bytes 6000000 | tf_op jit(solution)/shard_map/pallas_call | solution.py:39
  23.5 0.0 collective-permute-done.6.from_ax
  23.5 1.7 %collective-permute-done.7.from_ay = f32[2,16,512]{2,1,0:T(8,128)S(1)} collective-permute-done((f32[2,16,512]{2,1,0:T(8,128)S(1)}, f32[2,16,512]{2,1,0:T(8,128)S(1)}, u32[]{:S(2)}, u32[]{:S(2)}) %collective-permute-start.7) | collective-permute-done | bytes 65568 | tf_op jit(solution)/shard_map/ppermute | solution.py:614
  25.2 0.7 %shard_map.119 = (f32[2,32,512]{2,1,0:T(8,128)S(1)}, f32[2,16,512]{2,1,0:T(8,128)S(1)}, f32[2,16,512]{2,1,0:T(8,128)S(1)}, f32[8,512]{1,0:T(8,128)S(1)}, f32[8,512]{1,0:T(8,128)S(1)}) custom-call(s32[2]{0:T(128)S(1)} %copy-done.3, s32[2]{0:T(128)S(1)} %copy-done.4, f32[2,32,512]{2,1,0:T(8,128)S(1)} %get-tuple-element.42.refs_1_.old.refs_8_, ...), custom_call_target="tpu_custom_call" | custom-call | bytes 2000000 | tf_op jit(solution)/shard_map/pallas_call | solution.py:39
  25.9 0.7 %collective-permute-start.8 = (f32[8,512]{1,0:T(8,128)S(1)}, f32[8,512]{1,0:T(8,128)S(1)}, u32[]{:S(2)}, u32[]{:S(2)}) collective-permute-start(f32[8,512]{1,0:T(8,128)S(1)} %get-tuple-element.49), channel_id=1, source_target_pairs={{0,1},{2,3},{1,0},{3,2},{4,5},{6,7},{5,4},{7,6},{8,9},{10,11},{9,8... | collective-permute-start | bytes 49160 | tf_op jit(solution)/shard_map/ppermute | solution.py:614
  26.6 1.4 %collective-permute-start.10 = (f32[2,16,512]{2,1,0:T(8,128)S(1)}, f32[2,16,512]{2,1,0:T(8,128)S(1)}, u32[]{:S(2)}, u32[]{:S(2)}) collective-permute-start(f32[2,16,512]{2,1,0:T(8,128)S(1)} %get-tuple-element.51), channel_id=1, source_target_pairs={{0,4},{8,12},{16,20},{24,28},{4,0},{12,8},{20,16},{28,24},{1,5},{9... | collective-permute-start | bytes 196616 | tf_op jit(solution)/shard_map/ppermute | solution.py:614
  28.1 0.3 collective-permute-start.11
  28.3 0.0 collective-permute-done.8.from_dx
  28.3 0.1 add_select_fusion.1
  28.4 2.4 %collective-permute-start.9 = (f32[8,512]{1,0:T(8,128)S(1)}, f32[8,512]{1,0:T(8,128)S(1)}, u32[]{:S(2)}, u32[]{:S(2)}) collective-permute-start(f32[8,512]{1,0:T(8,128)S(1)} %add_select_fusion.1), channel_id=1, source_target_pairs={{1,2},{3,0},{2,1},{0,3},{5,6},{7,4},{6,5},{4,7},{9,10},{11,8},{10,... | collective-permute-start | bytes 49160 | tf_op jit(solution)/shard_map/ppermute | solution.py:614
  30.8 1.5 %shard_map.120.refs_0_.refs_4_ = f32[4,128]{1,0:T(4,128)S(1)} custom-call(f32[16,2,32,512]{3,2,1,0:T(8,128)S(1)} %get-tuple-element.32.basis, f32[2,32,512]{2,1,0:T(8,128)S(1)} %get-tuple-element.31.power.old.refs_0_.refs_7_, f32[2,32,512]{2,1,0:T(8,128)S(1)} %get-tuple-element.42.refs_1_.old.refs_8_, ...), custom_call_target="tpu_custom_call" | custom-call | bytes 2000000 | tf_op jit(solution)/shard_map/pallas_call | solution.py:39
  32.3 1.0 %shard_map.121.flame = f32[2,32,512]{2,1,0:T(8,128)S(1)} custom-call(s32[8,128]{1,0:T(8,128)S(1)} %get-tuple-element.34.live, s32[8]{0:T(128)S(1)} %copy-done.1, s32[8]{0:T(128)S(1)} %copy-done.2, f32[8,512]{1,0:T(8,128)S(1)} %add.29.sums, bf16[8,1024,512]{2,1,0:T(8,128)(2,1)S(1)} %get-tuple-element.45.mats, f32[4,128]{1,0:T(4,128)S(1)} %shard_map.120.refs_0_.refs_4_), custom_call_target="tpu_custom_call" | custom-call | bytes 6000000 | tf_op jit(solution)/shard_map/pallas_call | solution.py:39
  33.4 0.0 copy-start.5
  33.4 1.6 %collective-permute-done.11.from_ay = f32[2,16,512]{2,1,0:T(8,128)S(1)} collective-permute-done((f32[2,16,512]{2,1,0:T(8,128)S(1)}, f32[2,16,512]{2,1,0:T(8,128)S(1)}, u32[]{:S(2)}, u32[]{:S(2)}) %collective-permute-start.11) | collective-permute-done | bytes 65568 | tf_op jit(solution)/shard_map/ppermute | solution.py:614
  35.0 0.7 %shard_map.122 = (f32[2,32,512]{2,1,0:T(8,128)S(1)}, f32[2,16,512]{2,1,0:T(8,128)S(1)}, f32[2,16,512]{2,1,0:T(8,128)S(1)}, f32[8,512]{1,0:T(8,128)S(1)}, f32[8,512]{1,0:T(8,128)S(1)}) custom-call(s32[2]{0:T(128)S(1)} %copy-done.3, s32[2]{0:T(128)S(1)} %copy-done.4, f32[2,32,512]{2,1,0:T(8,128)S(1)} %get-tuple-element.48.refs_2_.old.refs_9_, ...), custom_call_target="tpu_custom_call" | custom-call | bytes 2000000 | tf_op jit(solution)/shard_map/pallas_call | solution.py:39
  35.7 1.2 %collective-permute-start.12 = (f32[8,512]{1,0:T(8,128)S(1)}, f32[8,512]{1,0:T(8,128)S(1)}, u32[]{:S(2)}, u32[]{:S(2)}) collective-permute-start(f32[8,512]{1,0:T(8,128)S(1)} %get-tuple-element.54), channel_id=1, source_target_pairs={{0,1},{2,3},{1,0},{3,2},{4,5},{6,7},{5,4},{7,6},{8,9},{10,11},{9,8... | collective-permute-start | bytes 49160 | tf_op jit(solution)/shard_map/ppermute | solution.py:614
  36.9 0.7 %collective-permute-start.14 = (f32[2,16,512]{2,1,0:T(8,128)S(1)}, f32[2,16,512]{2,1,0:T(8,128)S(1)}, u32[]{:S(2)}, u32[]{:S(2)}) collective-permute-start(f32[2,16,512]{2,1,0:T(8,128)S(1)} %get-tuple-element.56), channel_id=1, source_target_pairs={{0,4},{8,12},{16,20},{24,28},{4,0},{12,8},{20,16},{28,24},{1,5},{9... | collective-permute-start | bytes 196616 | tf_op jit(solution)/shard_map/ppermute | solution.py:614
  37.6 0.5 collective-permute-start.15
  38.1 0.1 add_select_fusion
  38.2 2.0 %collective-permute-start.13 = (f32[8,512]{1,0:T(8,128)S(1)}, f32[8,512]{1,0:T(8,128)S(1)}, u32[]{:S(2)}, u32[]{:S(2)}) collective-permute-start(f32[8,512]{1,0:T(8,128)S(1)} %add_select_fusion), channel_id=1, source_target_pairs={{1,2},{3,0},{2,1},{0,3},{5,6},{7,4},{6,5},{4,7},{9,10},{11,8},{10,... | collective-permute-start | bytes 49160 | tf_op jit(solution)/shard_map/ppermute | solution.py:614
  40.2 1.6 %shard_map.123.refs_0_.refs_11_ = f32[4,128]{1,0:T(4,128)S(1)} custom-call(f32[16,2,32,512]{3,2,1,0:T(8,128)S(1)} %get-tuple-element.32.basis, f32[2,32,512]{2,1,0:T(8,128)S(1)} %get-tuple-element.31.power.old.refs_0_.refs_7_, f32[2,32,512]{2,1,0:T(8,128)S(1)} %get-tuple-element.42.refs_1_.old.refs_8_, ...), custom_call_target="tpu_custom_call" | custom-call | bytes 2000000 | tf_op jit(solution)/shard_map/pallas_call | solution.py:39
  41.9 1.0 %shard_map.124.refs_1_ = f32[2,32,512]{2,1,0:T(8,128)S(1)} custom-call(s32[8,128]{1,0:T(8,128)S(1)} %get-tuple-element.34.live, s32[8]{0:T(128)S(1)} %copy-done.1, s32[8]{0:T(128)S(1)} %copy-done.2, f32[8,512]{1,0:T(8,128)S(1)} %add.31.sums, bf16[8,1024,512]{2,1,0:T(8,128)(2,1)S(1)} %get-tuple-element.45.mats, f32[4,128]{1,0:T(4,128)S(1)} %shard_map.123.refs_0_.refs_11_), custom_call_target="tpu_custom_call" | custom-call | bytes 6000000 | tf_op jit(solution)/shard_map/pallas_call | solution.py:39
  42.9 1.7 %collective-permute-done.15.refs_4_ = f32[2,16,512]{2,1,0:T(8,128)S(1)} collective-permute-done((f32[2,16,512]{2,1,0:T(8,128)S(1)}, f32[2,16,512]{2,1,0:T(8,128)S(1)}, u32[]{:S(2)}, u32[]{:S(2)}) %collective-permute-start.15) | collective-permute-done | bytes 65568 | tf_op jit(solution)/shard_map/ppermute | solution.py:614
  44.6 0.5 shard_map.125
  45.1 12.3 %all_to_all.5 = f32[32,4,128]{2,1,0:T(4,128)S(1)} all-to-all(f32[32,4,128]{2,1,0:T(4,128)S(1)} %broadcast_in_dim.2), channel_id=1, replica_groups=mesh['azim'=8,'dom'=4] {'azim','dom'}, dimensions={0} | all-to-all | bytes 131072 | tf_op jit(solution)/shard_map/all_to_all | solution.py:724
  57.4 2.3 %shard_map.126 = (f32[2,32,512]{2,1,0:T(8,128)}, f32[2]{0:T(128)}) custom-call(f32[2]{0:T(128)S(1)} %copy-done.5, f32[4,128]{1,0:T(4,128)S(1)} %reduce_sum.9.gram_s.gram, f32[4,128]{1,0:T(4,128)S(1)} %reduce_sum.9.gram_s.gram, f32[16,2,32,512]{3,2,1,0:T(8,128)S(1)} %get-tuple-element.32.basis, f32[2,32,512]{2,1,0:T(8,128)S(1)} %get-tuple-element.31.power.old.refs_0_.refs_7_, ...), custom_call_target="tpu_custom_call" | custom-call | bytes 2000000 | tf_op jit(solution)/shard_map/pallas_call | solution.py:39
  (22 shorter events, 0.1 us)
Async XLA Ops:
  2.9 6.7 %collective-permute-start = (f32[8,512]{1,0:T(8,128)S(1)}, f32[8,512]{1,0:T(8,128)S(1)}, u32[]{:S(2)}, u32[]{:S(2)}) collective-permute-start(f32[8,512]{1,0:T(8,128)S(1)} %get-tuple-element.35), channel_id=1, source_target_pairs={{0,1},{2,3},{1,0},{3,2},{4,5},{6,7},{5,4},{7,6},{8,9},{10,11},{9,8... | collective-permute-start | bytes 49160 | tf_op jit(solution)/shard_map/ppermute | solution.py:614
  3.5 12.3 %collective-permute-start.2 = (f32[2,16,512]{2,1,0:T(8,128)S(1)}, f32[2,16,512]{2,1,0:T(8,128)S(1)}, u32[]{:S(2)}, u32[]{:S(2)}) collective-permute-start(f32[2,16,512]{2,1,0:T(8,128)S(1)} %get-tuple-element.40), channel_id=1, source_target_pairs={{0,4},{8,12},{16,20},{24,28},{4,0},{12,8},{20,16},{28,24},{1,5},{9... | collective-permute-start | bytes 196616 | tf_op jit(solution)/shard_map/ppermute | solution.py:614
  6.0 9.8 %collective-permute-start.3 = (f32[2,16,512]{2,1,0:T(8,128)S(1)}, f32[2,16,512]{2,1,0:T(8,128)S(1)}, u32[]{:S(2)}, u32[]{:S(2)}) collective-permute-start(f32[2,16,512]{2,1,0:T(8,128)S(1)} %get-tuple-element.41), channel_id=1, source_target_pairs={{4,8},{12,16},{20,24},{28,0},{8,4},{16,12},{24,20},{0,28},{5,9},{1... | collective-permute-start | bytes 196616 | tf_op jit(solution)/shard_map/ppermute | solution.py:614
  9.7 3.5 %collective-permute-start.1 = (f32[8,512]{1,0:T(8,128)S(1)}, f32[8,512]{1,0:T(8,128)S(1)}, u32[]{:S(2)}, u32[]{:S(2)}) collective-permute-start(f32[8,512]{1,0:T(8,128)S(1)} %add_select_fusion.3), channel_id=1, source_target_pairs={{1,2},{3,0},{2,1},{0,3},{5,6},{7,4},{6,5},{4,7},{9,10},{11,8},{10,... | collective-permute-start | bytes 49160 | tf_op jit(solution)/shard_map/ppermute | solution.py:614
  11.3 1.9 %copy-start.1 = (s32[8]{0:T(128)S(1)}, s32[8]{0:T(128)}, u32[]{:S(2)}) copy-start(s32[8]{0:T(128)} %lines.7) | copy-start | bytes 100
  11.3 1.9 %copy-start.2 = (s32[8]{0:T(128)S(1)}, s32[8]{0:T(128)}, u32[]{:S(2)}) copy-start(s32[8]{0:T(128)} %burners.7) | copy-start | bytes 100
  13.3 2.6 %copy-start = (f32[2,16,512]{2,1,0:T(8,128)S(1)}, f32[2,16,512]{2,1,0:T(8,128)}, u32[]{:S(2)}) copy-start(f32[2,16,512]{2,1,0:T(8,128)} %param.13) | copy-start | bytes 196612
  13.3 2.6 %copy-start.3 = (s32[2]{0:T(128)S(1)}, s32[2]{0:T(128)}, u32[]{:S(2)}) copy-start(s32[2]{0:T(128)} %ref_part.5) | copy-start | bytes 28
  13.3 2.6 %copy-start.4 = (s32[2]{0:T(128)S(1)}, s32[2]{0:T(128)}, u32[]{:S(2)}) copy-start(s32[2]{0:T(128)} %ref_line.5) | copy-start | bytes 28
  16.6 2.6 %collective-permute-start.4 = (f32[8,512]{1,0:T(8,128)S(1)}, f32[8,512]{1,0:T(8,128)S(1)}, u32[]{:S(2)}, u32[]{:S(2)}) collective-permute-start(f32[8,512]{1,0:T(8,128)S(1)} %get-tuple-element.43), channel_id=1, source_target_pairs={{0,1},{2,3},{1,0},{3,2},{4,5},{6,7},{5,4},{7,6},{8,9},{10,11},{9,8... | collective-permute-start | bytes 49160 | tf_op jit(solution)/shard_map/ppermute | solution.py:614
  18.3 5.2 %collective-permute-start.6 = (f32[2,16,512]{2,1,0:T(8,128)S(1)}, f32[2,16,512]{2,1,0:T(8,128)S(1)}, u32[]{:S(2)}, u32[]{:S(2)}) collective-permute-start(f32[2,16,512]{2,1,0:T(8,128)S(1)} %get-tuple-element.46), channel_id=1, source_target_pairs={{0,4},{8,12},{16,20},{24,28},{4,0},{12,8},{20,16},{28,24},{1,5},{9... | collective-permute-start | bytes 196616 | tf_op jit(solution)/shard_map/ppermute | solution.py:614
  18.3 7.0 %collective-permute-start.7 = (f32[2,16,512]{2,1,0:T(8,128)S(1)}, f32[2,16,512]{2,1,0:T(8,128)S(1)}, u32[]{:S(2)}, u32[]{:S(2)}) collective-permute-start(f32[2,16,512]{2,1,0:T(8,128)S(1)} %get-tuple-element.47), channel_id=1, source_target_pairs={{4,8},{12,16},{20,24},{28,0},{8,4},{16,12},{24,20},{0,28},{5,9},{1... | collective-permute-start | bytes 196616 | tf_op jit(solution)/shard_map/ppermute | solution.py:614
  19.3 3.2 %collective-permute-start.5 = (f32[8,512]{1,0:T(8,128)S(1)}, f32[8,512]{1,0:T(8,128)S(1)}, u32[]{:S(2)}, u32[]{:S(2)}) collective-permute-start(f32[8,512]{1,0:T(8,128)S(1)} %add_select_fusion.2), channel_id=1, source_target_pairs={{1,2},{3,0},{2,1},{0,3},{5,6},{7,4},{6,5},{4,7},{9,10},{11,8},{10,... | collective-permute-start | bytes 49160 | tf_op jit(solution)/shard_map/ppermute | solution.py:614
  25.9 2.4 %collective-permute-start.8 = (f32[8,512]{1,0:T(8,128)S(1)}, f32[8,512]{1,0:T(8,128)S(1)}, u32[]{:S(2)}, u32[]{:S(2)}) collective-permute-start(f32[8,512]{1,0:T(8,128)S(1)} %get-tuple-element.49), channel_id=1, source_target_pairs={{0,1},{2,3},{1,0},{3,2},{4,5},{6,7},{5,4},{7,6},{8,9},{10,11},{9,8... | collective-permute-start | bytes 49160 | tf_op jit(solution)/shard_map/ppermute | solution.py:614
  26.6 6.8 %collective-permute-start.10 = (f32[2,16,512]{2,1,0:T(8,128)S(1)}, f32[2,16,512]{2,1,0:T(8,128)S(1)}, u32[]{:S(2)}, u32[]{:S(2)}) collective-permute-start(f32[2,16,512]{2,1,0:T(8,128)S(1)} %get-tuple-element.51), channel_id=1, source_target_pairs={{0,4},{8,12},{16,20},{24,28},{4,0},{12,8},{20,16},{28,24},{1,5},{9... | collective-permute-start | bytes 196616 | tf_op jit(solution)/shard_map/ppermute | solution.py:614
  28.1 7.0 %collective-permute-start.11 = (f32[2,16,512]{2,1,0:T(8,128)S(1)}, f32[2,16,512]{2,1,0:T(8,128)S(1)}, u32[]{:S(2)}, u32[]{:S(2)}) collective-permute-start(f32[2,16,512]{2,1,0:T(8,128)S(1)} %get-tuple-element.52), channel_id=1, source_target_pairs={{4,8},{12,16},{20,24},{28,0},{8,4},{16,12},{24,20},{0,28},{5,9},{1... | collective-permute-start | bytes 196616 | tf_op jit(solution)/shard_map/ppermute | solution.py:614
  28.4 3.9 %collective-permute-start.9 = (f32[8,512]{1,0:T(8,128)S(1)}, f32[8,512]{1,0:T(8,128)S(1)}, u32[]{:S(2)}, u32[]{:S(2)}) collective-permute-start(f32[8,512]{1,0:T(8,128)S(1)} %add_select_fusion.1), channel_id=1, source_target_pairs={{1,2},{3,0},{2,1},{0,3},{5,6},{7,4},{6,5},{4,7},{9,10},{11,8},{10,... | collective-permute-start | bytes 49160 | tf_op jit(solution)/shard_map/ppermute | solution.py:614
  33.4 24.0 %copy-start.5 = (f32[2]{0:T(128)S(1)}, f32[2]{0:T(128)}, u32[]{:S(2)}) copy-start(f32[2]{0:T(128)} %shift.1) | copy-start | bytes 28
  35.7 2.4 %collective-permute-start.12 = (f32[8,512]{1,0:T(8,128)S(1)}, f32[8,512]{1,0:T(8,128)S(1)}, u32[]{:S(2)}, u32[]{:S(2)}) collective-permute-start(f32[8,512]{1,0:T(8,128)S(1)} %get-tuple-element.54), channel_id=1, source_target_pairs={{0,1},{2,3},{1,0},{3,2},{4,5},{6,7},{5,4},{7,6},{8,9},{10,11},{9,8... | collective-permute-start | bytes 49160 | tf_op jit(solution)/shard_map/ppermute | solution.py:614
  36.9 6.0 %collective-permute-start.14 = (f32[2,16,512]{2,1,0:T(8,128)S(1)}, f32[2,16,512]{2,1,0:T(8,128)S(1)}, u32[]{:S(2)}, u32[]{:S(2)}) collective-permute-start(f32[2,16,512]{2,1,0:T(8,128)S(1)} %get-tuple-element.56), channel_id=1, source_target_pairs={{0,4},{8,12},{16,20},{24,28},{4,0},{12,8},{20,16},{28,24},{1,5},{9... | collective-permute-start | bytes 196616 | tf_op jit(solution)/shard_map/ppermute | solution.py:614
  37.6 7.0 %collective-permute-start.15 = (f32[2,16,512]{2,1,0:T(8,128)S(1)}, f32[2,16,512]{2,1,0:T(8,128)S(1)}, u32[]{:S(2)}, u32[]{:S(2)}) collective-permute-start(f32[2,16,512]{2,1,0:T(8,128)S(1)} %get-tuple-element.57), channel_id=1, source_target_pairs={{4,8},{12,16},{20,24},{28,0},{8,4},{16,12},{24,20},{0,28},{5,9},{1... | collective-permute-start | bytes 196616 | tf_op jit(solution)/shard_map/ppermute | solution.py:614
  38.2 3.6 %collective-permute-start.13 = (f32[8,512]{1,0:T(8,128)S(1)}, f32[8,512]{1,0:T(8,128)S(1)}, u32[]{:S(2)}, u32[]{:S(2)}) collective-permute-start(f32[8,512]{1,0:T(8,128)S(1)} %add_select_fusion), channel_id=1, source_target_pairs={{1,2},{3,0},{2,1},{0,3},{5,6},{7,4},{6,5},{4,7},{9,10},{11,8},{10,... | collective-permute-start | bytes 49160 | tf_op jit(solution)/shard_map/ppermute | solution.py:614

commit v6 on v5

--- a/solution.py
+++ b/solution.py
@@ -348,7 +348,7 @@
             held[pl.ds(count + i, 1), :] = folded(left_re * im - left_im * re)
             return carry
 
-        lax.fori_loop(0, count, one, 0)
+        lax.fori_loop(0, count, one, 0, unroll=4)
     first = held.shape[0] - 16
     for j, power in enumerate([*powers, current]):
         left_re, left_im = power[0], power[1]
@@ -577,14 +577,14 @@
         return jnp.tile(x[0:1, :], (1, width // 128))
 
     coefs = {k: Cx(wide(v.re), wide(v.im)) for k, v in coefs.items()}
-    for a in range(rows):
-        span = slice(a * depth, (a + 1) * depth)
-        real = jnp.zeros((depth, width), jnp.float32)
-        imag = real
+    for start in range(0, rows * depth, 8):
+        span = slice(start, start + 8)
+        real = imag = None
         for k, v in coefs.items():
             re, im = powers[k][0, span, :], powers[k][1, span, :]
-            real = real + (v.re * re - v.im * im)
-            imag = imag + (v.re * im + v.im * re)
+            one, two = v.re * re - v.im * im, v.re * im + v.im * re
+            real = one if real is None else real + one
+            imag = two if imag is None else imag + two
         for i in range(count):
             v = Cx(wide(column[0, i : i + 1, :]), wide(column[1, i : i + 1, :]))
             re, im = basis[i, 0, span, :], basis[i, 1, span, :]

time: 59.9 us -> 59.8 us (level)
  transfers between devices with their start and end apart: 16 -> 16, of which waited for: 4 -> 5; matrix products, arithmetic and copies ran while one was open for 1% -> 1% of each run, Pallas kernels for 20% -> 19%
where the time goes in v6:
time: 59.8 us; the launch traced here: 59.7 us
  starting transfers between devices  20.6 us (34%)
  Pallas kernels  18.7 us (31%)
  blocking collectives  12.3 us (21%)
  waiting for transfers between devices  6.13 us (10%)
  between operations  1.55 us (3%)
    ppermute x16, starting transfers between devices, exchange(): return lax.ppermute(values, axis, both)  20.6 us
    pallas_call x14, Pallas kernels, call(): pl.pallas_call(kernel, out_shape=outs, in_specs=specs, out_specs=out_spec...  18.7 us
    all_to_all x1, blocking collectives, on_device(): gram = jnp.sum(lax.all_to_all(spread, ('azim', 'dom'), 0, 0), axis=0)  12.3 us
    ppermute x16, waiting for transfers between devices, exchange(): return lax.ppermute(values, axis, both)  6.13 us
  transfers between devices with their start and end apart: 16, of which 5 were waited for; matrix products, arithmetic and copies ran while one was open for 1% of the time, Pallas kernels for 19%

profile of v6, /device:TPU:0, one launch (start us, length us, event | category | flops | bytes accessed | tf_op | source)
XLA Modules:
  0.0 59.7 jit_solution(8101530093407889743)
XLA Ops:
  0.6 2.3 %shard_map.113 = (f32[2,32,512]{2,1,0:T(8,128)S(1)}, f32[2,16,512]{2,1,0:T(8,128)S(1)}, f32[2,16,512]{2,1,0:T(8,128)S(1)}, f32[8,512]{1,0:T(8,128)S(1)}, f32[8,5...) custom-call(f32[2,16]{1,0:T(2,128)} %coef_in.1, s32[2]{0:T(128)} %ref_part.5, ...), custom_call_target="tpu_custom_call" | custom-call | bytes 8000000 | tf_op jit(solution)/shard_map/pallas_call | solution.py:39
  2.9 0.6 collective-permute-start
  3.5 2.6 %collective-permute-start.2 = (f32[2,16,512]{2,1,0:T(8,128)S(1)}, f32[2,16,512]{2,1,0:T(8,128)S(1)}, u32[]{:S(2)}, u32[]{:S(2)}) collective-permute-start(f32[2,16,512]{2,1,0:T(8,128)S(1)} %get-tuple-element.40), channel_id=1, source_target_pairs={{0,4},{8,12},{16,20},{24,28},{4,0},{12,8},{20,16},{28,24},{1,5},{9... | collective-permute-start | bytes 196616 | tf_op jit(solution)/shard_map/ppermute | solution.py:614
  6.0 3.5 %collective-permute-start.3 = (f32[2,16,512]{2,1,0:T(8,128)S(1)}, f32[2,16,512]{2,1,0:T(8,128)S(1)}, u32[]{:S(2)}, u32[]{:S(2)}) collective-permute-start(f32[2,16,512]{2,1,0:T(8,128)S(1)} %get-tuple-element.41), channel_id=1, source_target_pairs={{4,8},{12,16},{20,24},{28,0},{8,4},{16,12},{24,20},{0,28},{5,9},{1... | collective-permute-start | bytes 196616 | tf_op jit(solution)/shard_map/ppermute | solution.py:614
  9.6 0.1 add_select_fusion.3
  9.7 1.0 %collective-permute-start.1 = (f32[8,512]{1,0:T(8,128)S(1)}, f32[8,512]{1,0:T(8,128)S(1)}, u32[]{:S(2)}, u32[]{:S(2)}) collective-permute-start(f32[8,512]{1,0:T(8,128)S(1)} %add_select_fusion.3), channel_id=1, source_target_pairs={{1,2},{3,0},{2,1},{0,3},{5,6},{7,4},{6,5},{4,7},{9,10},{11,8},{10,... | collective-permute-start | bytes 49160 | tf_op jit(solution)/shard_map/ppermute | solution.py:614
  11.3 0.0 copy-start.1
  11.3 0.0 copy-start.2
  11.3 1.9 %shard_map.114 = (f32[4,128]{1,0:T(4,128)S(1)}, bf16[8,1024,512]{2,1,0:T(8,128)(2,1)S(1)}, s32[8,128]{1,0:T(8,128)S(1)}) custom-call(f32[16,2,32,512]{3,2,1,0:T(8,128)S(1)} %get-tuple-element.32.basis, f32[2,32,512]{2,1,0:T(8,128)S(1)} %get-tuple-element.31.power.old.refs_0_.refs_7_, s32[1,1]{1,0:T(1,128)} %bitcast.5.count, ...), custom_call_target="tpu_custom_call", output_to_operand_aliasing={{1}: (3, {})} | custom-call | bytes 4000000 | tf_op jit(solution)/shard_map/pallas_call | solution.py:39
  13.3 0.0 copy-start
  13.3 0.0 copy-start.3
  13.3 0.0 copy-start.4
  13.3 2.5 %shard_map.115 = (f32[2,32,512]{2,1,0:T(8,128)S(1)}, bf16[8,1024,512]{2,1,0:T(8,128)(2,1)S(1)}) custom-call(s32[8,128]{1,0:T(8,128)S(1)} %get-tuple-element.34.live, s32[8]{0:T(128)S(1)} %copy-done.1, s32[8]{0:T(128)S(1)} %copy-done.2, f32[8,512]{1,0:T(8,128)S(1)} %add.25.sums, ...), custom_call_target="tpu_custom_call", output_to_operand_aliasing={{1}: (4, {})} | custom-call | bytes 6000000 | tf_op jit(solution)/shard_map/pallas_call | solution.py:39
  15.8 0.0 collective-permute-done.3.from_ay
  15.8 0.7 %shard_map.116 = (f32[2,32,512]{2,1,0:T(8,128)S(1)}, f32[2,16,512]{2,1,0:T(8,128)S(1)}, f32[2,16,512]{2,1,0:T(8,128)S(1)}, f32[8,512]{1,0:T(8,128)S(1)}, f32[8,512]{1,0:T(8,128)S(1)}) custom-call(s32[2]{0:T(128)S(1)} %copy-done.3, s32[2]{0:T(128)S(1)} %copy-done.4, f32[2,32,512]{2,1,0:T(8,128)S(1)} %get-tuple-element.31.power.old.refs_0_.refs_7_, ...), custom_call_target="tpu_custom_call" | custom-call | bytes 2000000 | tf_op jit(solution)/shard_map/pallas_call | solution.py:39
  16.6 1.7 %collective-permute-start.4 = (f32[8,512]{1,0:T(8,128)S(1)}, f32[8,512]{1,0:T(8,128)S(1)}, u32[]{:S(2)}, u32[]{:S(2)}) collective-permute-start(f32[8,512]{1,0:T(8,128)S(1)} %get-tuple-element.43), channel_id=1, source_target_pairs={{0,1},{2,3},{1,0},{3,2},{4,5},{6,7},{5,4},{7,6},{8,9},{10,11},{9,8... | collective-permute-start | bytes 49160 | tf_op jit(solution)/shard_map/ppermute | solution.py:614
  18.3 0.9 %collective-permute-start.7 = (f32[2,16,512]{2,1,0:T(8,128)S(1)}, f32[2,16,512]{2,1,0:T(8,128)S(1)}, u32[]{:S(2)}, u32[]{:S(2)}) collective-permute-start(f32[2,16,512]{2,1,0:T(8,128)S(1)} %get-tuple-element.47), channel_id=1, source_target_pairs={{4,8},{12,16},{20,24},{28,0},{8,4},{16,12},{24,20},{0,28},{5,9},{1... | collective-permute-start | bytes 196616 | tf_op jit(solution)/shard_map/ppermute | solution.py:614
  19.2 0.0 collective-permute-done.4.from_dx
  19.2 0.1 add_select_fusion.2
  19.3 1.1 %collective-permute-start.5 = (f32[8,512]{1,0:T(8,128)S(1)}, f32[8,512]{1,0:T(8,128)S(1)}, u32[]{:S(2)}, u32[]{:S(2)}) collective-permute-start(f32[8,512]{1,0:T(8,128)S(1)} %add_select_fusion.2), channel_id=1, source_target_pairs={{1,2},{3,0},{2,1},{0,3},{5,6},{7,4},{6,5},{4,7},{9,10},{11,8},{10,... | collective-permute-start | bytes 49160 | tf_op jit(solution)/shard_map/ppermute | solution.py:614
  20.4 1.4 %shard_map.117.refs_0_.refs_3_ = f32[4,128]{1,0:T(4,128)S(1)} custom-call(f32[16,2,32,512]{3,2,1,0:T(8,128)S(1)} %get-tuple-element.32.basis, f32[2,32,512]{2,1,0:T(8,128)S(1)} %get-tuple-element.31.power.old.refs_0_.refs_7_, f32[2,32,512]{2,1,0:T(8,128)S(1)} %get-tuple-element.42.refs_1_.old.refs_8_, f32[4,128]{1,0:T(4,128)S(1)} %get-tuple-element.38.order.refs_2_), custom_call_target="tpu_custom_call" | custom-call | bytes 2000000 | tf_op jit(solution)/shard_map/pallas_call | solution.py:39
  21.7 0.7 %collective-permute-done.5.from_dy = f32[8,512]{1,0:T(8,128)S(1)} collective-permute-done((f32[8,512]{1,0:T(8,128)S(1)}, f32[8,512]{1,0:T(8,128)S(1)}, u32[]{:S(2)}, u32[]{:S(2)}) %collective-permute-start.5) | collective-permute-done | bytes 16416 | tf_op jit(solution)/shard_map/ppermute | solution.py:614
  22.4 1.0 %shard_map.118.flame = f32[2,32,512]{2,1,0:T(8,128)S(1)} custom-call(s32[8,128]{1,0:T(8,128)S(1)} %get-tuple-element.34.live, s32[8]{0:T(128)S(1)} %copy-done.1, s32[8]{0:T(128)S(1)} %copy-done.2, f32[8,512]{1,0:T(8,128)S(1)} %add.27.sums, bf16[8,1024,512]{2,1,0:T(8,128)(2,1)S(1)} %get-tuple-element.45.mats, f32[4,128]{1,0:T(4,128)S(1)} %shard_map.117.refs_0_.refs_3_), custom_call_target="tpu_custom_call" | custom-call | bytes 6000000 | tf_op jit(solution)/shard_map/pallas_call | solution.py:39
  23.5 1.7 %collective-permute-done.7.from_ay = f32[2,16,512]{2,1,0:T(8,128)S(1)} collective-permute-done((f32[2,16,512]{2,1,0:T(8,128)S(1)}, f32[2,16,512]{2,1,0:T(8,128)S(1)}, u32[]{:S(2)}, u32[]{:S(2)}) %collective-permute-start.7) | collective-permute-done | bytes 65568 | tf_op jit(solution)/shard_map/ppermute | solution.py:614
  25.2 0.7 %shard_map.119 = (f32[2,32,512]{2,1,0:T(8,128)S(1)}, f32[2,16,512]{2,1,0:T(8,128)S(1)}, f32[2,16,512]{2,1,0:T(8,128)S(1)}, f32[8,512]{1,0:T(8,128)S(1)}, f32[8,512]{1,0:T(8,128)S(1)}) custom-call(s32[2]{0:T(128)S(1)} %copy-done.3, s32[2]{0:T(128)S(1)} %copy-done.4, f32[2,32,512]{2,1,0:T(8,128)S(1)} %get-tuple-element.42.refs_1_.old.refs_8_, ...), custom_call_target="tpu_custom_call" | custom-call | bytes 2000000 | tf_op jit(solution)/shard_map/pallas_call | solution.py:39
  25.9 0.7 %collective-permute-start.8 = (f32[8,512]{1,0:T(8,128)S(1)}, f32[8,512]{1,0:T(8,128)S(1)}, u32[]{:S(2)}, u32[]{:S(2)}) collective-permute-start(f32[8,512]{1,0:T(8,128)S(1)} %get-tuple-element.49), channel_id=1, source_target_pairs={{0,1},{2,3},{1,0},{3,2},{4,5},{6,7},{5,4},{7,6},{8,9},{10,11},{9,8... | collective-permute-start | bytes 49160 | tf_op jit(solution)/shard_map/ppermute | solution.py:614
  26.6 1.4 %collective-permute-start.10 = (f32[2,16,512]{2,1,0:T(8,128)S(1)}, f32[2,16,512]{2,1,0:T(8,128)S(1)}, u32[]{:S(2)}, u32[]{:S(2)}) collective-permute-start(f32[2,16,512]{2,1,0:T(8,128)S(1)} %get-tuple-element.51), channel_id=1, source_target_pairs={{0,4},{8,12},{16,20},{24,28},{4,0},{12,8},{20,16},{28,24},{1,5},{9... | collective-permute-start | bytes 196616 | tf_op jit(solution)/shard_map/ppermute | solution.py:614
  28.1 0.3 collective-permute-start.11
  28.3 0.1 add_select_fusion.1
  28.4 2.4 %collective-permute-start.9 = (f32[8,512]{1,0:T(8,128)S(1)}, f32[8,512]{1,0:T(8,128)S(1)}, u32[]{:S(2)}, u32[]{:S(2)}) collective-permute-start(f32[8,512]{1,0:T(8,128)S(1)} %add_select_fusion.1), channel_id=1, source_target_pairs={{1,2},{3,0},{2,1},{0,3},{5,6},{7,4},{6,5},{4,7},{9,10},{11,8},{10,... | collective-permute-start | bytes 49160 | tf_op jit(solution)/shard_map/ppermute | solution.py:614
  30.8 1.3 %shard_map.120.refs_0_.refs_4_ = f32[4,128]{1,0:T(4,128)S(1)} custom-call(f32[16,2,32,512]{3,2,1,0:T(8,128)S(1)} %get-tuple-element.32.basis, f32[2,32,512]{2,1,0:T(8,128)S(1)} %get-tuple-element.31.power.old.refs_0_.refs_7_, f32[2,32,512]{2,1,0:T(8,128)S(1)} %get-tuple-element.42.refs_1_.old.refs_8_, ...), custom_call_target="tpu_custom_call" | custom-call | bytes 2000000 | tf_op jit(solution)/shard_map/pallas_call | solution.py:39
  32.1 0.1 collective-permute-done.9.from_dy
  32.3 1.0 %shard_map.121.flame = f32[2,32,512]{2,1,0:T(8,128)S(1)} custom-call(s32[8,128]{1,0:T(8,128)S(1)} %get-tuple-element.34.live, s32[8]{0:T(128)S(1)} %copy-done.1, s32[8]{0:T(128)S(1)} %copy-done.2, f32[8,512]{1,0:T(8,128)S(1)} %add.29.sums, bf16[8,1024,512]{2,1,0:T(8,128)(2,1)S(1)} %get-tuple-element.45.mats, f32[4,128]{1,0:T(4,128)S(1)} %shard_map.120.refs_0_.refs_4_), custom_call_target="tpu_custom_call" | custom-call | bytes 6000000 | tf_op jit(solution)/shard_map/pallas_call | solution.py:39
  33.3 0.0 copy-start.5
  33.3 1.7 %collective-permute-done.11.from_ay = f32[2,16,512]{2,1,0:T(8,128)S(1)} collective-permute-done((f32[2,16,512]{2,1,0:T(8,128)S(1)}, f32[2,16,512]{2,1,0:T(8,128)S(1)}, u32[]{:S(2)}, u32[]{:S(2)}) %collective-permute-start.11) | collective-permute-done | bytes 65568 | tf_op jit(solution)/shard_map/ppermute | solution.py:614
  35.0 0.7 %shard_map.122 = (f32[2,32,512]{2,1,0:T(8,128)S(1)}, f32[2,16,512]{2,1,0:T(8,128)S(1)}, f32[2,16,512]{2,1,0:T(8,128)S(1)}, f32[8,512]{1,0:T(8,128)S(1)}, f32[8,512]{1,0:T(8,128)S(1)}) custom-call(s32[2]{0:T(128)S(1)} %copy-done.3, s32[2]{0:T(128)S(1)} %copy-done.4, f32[2,32,512]{2,1,0:T(8,128)S(1)} %get-tuple-element.48.refs_2_.old.refs_9_, ...), custom_call_target="tpu_custom_call" | custom-call | bytes 2000000 | tf_op jit(solution)/shard_map/pallas_call | solution.py:39
  35.7 1.1 %collective-permute-start.12 = (f32[8,512]{1,0:T(8,128)S(1)}, f32[8,512]{1,0:T(8,128)S(1)}, u32[]{:S(2)}, u32[]{:S(2)}) collective-permute-start(f32[8,512]{1,0:T(8,128)S(1)} %get-tuple-element.54), channel_id=1, source_target_pairs={{0,1},{2,3},{1,0},{3,2},{4,5},{6,7},{5,4},{7,6},{8,9},{10,11},{9,8... | collective-permute-start | bytes 49160 | tf_op jit(solution)/shard_map/ppermute | solution.py:614
  36.8 0.8 %collective-permute-start.14 = (f32[2,16,512]{2,1,0:T(8,128)S(1)}, f32[2,16,512]{2,1,0:T(8,128)S(1)}, u32[]{:S(2)}, u32[]{:S(2)}) collective-permute-start(f32[2,16,512]{2,1,0:T(8,128)S(1)} %get-tuple-element.56), channel_id=1, source_target_pairs={{0,4},{8,12},{16,20},{24,28},{4,0},{12,8},{20,16},{28,24},{1,5},{9... | collective-permute-start | bytes 196616 | tf_op jit(solution)/shard_map/ppermute | solution.py:614
  37.6 0.5 collective-permute-start.15
  38.1 0.1 add_select_fusion
  38.2 2.0 %collective-permute-start.13 = (f32[8,512]{1,0:T(8,128)S(1)}, f32[8,512]{1,0:T(8,128)S(1)}, u32[]{:S(2)}, u32[]{:S(2)}) collective-permute-start(f32[8,512]{1,0:T(8,128)S(1)} %add_select_fusion), channel_id=1, source_target_pairs={{1,2},{3,0},{2,1},{0,3},{5,6},{7,4},{6,5},{4,7},{9,10},{11,8},{10,... | collective-permute-start | bytes 49160 | tf_op jit(solution)/shard_map/ppermute | solution.py:614
  40.2 1.4 %shard_map.123.refs_0_.refs_11_ = f32[4,128]{1,0:T(4,128)S(1)} custom-call(f32[16,2,32,512]{3,2,1,0:T(8,128)S(1)} %get-tuple-element.32.basis, f32[2,32,512]{2,1,0:T(8,128)S(1)} %get-tuple-element.31.power.old.refs_0_.refs_7_, f32[2,32,512]{2,1,0:T(8,128)S(1)} %get-tuple-element.42.refs_1_.old.refs_8_, ...), custom_call_target="tpu_custom_call" | custom-call | bytes 2000000 | tf_op jit(solution)/shard_map/pallas_call | solution.py:39
  41.7 0.0 collective-permute-done.13.refs_6_
  41.7 1.0 %shard_map.124.refs_1_ = f32[2,32,512]{2,1,0:T(8,128)S(1)} custom-call(s32[8,128]{1,0:T(8,128)S(1)} %get-tuple-element.34.live, s32[8]{0:T(128)S(1)} %copy-done.1, s32[8]{0:T(128)S(1)} %copy-done.2, f32[8,512]{1,0:T(8,128)S(1)} %add.31.sums, bf16[8,1024,512]{2,1,0:T(8,128)(2,1)S(1)} %get-tuple-element.45.mats, f32[4,128]{1,0:T(4,128)S(1)} %shard_map.123.refs_0_.refs_11_), custom_call_target="tpu_custom_call" | custom-call | bytes 6000000 | tf_op jit(solution)/shard_map/pallas_call | solution.py:39
  42.8 1.8 %collective-permute-done.15.refs_4_ = f32[2,16,512]{2,1,0:T(8,128)S(1)} collective-permute-done((f32[2,16,512]{2,1,0:T(8,128)S(1)}, f32[2,16,512]{2,1,0:T(8,128)S(1)}, u32[]{:S(2)}, u32[]{:S(2)}) %collective-permute-start.15) | collective-permute-done | bytes 65568 | tf_op jit(solution)/shard_map/ppermute | solution.py:614
  44.6 0.5 shard_map.125
  45.1 12.3 %all_to_all.5 = f32[32,4,128]{2,1,0:T(4,128)S(1)} all-to-all(f32[32,4,128]{2,1,0:T(4,128)S(1)} %broadcast_in_dim.2), channel_id=1, replica_groups=mesh['azim'=8,'dom'=4] {'azim','dom'}, dimensions={0} | all-to-all | bytes 131072 | tf_op jit(solution)/shard_map/all_to_all | solution.py:724
  57.4 2.3 %shard_map.126 = (f32[2,32,512]{2,1,0:T(8,128)}, f32[2]{0:T(128)}) custom-call(f32[2]{0:T(128)S(1)} %copy-done.5, f32[4,128]{1,0:T(4,128)S(1)} %reduce_sum.9.gram_s.gram, f32[4,128]{1,0:T(4,128)S(1)} %reduce_sum.9.gram_s.gram, f32[16,2,32,512]{3,2,1,0:T(8,128)S(1)} %get-tuple-element.32.basis, f32[2,32,512]{2,1,0:T(8,128)S(1)} %get-tuple-element.31.power.old.refs_0_.refs_7_, ...), custom_call_target="tpu_custom_call" | custom-call | bytes 2000000 | tf_op jit(solution)/shard_map/pallas_call | solution.py:39
  (22 shorter events, 0.1 us)
Async XLA Ops:
  2.9 6.7 %collective-permute-start = (f32[8,512]{1,0:T(8,128)S(1)}, f32[8,512]{1,0:T(8,128)S(1)}, u32[]{:S(2)}, u32[]{:S(2)}) collective-permute-start(f32[8,512]{1,0:T(8,128)S(1)} %get-tuple-element.35), channel_id=1, source_target_pairs={{0,1},{2,3},{1,0},{3,2},{4,5},{6,7},{5,4},{7,6},{8,9},{10,11},{9,8... | collective-permute-start | bytes 49160 | tf_op jit(solution)/shard_map/ppermute | solution.py:614
  3.5 12.3 %collective-permute-start.2 = (f32[2,16,512]{2,1,0:T(8,128)S(1)}, f32[2,16,512]{2,1,0:T(8,128)S(1)}, u32[]{:S(2)}, u32[]{:S(2)}) collective-permute-start(f32[2,16,512]{2,1,0:T(8,128)S(1)} %get-tuple-element.40), channel_id=1, source_target_pairs={{0,4},{8,12},{16,20},{24,28},{4,0},{12,8},{20,16},{28,24},{1,5},{9... | collective-permute-start | bytes 196616 | tf_op jit(solution)/shard_map/ppermute | solution.py:614
  6.0 9.8 %collective-permute-start.3 = (f32[2,16,512]{2,1,0:T(8,128)S(1)}, f32[2,16,512]{2,1,0:T(8,128)S(1)}, u32[]{:S(2)}, u32[]{:S(2)}) collective-permute-start(f32[2,16,512]{2,1,0:T(8,128)S(1)} %get-tuple-element.41), channel_id=1, source_target_pairs={{4,8},{12,16},{20,24},{28,0},{8,4},{16,12},{24,20},{0,28},{5,9},{1... | collective-permute-start | bytes 196616 | tf_op jit(solution)/shard_map/ppermute | solution.py:614
  9.7 3.5 %collective-permute-start.1 = (f32[8,512]{1,0:T(8,128)S(1)}, f32[8,512]{1,0:T(8,128)S(1)}, u32[]{:S(2)}, u32[]{:S(2)}) collective-permute-start(f32[8,512]{1,0:T(8,128)S(1)} %add_select_fusion.3), channel_id=1, source_target_pairs={{1,2},{3,0},{2,1},{0,3},{5,6},{7,4},{6,5},{4,7},{9,10},{11,8},{10,... | collective-permute-start | bytes 49160 | tf_op jit(solution)/shard_map/ppermute | solution.py:614
  11.3 1.9 %copy-start.1 = (s32[8]{0:T(128)S(1)}, s32[8]{0:T(128)}, u32[]{:S(2)}) copy-start(s32[8]{0:T(128)} %lines.7) | copy-start | bytes 100
  11.3 1.9 %copy-start.2 = (s32[8]{0:T(128)S(1)}, s32[8]{0:T(128)}, u32[]{:S(2)}) copy-start(s32[8]{0:T(128)} %burners.7) | copy-start | bytes 100
  13.3 2.6 %copy-start = (f32[2,16,512]{2,1,0:T(8,128)S(1)}, f32[2,16,512]{2,1,0:T(8,128)}, u32[]{:S(2)}) copy-start(f32[2,16,512]{2,1,0:T(8,128)} %param.13) | copy-start | bytes 196612
  13.3 2.6 %copy-start.3 = (s32[2]{0:T(128)S(1)}, s32[2]{0:T(128)}, u32[]{:S(2)}) copy-start(s32[2]{0:T(128)} %ref_part.5) | copy-start | bytes 28
  13.3 2.6 %copy-start.4 = (s32[2]{0:T(128)S(1)}, s32[2]{0:T(128)}, u32[]{:S(2)}) copy-start(s32[2]{0:T(128)} %ref_line.5) | copy-start | bytes 28
  16.6 2.6 %collective-permute-start.4 = (f32[8,512]{1,0:T(8,128)S(1)}, f32[8,512]{1,0:T(8,128)S(1)}, u32[]{:S(2)}, u32[]{:S(2)}) collective-permute-start(f32[8,512]{1,0:T(8,128)S(1)} %get-tuple-element.43), channel_id=1, source_target_pairs={{0,1},{2,3},{1,0},{3,2},{4,5},{6,7},{5,4},{7,6},{8,9},{10,11},{9,8... | collective-permute-start | bytes 49160 | tf_op jit(solution)/shard_map/ppermute | solution.py:614
  18.3 5.2 %collective-permute-start.6 = (f32[2,16,512]{2,1,0:T(8,128)S(1)}, f32[2,16,512]{2,1,0:T(8,128)S(1)}, u32[]{:S(2)}, u32[]{:S(2)}) collective-permute-start(f32[2,16,512]{2,1,0:T(8,128)S(1)} %get-tuple-element.46), channel_id=1, source_target_pairs={{0,4},{8,12},{16,20},{24,28},{4,0},{12,8},{20,16},{28,24},{1,5},{9... | collective-permute-start | bytes 196616 | tf_op jit(solution)/shard_map/ppermute | solution.py:614
  18.3 7.0 %collective-permute-start.7 = (f32[2,16,512]{2,1,0:T(8,128)S(1)}, f32[2,16,512]{2,1,0:T(8,128)S(1)}, u32[]{:S(2)}, u32[]{:S(2)}) collective-permute-start(f32[2,16,512]{2,1,0:T(8,128)S(1)} %get-tuple-element.47), channel_id=1, source_target_pairs={{4,8},{12,16},{20,24},{28,0},{8,4},{16,12},{24,20},{0,28},{5,9},{1... | collective-permute-start | bytes 196616 | tf_op jit(solution)/shard_map/ppermute | solution.py:614
  19.3 3.2 %collective-permute-start.5 = (f32[8,512]{1,0:T(8,128)S(1)}, f32[8,512]{1,0:T(8,128)S(1)}, u32[]{:S(2)}, u32[]{:S(2)}) collective-permute-start(f32[8,512]{1,0:T(8,128)S(1)} %add_select_fusion.2), channel_id=1, source_target_pairs={{1,2},{3,0},{2,1},{0,3},{5,6},{7,4},{6,5},{4,7},{9,10},{11,8},{10,... | collective-permute-start | bytes 49160 | tf_op jit(solution)/shard_map/ppermute | solution.py:614
  25.9 2.4 %collective-permute-start.8 = (f32[8,512]{1,0:T(8,128)S(1)}, f32[8,512]{1,0:T(8,128)S(1)}, u32[]{:S(2)}, u32[]{:S(2)}) collective-permute-start(f32[8,512]{1,0:T(8,128)S(1)} %get-tuple-element.49), channel_id=1, source_target_pairs={{0,1},{2,3},{1,0},{3,2},{4,5},{6,7},{5,4},{7,6},{8,9},{10,11},{9,8... | collective-permute-start | bytes 49160 | tf_op jit(solution)/shard_map/ppermute | solution.py:614
  26.6 6.7 %collective-permute-start.10 = (f32[2,16,512]{2,1,0:T(8,128)S(1)}, f32[2,16,512]{2,1,0:T(8,128)S(1)}, u32[]{:S(2)}, u32[]{:S(2)}) collective-permute-start(f32[2,16,512]{2,1,0:T(8,128)S(1)} %get-tuple-element.51), channel_id=1, source_target_pairs={{0,4},{8,12},{16,20},{24,28},{4,0},{12,8},{20,16},{28,24},{1,5},{9... | collective-permute-start | bytes 196616 | tf_op jit(solution)/shard_map/ppermute | solution.py:614
  28.1 7.0 %collective-permute-start.11 = (f32[2,16,512]{2,1,0:T(8,128)S(1)}, f32[2,16,512]{2,1,0:T(8,128)S(1)}, u32[]{:S(2)}, u32[]{:S(2)}) collective-permute-start(f32[2,16,512]{2,1,0:T(8,128)S(1)} %get-tuple-element.52), channel_id=1, source_target_pairs={{4,8},{12,16},{20,24},{28,0},{8,4},{16,12},{24,20},{0,28},{5,9},{1... | collective-permute-start | bytes 196616 | tf_op jit(solution)/shard_map/ppermute | solution.py:614
  28.4 3.9 %collective-permute-start.9 = (f32[8,512]{1,0:T(8,128)S(1)}, f32[8,512]{1,0:T(8,128)S(1)}, u32[]{:S(2)}, u32[]{:S(2)}) collective-permute-start(f32[8,512]{1,0:T(8,128)S(1)} %add_select_fusion.1), channel_id=1, source_target_pairs={{1,2},{3,0},{2,1},{0,3},{5,6},{7,4},{6,5},{4,7},{9,10},{11,8},{10,... | collective-permute-start | bytes 49160 | tf_op jit(solution)/shard_map/ppermute | solution.py:614
  33.3 24.1 %copy-start.5 = (f32[2]{0:T(128)S(1)}, f32[2]{0:T(128)}, u32[]{:S(2)}) copy-start(f32[2]{0:T(128)} %shift.1) | copy-start | bytes 28
  35.7 2.4 %collective-permute-start.12 = (f32[8,512]{1,0:T(8,128)S(1)}, f32[8,512]{1,0:T(8,128)S(1)}, u32[]{:S(2)}, u32[]{:S(2)}) collective-permute-start(f32[8,512]{1,0:T(8,128)S(1)} %get-tuple-element.54), channel_id=1, source_target_pairs={{0,1},{2,3},{1,0},{3,2},{4,5},{6,7},{5,4},{7,6},{8,9},{10,11},{9,8... | collective-permute-start | bytes 49160 | tf_op jit(solution)/shard_map/ppermute | solution.py:614
  36.8 5.9 %collective-permute-start.14 = (f32[2,16,512]{2,1,0:T(8,128)S(1)}, f32[2,16,512]{2,1,0:T(8,128)S(1)}, u32[]{:S(2)}, u32[]{:S(2)}) collective-permute-start(f32[2,16,512]{2,1,0:T(8,128)S(1)} %get-tuple-element.56), channel_id=1, source_target_pairs={{0,4},{8,12},{16,20},{24,28},{4,0},{12,8},{20,16},{28,24},{1,5},{9... | collective-permute-start | bytes 196616 | tf_op jit(solution)/shard_map/ppermute | solution.py:614
  37.6 7.0 %collective-permute-start.15 = (f32[2,16,512]{2,1,0:T(8,128)S(1)}, f32[2,16,512]{2,1,0:T(8,128)S(1)}, u32[]{:S(2)}, u32[]{:S(2)}) collective-permute-start(f32[2,16,512]{2,1,0:T(8,128)S(1)} %get-tuple-element.57), channel_id=1, source_target_pairs={{4,8},{12,16},{20,24},{28,0},{8,4},{16,12},{24,20},{0,28},{5,9},{1... | collective-permute-start | bytes 196616 | tf_op jit(solution)/shard_map/ppermute | solution.py:614
  38.2 3.5 %collective-permute-start.13 = (f32[8,512]{1,0:T(8,128)S(1)}, f32[8,512]{1,0:T(8,128)S(1)}, u32[]{:S(2)}, u32[]{:S(2)}) collective-permute-start(f32[8,512]{1,0:T(8,128)S(1)} %add_select_fusion), channel_id=1, source_target_pairs={{1,2},{3,0},{2,1},{0,3},{5,6},{7,4},{6,5},{4,7},{9,10},{11,8},{10,... | collective-permute-start | bytes 49160 | tf_op jit(solution)/shard_map/ppermute | solution.py:614
